TPU v7x, 512 devices: a whole 4x8x8 slice. The times are simulated.
512 devices in a mesh: dp: 16 (over y, core), tensor: 32 (over z, x).
Axes of the slice: x: 4, y: 8, z: 8, core: 2. Of those that a mesh axis runs over, the one named last changes fastest.
Arguments:
- tokens: bfloat16 [5632, 4096], P('dp', 'tensor'), may hold values from -6 to 6
- grad_out: bfloat16 [5632, 4096], P('dp', 'tensor'), may hold values from -6 to 6
- routes: float32 [16, 2, 16], P('dp'), may hold values from 0.005 to 0.3
- counts: int32 [16], P('dp'), may hold values from 176 to 352
- up_weight: bfloat16 [16, 4096, 4096], P(None, 'dp', 'tensor'), may hold values from -0.09375 to 0.09375
- down_weight: bfloat16 [16, 4096, 4096], P(None, 'tensor', 'dp'), may hold values from -0.09375 to 0.09375
Outputs:
- input_grad: bfloat16 [5632, 4096], P('dp', 'tensor')
- up_grad: bfloat16 [16, 4096, 4096], P(None, 'dp', 'tensor')
- down_grad: bfloat16 [16, 4096, 4096], P(None, 'tensor', 'dp')
- route_grad: float32 [16, 2, 16], P('dp')
Inputs may be any that keep to these rules, and one draw needn't show every extreme that they name: `counts`: the valid tokens of a data group, at least one whole segment.
All inputs are finite; a program needn't handle non-finite values.
Results may differ from a plain program's by a relative error of at most 0.02.
Values may be sent and summed in bfloat16 or wider, within the bound.
No kernel may reach another device: no remote copies, remote signals or barrier semaphores. Data moves between devices by JAX's collectives and lax.ppermute only.
A program may use at most 64 MiB of HBM per device.

v0:
```python
import jax
import jax.numpy as jnp
from jax import lax
from jax.sharding import PartitionSpec as P

gelu_scale = 0.7978845608
gelu_cubic = 0.044715


def gelu_pair(inputs):
    inner = gelu_scale * (inputs + gelu_cubic * inputs * inputs * inputs)
    tangent = jnp.tanh(inner)
    activated = 0.5 * inputs * (1.0 + tangent)
    derivative = 0.5 * (1.0 + tangent) + 0.5 * inputs * (1.0 - tangent * tangent) * gelu_scale * (
        1.0 + 3.0 * gelu_cubic * inputs * inputs
    )
    return (activated, derivative)


def body(tokens, grad_out, routes, counts, up_weight, down_weight):
    group_rows = tokens.shape[0]
    experts = up_weight.shape[0]
    segments = routes.shape[1]
    seg_rows = group_rows // segments
    high = lax.Precision.HIGHEST
    valid = (jnp.arange(group_rows, dtype=jnp.int32) < counts[0])[:, None]
    masked = jnp.where(valid, grad_out, jnp.zeros_like(grad_out))
    full_tokens, full_grads = (
        lax.all_gather(tokens, "tensor", axis=1, tiled=True),
        lax.all_gather(masked, "tensor", axis=1, tiled=True),
    )
    all_routes = lax.all_gather(routes, "dp", axis=0, tiled=True)
    flat_routes = all_routes.reshape(-1, experts)
    local_up = jnp.dot(
        flat_routes, up_weight.reshape(experts, -1).astype(jnp.float32), precision=high
    )
    local_up = local_up.reshape((-1,) + up_weight.shape[1:]).astype(jnp.bfloat16)
    down_turned = jnp.swapaxes(down_weight, 1, 2)
    local_down = jnp.dot(
        flat_routes, down_turned.reshape(experts, -1).astype(jnp.float32), precision=high
    )
    local_down = local_down.reshape((-1,) + down_turned.shape[1:]).astype(jnp.bfloat16)
    merged_up, merged_down = (
        lax.all_to_all(local_up, "dp", split_axis=0, concat_axis=1, tiled=True),
        lax.all_to_all(local_down, "dp", split_axis=0, concat_axis=1, tiled=True),
    )
    down_terms = []
    slopes = []
    for segment in range(segments):
        seg_tokens = full_tokens[segment * seg_rows : (segment + 1) * seg_rows]
        seg_grads = full_grads[segment * seg_rows : (segment + 1) * seg_rows]
        pre = jnp.dot(seg_tokens, merged_up[segment], preferred_element_type=jnp.float32)
        activated, derivative = gelu_pair(pre)
        activated = activated.astype(jnp.bfloat16)
        slopes.append(derivative)
        down_terms.append(
            jnp.einsum(
                "rd,rh->dh", seg_grads, activated, preferred_element_type=jnp.float32
            ).astype(jnp.bfloat16)
        )
    down_stack = jnp.stack(down_terms, axis=0)
    up_terms = []
    hidden_grads = []
    for segment in range(segments):
        seg_tokens = full_tokens[segment * seg_rows : (segment + 1) * seg_rows]
        seg_grads = full_grads[segment * seg_rows : (segment + 1) * seg_rows]
        back = jnp.einsum(
            "rd,dh->rh", seg_grads, merged_down[segment], preferred_element_type=jnp.float32
        )
        hidden_grad = (back * slopes[segment]).astype(jnp.bfloat16)
        hidden_grads.append(hidden_grad)
        up_terms.append(
            jnp.einsum(
                "rd,rh->dh", seg_tokens, hidden_grad, preferred_element_type=jnp.float32
            ).astype(jnp.bfloat16)
        )
    up_stack = jnp.stack(up_terms, axis=0)
    recv_up, recv_down = (
        lax.all_to_all(up_stack, "dp", split_axis=1, concat_axis=0, tiled=True),
        lax.all_to_all(down_stack, "dp", split_axis=1, concat_axis=0, tiled=True),
    )
    partials = [
        jnp.einsum(
            "rh,dh->rd",
            hidden_grads[segment],
            merged_up[segment],
            preferred_element_type=jnp.float32,
        )
        for segment in range(segments)
    ]
    rounded = lax.optimization_barrier(jnp.concatenate(partials, axis=0).astype(jnp.bfloat16))
    summed = lax.psum_scatter(
        rounded.astype(jnp.float32).astype(jnp.bfloat16), "tensor", scatter_dimension=1, tiled=True
    )
    up_grad = jnp.einsum(
        "ke,kdh->edh", flat_routes, recv_up.astype(jnp.float32), precision=high
    ).astype(jnp.bfloat16)
    down_grad = jnp.einsum(
        "ke,kdh->ehd", flat_routes, recv_down.astype(jnp.float32), precision=high
    ).astype(jnp.bfloat16)
    inner_sums = jnp.einsum("kdh,edh->ke", recv_up, up_weight, preferred_element_type=jnp.float32)
    inner_sums = inner_sums + jnp.einsum(
        "kdh,ehd->ke", recv_down, down_weight, preferred_element_type=jnp.float32
    )
    table = inner_sums.reshape(all_routes.shape)
    totals = lax.psum(table, ("dp", "tensor"))
    route_grad = lax.dynamic_slice_in_dim(totals, lax.axis_index("dp"), 1, 0)
    return (summed, up_grad, down_grad, route_grad)


def solution(mesh):
    return jax.shard_map(
        body,
        mesh=mesh,
        in_specs=(
            P("dp", "tensor"),
            P("dp", "tensor"),
            P("dp", None, None),
            P("dp"),
            P(None, "dp", "tensor"),
            P(None, "tensor", "dp"),
        ),
        out_specs=(
            P("dp", "tensor"),
            P(None, "dp", "tensor"),
            P(None, "tensor", "dp"),
            P("dp", None, None),
        ),
        check_vma=False,
    )
```

profile of v0, /device:TPU:1, one launch (start us, length us, event | category | flops | bytes accessed | tf_op | source)
XLA Modules:
  0.0 441.6 jit_solution(14864564712320135347)
XLA Ops:
  7.9 21.2 %all_gather.10 = f32[16,2,16]{2,1,0:T(2,128)S(1)} all-gather(f32[1,2,16]{2,1,0:T(2,128)} %param.8), channel_id=1, replica_groups=mesh['dp'=16,'tensor'=32] {'dp'}, dimensions={0}, use_global_device_ids=true | all-gather | bytes 2176 | tf_op jit(solution)/shard_map/all_gather | solution.py:32
  29.1 3.1 convolution_convert_fusion.6
  32.2 2.2 copy.65
  34.3 3.8 all-to-all-start.1
  43.2 2.2 copy.62
  45.4 41.8 %all-to-all-done.1 = bf16[32,256,128]{2,1,0:T(8,128)(2,1)S(1)} async-done(((bf16[32,256,128]{2,1,0:T(8,128)(2,1)}), bf16[32,256,128]{2,1,0:T(8,128)(2,1)S(1)}, u32[]{:S(2)}, u32[]{:S(2)}) %all-to-all-start.1) | async-done | bytes 2097184 | tf_op jit(solution)/shard_map/all_to_all | solution.py:44
  87.2 5.0 %all-to-all-start = ((bf16[32,256,128]{2,1,0:T(8,128)(2,1)}), bf16[32,256,128]{2,1,0:T(8,128)(2,1)}, u32[]{:S(2)}, u32[]{:S(2)}) async-start(bf16[32,256,128]{2,1,0:T(8,128)(2,1)} %copy.62), calls=%async_computation | async-start | bytes 4194304 | tf_op jit(solution)/shard_map/all_to_all | solution.py:45
  93.3 47.9 %all-to-all-done = bf16[32,256,128]{2,1,0:T(8,128)(2,1)} async-done(((bf16[32,256,128]{2,1,0:T(8,128)(2,1)}), bf16[32,256,128]{2,1,0:T(8,128)(2,1)}, u32[]{:S(2)}, u32[]{:S(2)}) %all-to-all-start) | async-done | bytes 2097184 | tf_op jit(solution)/shard_map/all_to_all | solution.py:45
  141.2 2.8 fusion.99
  145.9 39.0 %all-gather.3.cloned.1.call-done = bf16[352,4096]{1,0:T(8,128)(2,1)} async-done(((bf16[352,128]{1,0:T(8,128)(2,1)}), bf16[352,4096]{1,0:T(8,128)(2,1)}) %all-gather.3.cloned.1.call-update) | async-done | bytes 2883600 | tf_op jit(solution)/shard_map/all_gather | solution.py:30
  184.9 2.3 fusion.51
  190.4 3.8 copy.66
  194.2 9.9 %all-to-all-start.2 = ((bf16[2,4096,128]{2,0,1:T(2,128)(2,1)}), bf16[2,4096,128]{2,0,1:T(2,128)(2,1)S(1)}, u32[]{:S(2)}, u32[]{:S(2)}) async-start(bf16[2,4096,128]{2,0,1:T(2,128)(2,1)} %copy.66), calls=%async_computation.2 | async-start | bytes 4194304 | tf_op jit(solution)/shard_map/all_to_all | solution.py:79
  208.5 4.6 %copy.95 = bf16[352,4096]{0,1:T(8,128)(2,1)} copy(bf16[352,4096]{1,0:T(8,128)(2,1)} %pad_maximum_fusion) | data formatting | bytes 5767168
  213.1 2.1 fusion.2
  215.2 2.1 fusion.3
  217.6 18.1 %copy.70 = bf16[2,4096,128]{2,0,1:T(2,128)(2,1)} copy(bf16[2,4096,128]{2,1,0:T(8,128)(2,1)S(1)} %pad_maximum_fusion.2) | data formatting | bytes 4194304 | tf_op jit(solution)/shard_map/stack | solution.py:61
  235.7 17.4 %all-to-all-done.2 = bf16[2,4096,128]{2,0,1:T(2,128)(2,1)S(1)} async-done(((bf16[2,4096,128]{2,0,1:T(2,128)(2,1)}), bf16[2,4096,128]{2,0,1:T(2,128)(2,1)S(1)}, u32[]{:S(2)}, u32[]{:S(2)}) %all-to-all-start.2) | async-done | bytes 2097184 | tf_op jit(solution)/shard_map/all_to_all | solution.py:79
  253.1 5.0 %all-to-all-start.3 = ((bf16[2,4096,128]{2,0,1:T(2,128)(2,1)}), bf16[2,4096,128]{2,0,1:T(2,128)(2,1)}, u32[]{:S(2)}, u32[]{:S(2)}) async-start(bf16[2,4096,128]{2,0,1:T(2,128)(2,1)} %copy.70), calls=%async_computation.3 | async-start | bytes 4194304 | tf_op jit(solution)/shard_map/all_to_all | solution.py:80
  261.7 45.4 %all-to-all-done.3 = bf16[2,4096,128]{2,0,1:T(2,128)(2,1)} async-done(((bf16[2,4096,128]{2,0,1:T(2,128)(2,1)}), bf16[2,4096,128]{2,0,1:T(2,128)(2,1)}, u32[]{:S(2)}, u32[]{:S(2)}) %all-to-all-start.3) | async-done | bytes 2097184 | tf_op jit(solution)/shard_map/all_to_all | solution.py:80
  307.1 2.2 copy.94
  316.2 3.5 fusion.21
  321.2 98.3 %psum.7 = f32[16,2,16]{2,1,0:T(2,128)S(1)} all-reduce(f32[16,2,16]{2,1,0:T(2,128)S(1)} %bitcast.141), channel_id=1, replica_groups=mesh['dp'=16,'tensor'=32] {'dp','tensor'}, use_global_device_ids=true, to_apply=%region_1.2 | all-reduce | flops 512 | bytes 4096 | tf_op jit(solution)/shard_map/psum | solution.py:106
  420.2 13.3 %reduce-scatter.4.cloned.1.call-done = bf16[128,352]{1,0:T(8,128)(2,1)} async-done(((bf16[4096,352]{1,0:T(8,128)(2,1)}), bf16[128,352]{1,0:T(8,128)(2,1)}) %reduce-scatter.4.cloned.1.call-update) | async-done | bytes 90128
  (48 shorter events, 30.1 us)
Async XLA Ops:
  7.2 136.8 %all-gather.5.cloned.1.call-start = ((), (), s32[]{:S(2)}) async-start(), calls=%async_computation.6 | async-start | bytes 2973696 | tf_op jit(solution)/shard_map/all_gather | solution.py:29
  34.3 4.5 %copy-start.7 = (bf16[352,128]{1,0:T(8,128)(2,1)S(1)}, bf16[352,128]{1,0:T(8,128)(2,1)}, u32[]{:S(2)}) copy-start(bf16[352,128]{1,0:T(8,128)(2,1)} %param.7) | copy-start | bytes 270340
  34.3 52.8 %all-to-all-start.1 = ((bf16[32,256,128]{2,1,0:T(8,128)(2,1)}), bf16[32,256,128]{2,1,0:T(8,128)(2,1)S(1)}, u32[]{:S(2)}, u32[]{:S(2)}) async-start(bf16[32,256,128]{2,1,0:T(8,128)(2,1)} %copy.65), calls=%async_computation.1 | async-start | bytes 4194304 | tf_op jit(solution)/shard_map/all_to_all | solution.py:44
  38.2 146.7 %all-gather.3.cloned.1.call-start = ((), (), s32[]{:S(2)}) async-start(), calls=%async_computation.5 | async-start | bytes 2973696 | tf_op jit(solution)/shard_map/all_gather | solution.py:30
  87.2 54.0 %all-to-all-start = ((bf16[32,256,128]{2,1,0:T(8,128)(2,1)}), bf16[32,256,128]{2,1,0:T(8,128)(2,1)}, u32[]{:S(2)}, u32[]{:S(2)}) async-start(bf16[32,256,128]{2,1,0:T(8,128)(2,1)} %copy.62), calls=%async_computation | async-start | bytes 4194304 | tf_op jit(solution)/shard_map/all_to_all | solution.py:45
  141.2 2.8 copy-start.1
  184.9 2.6 copy-start.3
  187.4 1.8 copy-start.2
  194.2 58.8 %all-to-all-start.2 = ((bf16[2,4096,128]{2,0,1:T(2,128)(2,1)}), bf16[2,4096,128]{2,0,1:T(2,128)(2,1)S(1)}, u32[]{:S(2)}, u32[]{:S(2)}) async-start(bf16[2,4096,128]{2,0,1:T(2,128)(2,1)} %copy.66), calls=%async_computation.2 | async-start | bytes 4194304 | tf_op jit(solution)/shard_map/all_to_all | solution.py:79
  204.1 229.3 %reduce-scatter.4.cloned.1.call-start = ((), (), s32[]{:S(2)}) async-start(), calls=%async_computation.7 | async-start | bytes 3244032
  235.7 22.4 %copy-start = (bf16[16,128,256]{2,1,0:T(8,128)(2,1)S(1)}, bf16[16,128,256]{2,1,0:T(8,128)(2,1)}, u32[]{:S(2)}) copy-start(bf16[16,128,256]{2,1,0:T(8,128)(2,1)} %param.11) | copy-start | bytes 3145732
  253.1 54.0 %all-to-all-start.3 = ((bf16[2,4096,128]{2,0,1:T(2,128)(2,1)}), bf16[2,4096,128]{2,0,1:T(2,128)(2,1)}, u32[]{:S(2)}, u32[]{:S(2)}) async-start(bf16[2,4096,128]{2,0,1:T(2,128)(2,1)} %copy.70), calls=%async_computation.3 | async-start | bytes 4194304 | tf_op jit(solution)/shard_map/all_to_all | solution.py:80
  307.1 2.3 copy-start.4
  307.1 2.5 copy-start.5
  309.4 2.3 copy-start.6
Sparse Core Ops, SparseCore 0:
  11.0 86.7 all-gather.4
  101.5 83.3 all-gather.2
  213.2 220.1 reduce-scatter.3
where the time goes:
time: 447 us; the launch traced here: 442 us
  waiting for transfers between devices  205 us (46%)
  blocking collectives  120 us (27%)
  local copies, waits for them, and re-layouts  48.7 us (11%)
  matrix products  26.5 us (6%)
  starting transfers between devices  24 us (5%)
  between operations  14.6 us (3%)
    psum x1, blocking collectives, body(): totals = lax.psum(table, ('dp', 'tensor'))  98.3 us
    all_to_all x1, waiting for transfers between devices, body(): lax.all_to_all(local_down, 'dp', split_axis=0, concat_axis=1, tiled=True)  47.9 us
    all_to_all x1, waiting for transfers between devices, body(): lax.all_to_all(down_stack, 'dp', split_axis=1, concat_axis=0, tiled=True)  45.4 us
    all_to_all x1, waiting for transfers between devices, body(): lax.all_to_all(local_up, 'dp', split_axis=0, concat_axis=1, tiled=True)  41.8 us
    all_gather x1, waiting for transfers between devices, body(): lax.all_gather(masked, 'tensor', axis=1, tiled=True)  39 us
    all_gather x1, blocking collectives, body(): all_routes = lax.all_gather(routes, 'dp', axis=0, tiled=True)  21.2 us
    another operation x1, local copies, waits for them, and re-layouts, body(): down_stack = jnp.stack(down_terms, axis=0)  18.1 us
    all_to_all x1, waiting for transfers between devices, body(): lax.all_to_all(up_stack, 'dp', split_axis=1, concat_axis=0, tiled=True)  17.4 us
  transfers between devices with their start and end apart: 7, of which 6 were waited for; matrix products, arithmetic and copies ran while one was open for 15% of the time, Pallas kernels for 0%

commit v1 on v0

v1 whole, which is shorter than its diff:
```python
import functools

import jax
import jax.numpy as jnp
from jax import lax
from jax.experimental import pallas as pl
from jax.experimental.pallas import tpu as pltpu
from jax.sharding import Mesh, PartitionSpec as P

gelu_scale = 0.7978845608
gelu_cubic = 0.044715

DP = ("y", "c")
TENSOR = ("z", "x")


def gelu_pair(inputs):
    inner = gelu_scale * (inputs + gelu_cubic * inputs * inputs * inputs)
    tangent = jnp.tanh(inner)
    activated = 0.5 * inputs * (1.0 + tangent)
    derivative = 0.5 * (1.0 + tangent) + 0.5 * inputs * (1.0 - tangent * tangent) * gelu_scale * (
        1.0 + 3.0 * gelu_cubic * inputs * inputs
    )
    return (activated, derivative)


def dot(lhs, rhs, lhs_dim, rhs_dim):
    return lax.dot_general(
        lhs, rhs, (((lhs_dim,), (rhs_dim,)), ((), ())), preferred_element_type=jnp.float32
    )


def vmem(count):
    return [pl.BlockSpec(memory_space=pltpu.VMEM) for _ in range(count)]


def local_kernel(kernel, out_shapes, scalars, *args):
    smem = [pl.BlockSpec(memory_space=pltpu.SMEM) for _ in range(scalars)]
    return pl.pallas_call(
        kernel,
        out_shape=out_shapes,
        in_specs=smem + vmem(len(args) - scalars),
        out_specs=jax.tree.map(lambda _: vmem(1)[0], out_shapes),
        compiler_params=pltpu.CompilerParams(vmem_limit_bytes=56 * 1024 * 1024),
    )(*args)


def pair(full_ref, i, start, rows):
    return jnp.concatenate(
        [
            full_ref[2 * i, pl.ds(start, rows), :],
            full_ref[2 * i + 1, pl.ds(start, rows), :],
        ],
        axis=1,
    )


def pre_kernel(full_ref, up_ref, act_ref, slope_ref):
    slices, segments = up_ref.shape[0], up_ref.shape[1]
    rows = slope_ref.shape[0] // segments
    for s in range(segments):
        pre = jnp.zeros((rows, slope_ref.shape[1]), jnp.float32)
        for i in range(slices):
            pre = pre + dot(pair(full_ref, i, s * rows, rows), up_ref[i, s], 1, 0)
        activated, derivative = gelu_pair(pre)
        activated = activated.astype(jnp.bfloat16)
        slope_ref[pl.ds(s * rows, rows), :] = derivative
        for copy in range(act_ref.shape[0]):
            act_ref[copy, pl.ds(s * rows, rows), :] = activated


def back_kernel(full_ref, down_ref, slope_ref, hid_ref):
    slices, segments = down_ref.shape[0], down_ref.shape[1]
    group_rows = slope_ref.shape[0]
    rows = group_rows // segments
    for s in range(segments):
        back = jnp.zeros((rows, slope_ref.shape[1]), jnp.float32)
        for i in range(slices):
            back = back + dot(pair(full_ref, i, group_rows + s * rows, rows), down_ref[i, s], 1, 1)
        hidden = (back * slope_ref[pl.ds(s * rows, rows), :]).astype(jnp.bfloat16)
        for copy in range(hid_ref.shape[0]):
            hid_ref[copy, pl.ds(s * rows, rows), :] = hidden


def terms_kernel(which, where_ref, blocks_ref, same_ref, other_ref, out_ref):
    n_x, n_z = blocks_ref.shape[0], blocks_ref.shape[1]
    group_rows = same_ref.shape[1]
    segments = out_ref.shape[0] // (2 * n_z)
    rows = group_rows // segments
    z, x, core = where_ref[0], where_ref[1], where_ref[2]

    def step(g, carry):
        k = lax.rem(z - g + n_z, n_z)
        for c in range(2):
            low = lax.rem(x - 2 * c + n_x, n_x)
            high = lax.rem(x - 2 * c - 1 + n_x, n_x)
            for s in range(segments):
                own = pl.ds(s * rows, rows)
                rows_at = pl.ds(which * group_rows + s * rows, rows)
                block = jnp.concatenate(
                    [blocks_ref[low, k, rows_at, :], blocks_ref[high, k, rows_at, :]], axis=1
                )
                side = jnp.where(core == c, same_ref[g, own, :], other_ref[g, own, :])
                term = dot(side, block, 0, 0) if which else dot(block, side, 0, 0)
                out_ref[(2 * g + c) * segments + s] = term.astype(jnp.bfloat16)
        return carry

    lax.fori_loop(0, n_z, step, 0)


def input_kernel(where_ref, hid_ref, up_ref, out_ref):
    slices, segments = up_ref.shape[0], up_ref.shape[1]
    n_x, n_z, group_rows = out_ref.shape[0], out_ref.shape[1], out_ref.shape[2]
    rows = group_rows // segments
    z, x = where_ref[0], where_ref[1]
    for s in range(segments):
        hidden = hid_ref[0, pl.ds(s * rows, rows), :]
        for i in range(slices):
            part = dot(hidden, up_ref[i, s], 1, 1).astype(jnp.bfloat16)
            for half in range(2):
                t = 2 * i + half
                to_x = lax.rem(t % n_x - x + n_x, n_x)
                to_z = lax.rem(t // n_x - z + n_z, n_z)
                out_ref[to_x, to_z, pl.ds(s * rows, rows), :] = part[
                    :, half * 128 : (half + 1) * 128
                ]


def exchange(value, axes):
    return lax.all_to_all(value, axes, split_axis=0, concat_axis=0, tiled=True)


def shift(value, axis, by):
    size = lax.axis_size(axis)
    return lax.ppermute(value, axis, [(i, (i + by) % size) for i in range(size)])


def add(*values):
    return functools.reduce(lambda a, b: a + b, [v.astype(jnp.float32) for v in values])


def turn(value):
    n_dp = lax.axis_size("y") * lax.axis_size("c")
    n_t = lax.axis_size("z") * lax.axis_size("x")
    moves = [
        (g * n_t + t, (t // 2) * n_t + 2 * g + t % 2) for g in range(n_dp) for t in range(n_t)
    ]
    return lax.ppermute(value, DP + TENSOR, moves)


def scatter_sum(parts):
    n_z = parts.shape[1]
    half = n_z // 2
    bf16 = jnp.bfloat16
    from_left = shift(parts[2, :half], "x", 1)
    from_right = shift(parts[2, half:], "x", -1)
    right = jnp.concatenate([add(parts[1, :half], from_left).astype(bf16), parts[1, half:]])
    left = jnp.concatenate([parts[3, :half], add(parts[3, half:], from_right).astype(bf16)])
    near = add(parts[0], shift(right, "x", 1), shift(left, "x", -1)).astype(bf16)
    return add(near[0], *[shift(near[k], "z", k) for k in range(1, n_z)]).astype(bf16)


def body(tokens, grad_out, routes, counts, up_weight, down_weight):
    group_rows, lanes = tokens.shape
    experts, width, hidden = up_weight.shape
    segments = routes.shape[1]
    high = lax.Precision.HIGHEST
    n_y = lax.axis_size("y")
    n_dp = n_y * lax.axis_size("c")
    n_z, n_x = lax.axis_size("z"), lax.axis_size("x")
    bf16 = jnp.bfloat16
    shape = jax.ShapeDtypeStruct
    here = jnp.stack([lax.axis_index(a).astype(jnp.int32) for a in ("z", "x", "c")])
    routes_out = jnp.broadcast_to(routes, (n_dp,) + routes.shape[1:])
    all_routes = exchange(routes_out, DP)
    flat_routes = all_routes.reshape(-1, experts)
    valid = (jnp.arange(group_rows, dtype=jnp.int32) < counts[0])[:, None]
    masked = jnp.where(valid, grad_out, jnp.zeros_like(grad_out))
    both = jnp.concatenate([tokens, masked], axis=0)
    turned = turn(both)
    full = lax.all_gather(both, TENSOR)
    local_up = jnp.einsum(
        "ke,edh->kdh", flat_routes, up_weight.astype(jnp.float32), precision=high
    ).astype(bf16)
    local_up, turned = lax.optimization_barrier((local_up, turned))
    merged_up = exchange(local_up, DP).reshape(n_dp, segments, width, hidden)
    local_down = jnp.einsum(
        "ke,ehd->khd", flat_routes, down_weight.astype(jnp.float32), precision=high
    ).astype(bf16)
    near = jnp.stack([turned] + [shift(turned, "z", k) for k in range(1, n_z)])
    local_down, near = lax.optimization_barrier((local_down, near))
    merged_down = exchange(local_down, DP).reshape(n_dp, segments, hidden, width)
    right = shift(near, "x", 1)
    left = shift(near, "x", -1)
    merged_down, right, left = lax.optimization_barrier((merged_down, right, left))
    half = n_z // 2
    far = jnp.concatenate([shift(right[:half], "x", 1), shift(left[half:], "x", -1)], axis=0)
    blocks = jnp.stack([near, right, far, left])

    copies = shape((n_y, group_rows, hidden), bf16)
    act, slope = local_kernel(
        pre_kernel, (copies, shape((group_rows, hidden), jnp.float32)), 0, full, merged_up
    )
    hid = local_kernel(back_kernel, copies, 0, full, merged_down, slope)
    act_same = exchange(act, "y")
    act_other = shift(act_same, "c", 1)
    hid_same = exchange(hid, "y")
    parts = local_kernel(
        input_kernel, shape((n_x, n_z, group_rows, lanes), bf16), 1, here, hid, merged_up
    )
    summed = scatter_sum(parts)
    down_terms = local_kernel(
        functools.partial(terms_kernel, 1),
        shape((n_dp * segments, hidden, width), bf16),
        1,
        here,
        blocks,
        act_same,
        act_other,
    )
    down_grad = jnp.einsum(
        "ke,khd->ehd", flat_routes, down_terms.astype(jnp.float32), precision=high
    ).astype(bf16)
    down_inner = jnp.einsum(
        "khd,ehd->ke", down_terms, down_weight, preferred_element_type=jnp.float32
    )
    hid_same, down_grad, down_inner = lax.optimization_barrier((hid_same, down_grad, down_inner))
    hid_other = shift(hid_same, "c", 1)
    up_terms = local_kernel(
        functools.partial(terms_kernel, 0),
        shape((n_dp * segments, width, hidden), bf16),
        1,
        here,
        blocks,
        hid_same,
        hid_other,
    )
    up_grad = jnp.einsum(
        "ke,kdh->edh", flat_routes, up_terms.astype(jnp.float32), precision=high
    ).astype(bf16)
    inner = down_inner + jnp.einsum(
        "kdh,edh->ke", up_terms, up_weight, preferred_element_type=jnp.float32
    )
    own = jnp.sum(exchange(inner.reshape(all_routes.shape), DP), axis=0)
    pieces = exchange(jnp.broadcast_to(own[None], (n_z * n_x,) + own.shape), TENSOR)
    route_grad = jnp.sum(pieces, axis=0)[None]
    return (summed, up_grad, down_grad, route_grad)


def solution(mesh):
    fine = Mesh(mesh.devices.reshape(8, 2, 8, 4), DP + TENSOR)
    return jax.shard_map(
        body,
        mesh=fine,
        in_specs=(
            P(DP, TENSOR),
            P(DP, TENSOR),
            P(DP, None, None),
            P(DP),
            P(None, DP, TENSOR),
            P(None, TENSOR, DP),
        ),
        out_specs=(
            P(DP, TENSOR),
            P(None, DP, TENSOR),
            P(None, TENSOR, DP),
            P(DP, None, None),
        ),
        check_vma=False,
    )
```

time: 447 us -> 353 us (0.79)
  starting transfers between devices: 24 us -> 158 us
  waiting for transfers between devices: 205 us -> 82.7 us
  blocking collectives: 120 us -> 0 us
  Pallas kernels: 0 us -> 28.3 us
  other arithmetic: 2.97 us -> 20.9 us
  local copies, waits for them, and re-layouts: 48.7 us -> 30.8 us
  matrix products: 26.5 us -> 15.3 us
    all_to_all x4 -> x7, waiting for transfers between devices: 152 us -> 50.2 us  [exchange(): return lax.all_to_all(value, axes, split_axis=0, concat_axis=0, tiled=True)]
    psum x1 -> x0, blocking collectives: 98.3 us -> none  [body(): totals = lax.psum(table, ('dp', 'tensor'))]
    ppermute x0 -> x25, starting transfers between devices: none -> 87.1 us  [the longest x24 84 us: shift(): lax.ppermute(value, axis, [(i, (i + by) % size) for i in range(size)])]
    all_to_all x4 -> x7, starting transfers between devices: 23.7 us -> 71 us  [exchange(): return lax.all_to_all(value, axes, split_axis=0, concat_axis=0, tiled=True)]
    all_gather x2 -> x1, waiting for transfers between devices: 39 us -> 0.02 us  [body(): full = lax.all_gather(both, TENSOR)]
    ppermute x0 -> x25, waiting for transfers between devices: none -> 32.4 us  [the longest x24 32.4 us: shift(): lax.ppermute(value, axis, [(i, (i + by) % size) for i in range(size)])]
    pallas_call x0 -> x5, Pallas kernels: none -> 28.3 us  [local_kernel(): pl.pallas_call(kernel, out_shape=out_shapes, in_specs=smem + vmem(len(arg...]
    another operation x2 -> x1, local copies, waits for them, and re-layouts: 21.9 us -> 0.7 us  [body(): near = jnp.stack([turned] + [shift(turned, 'z', k) for k in range(1, n_z)])]
  transfers between devices with their start and end apart: 7 -> 33, of which waited for: 6 -> 8; matrix products, arithmetic and copies ran while one was open for 15% -> 17% of each run, Pallas kernels for 0% -> 8%
where the time goes in v1:
time: 353 us; the launch traced here: 351 us
  starting transfers between devices  158 us (45%)
  waiting for transfers between devices  82.7 us (23%)
  local copies, waits for them, and re-layouts  30.8 us (9%)
  Pallas kernels  28.3 us (8%)
  other arithmetic  20.9 us (6%)
  matrix products  15.3 us (4%)
  between operations  15.2 us (4%)
    ppermute x24, starting transfers between devices, shift(): lax.ppermute(value, axis, [(i, (i + by) % size) for i in range(size)])  84 us
    all_to_all x7, starting transfers between devices, exchange(): return lax.all_to_all(value, axes, split_axis=0, concat_axis=0, tiled=True)  71 us
    all_to_all x7, waiting for transfers between devices, exchange(): return lax.all_to_all(value, axes, split_axis=0, concat_axis=0, tiled=True)  50.2 us
    ppermute x24, waiting for transfers between devices, shift(): lax.ppermute(value, axis, [(i, (i + by) % size) for i in range(size)])  32.4 us
    pallas_call x5, Pallas kernels, local_kernel(): pl.pallas_call(kernel, out_shape=out_shapes, in_specs=smem + vmem(len(arg...  28.3 us
    unnamed x28, local copies, waits for them, and re-layouts  12.1 us
  transfers between devices with their start and end apart: 33, of which 8 were waited for; matrix products, arithmetic and copies ran while one was open for 17% of the time, Pallas kernels for 8%

profile of v1, /device:TPU:1, one launch (start us, length us, event | category | flops | bytes accessed | tf_op | source)
XLA Modules:
  0.0 351.4 jit_solution(14313018004807571270)
XLA Ops:
  11.9 10.2 %all-to-all-start = ((f32[16,2,16]{2,1,0:T(2,128)}), f32[16,2,16]{2,1,0:T(2,128)S(1)}, u32[]{:S(2)}, u32[]{:S(2)}) async-start(f32[16,2,16]{2,1,0:T(2,128)} %broadcast_in_dim.31), calls=%async_computation | async-start | bytes 32768 | tf_op jit(solution)/shard_map/all_to_all | solution.py:130
  25.1 4.3 %all-to-all-done = f32[16,2,16]{2,1,0:T(2,128)S(1)} async-done(((f32[16,2,16]{2,1,0:T(2,128)}), f32[16,2,16]{2,1,0:T(2,128)S(1)}, u32[]{:S(2)}, u32[]{:S(2)}) %all-to-all-start) | async-done | bytes 2080 | tf_op jit(solution)/shard_map/all_to_all | solution.py:130
  33.5 23.1 %all-to-all-start.2 = ((bf16[32,256,128]{2,1,0:T(8,128)(2,1)}), bf16[32,256,128]{2,1,0:T(8,128)(2,1)S(1)}, u32[]{:S(2)}, u32[]{:S(2)}) async-start(bf16[32,256,128]{2,1,0:T(8,128)(2,1)} %copy.79), calls=%async_computation.2 | async-start | bytes 4194304 | tf_op jit(solution)/shard_map/all_to_all | solution.py:130
  61.6 6.7 %collective-permute-start.2 = (bf16[704,128]{1,0:T(8,128)(2,1)S(1)}, bf16[704,128]{1,0:T(8,128)(2,1)S(1)}, u32[]{:S(2)}, u32[]{:S(2)}) collective-permute-start(bf16[704,128]{1,0:T(8,128)(2,1)S(1)} %collective-permute-done), channel_id=1, source_target_pairs={{0,8},{4,12},{8,16},{12,20},{16,24},{20,28},{24,0},{28,4},{1,9},{5... | collective-permute-start | bytes 540680 | tf_op jit(solution)/shard_map/ppermute | solution.py:135
  75.0 6.4 %collective-permute-start.5 = (bf16[704,128]{1,0:T(8,128)(2,1)S(1)}, bf16[704,128]{1,0:T(8,128)(2,1)S(1)}, u32[]{:S(2)}, u32[]{:S(2)}) collective-permute-start(bf16[704,128]{1,0:T(8,128)(2,1)S(1)} %collective-permute-done), channel_id=1, source_target_pairs={{0,20},{4,24},{8,28},{12,0},{16,4},{20,8},{24,12},{28,16},{1,21},{... | collective-permute-start | bytes 540680 | tf_op jit(solution)/shard_map/ppermute | solution.py:135
  90.8 11.3 %collective-permute-done.4 = bf16[704,128]{1,0:T(8,128)(2,1)S(1)} collective-permute-done((bf16[704,128]{1,0:T(8,128)(2,1)S(1)}, bf16[704,128]{1,0:T(8,128)(2,1)S(1)}, u32[]{:S(2)}, u32[]{:S(2)}) %collective-permute-start.4) | collective-permute-done | bytes 180256 | tf_op jit(solution)/shard_map/ppermute | solution.py:135
  103.5 10.5 %collective-permute-done.6 = bf16[704,128]{1,0:T(8,128)(2,1)S(1)} collective-permute-done((bf16[704,128]{1,0:T(8,128)(2,1)S(1)}, bf16[704,128]{1,0:T(8,128)(2,1)S(1)}, u32[]{:S(2)}, u32[]{:S(2)}) %collective-permute-start.6) | collective-permute-done | bytes 180256 | tf_op jit(solution)/shard_map/ppermute | solution.py:135
  114.7 6.6 %collective-permute-done.7 = bf16[704,128]{1,0:T(8,128)(2,1)S(1)} collective-permute-done((bf16[704,128]{1,0:T(8,128)(2,1)S(1)}, bf16[704,128]{1,0:T(8,128)(2,1)S(1)}, u32[]{:S(2)}, u32[]{:S(2)}) %collective-permute-start.7) | collective-permute-done | bytes 180256 | tf_op jit(solution)/shard_map/ppermute | solution.py:135
  124.5 9.9 %all-to-all-start.1 = ((bf16[32,128,256]{2,1,0:T(8,128)(2,1)}), bf16[32,128,256]{2,1,0:T(8,128)(2,1)}, u32[]{:S(2)}, u32[]{:S(2)}) async-start(bf16[32,128,256]{2,1,0:T(8,128)(2,1)} %copy.78), calls=%async_computation.1 | async-start | bytes 4194304 | tf_op jit(solution)/shard_map/all_to_all | solution.py:130
  140.9 5.1 %shard_map.93 = (bf16[8,352,128]{2,1,0:T(8,128)(2,1)}, f32[352,128]{1,0:T(8,128)}) custom-call(bf16[32,704,128]{2,1,0:T(8,128)(2,1)} %bitcast.94, bf16[16,2,256,128]{3,2,1,0:T(8,128)(2,1)} %bitcast.96), custom_call_target="tpu_custom_call" | custom-call | tf_op jit(solution)/shard_map/pallas_call | solution.py:39
  146.1 37.4 %all-to-all-done.1 = bf16[32,128,256]{2,1,0:T(8,128)(2,1)} async-done(((bf16[32,128,256]{2,1,0:T(8,128)(2,1)}), bf16[32,128,256]{2,1,0:T(8,128)(2,1)}, u32[]{:S(2)}, u32[]{:S(2)}) %all-to-all-start.1) | async-done | bytes 2097184 | tf_op jit(solution)/shard_map/all_to_all | solution.py:130
  183.5 4.3 %all-to-all-start.4 = ((bf16[8,352,128]{2,1,0:T(8,128)(2,1)}), bf16[8,352,128]{2,1,0:T(8,128)(2,1)S(1)}, u32[]{:S(2)}, u32[]{:S(2)}) async-start(bf16[8,352,128]{2,1,0:T(8,128)(2,1)} %get-tuple-element.24), calls=%async_computation.4 | async-start | bytes 1441792 | tf_op jit(solution)/shard_map/all_to_all | solution.py:130
  198.3 5.1 %shard_map.94.hid_ref = bf16[8,352,128]{2,1,0:T(8,128)(2,1)} custom-call(bf16[32,704,128]{2,1,0:T(8,128)(2,1)} %bitcast.95, bf16[16,2,128,256]{3,2,1,0:T(8,128)(2,1)} %bitcast.17.down_ref, f32[352,128]{1,0:T(8,128)} %get-tuple-element.21.slope_ref), custom_call_target="tpu_custom_call" | custom-call | tf_op jit(solution)/shard_map/pallas_call | solution.py:39
  203.4 4.3 %shard_map.95 = bf16[4,8,352,128]{3,2,1,0:T(8,128)(2,1)} custom-call(s32[3]{0:T(128)} %pad_add_fusion.where_ref, bf16[8,352,128]{2,1,0:T(8,128)(2,1)} %shard_map.94.hid_ref, bf16[16,2,256,128]{3,2,1,0:T(8,128)(2,1)} %bitcast.97), custom_call_target="tpu_custom_call" | custom-call | tf_op jit(solution)/shard_map/pallas_call | solution.py:39
  212.3 4.7 %collective-permute-start.12 = (bf16[4,352,128]{2,1,0:T(8,128)(2,1)}, bf16[4,352,128]{2,1,0:T(8,128)(2,1)}, u32[]{:S(2)}, u32[]{:S(2)}) collective-permute-start(bf16[4,352,128]{2,1,0:T(8,128)(2,1)} %get-tuple-element.51), channel_id=1, source_target_pairs={{0,3},{1,0},{2,1},{3,2},{4,7},{5,4},{6,5},{7,6},{8,11},{9,8},{10,9... | collective-permute-start | bytes 1081352 | tf_op jit(solution)/shard_map/ppermute | solution.py:135
  226.6 6.5 %all-to-all-start.3 = ((bf16[8,352,128]{2,1,0:T(8,128)(2,1)}), bf16[8,352,128]{2,1,0:T(8,128)(2,1)}, u32[]{:S(2)}, u32[]{:S(2)}) async-start(bf16[8,352,128]{2,1,0:T(8,128)(2,1)} %shard_map.94.hid_ref), calls=%async_computation.3 | async-start | bytes 1441792 | tf_op jit(solution)/shard_map/all_to_all | solution.py:130
  239.0 5.3 %collective-permute-start.13 = (bf16[8,352,128]{2,1,0:T(8,128)(2,1)}, bf16[8,352,128]{2,1,0:T(8,128)(2,1)}, u32[]{:S(2)}, u32[]{:S(2)}) collective-permute-start(bf16[8,352,128]{2,1,0:T(8,128)(2,1)} %pad_maximum_fusion.2), channel_id=1, source_target_pairs={{0,3},{1,0},{2,1},{3,2},{4,7},{5,4},{6,5},{7,6},{8,11},{9,8},{10,9... | collective-permute-start | bytes 2162696 | tf_op jit(solution)/shard_map/ppermute | solution.py:135
  248.2 5.6 %pad_maximum_fusion.blocks_ref = bf16[4,8,704,128]{3,2,1,0:T(8,128)(2,1)} fusion(bf16[1,8,704,128]{3,2,1,0:T(8,128)(2,1)} %bitcast.37, bf16[1,8,704,128]{3,2,1,0:T(8,128)(2,1)S(1)} %maximum_bitcast_fusion, bf16[1,8,704,128]{3,2,1,0:T(8,128)(2,1)} %bitcast.35, bf16[1,8,704,128]{3,2,1,0:T(8,128)(2,1)} %bitcast.34), kind=kLoop, calls=%fused_computation | loop fusion | flops 8650752 | bytes 11534336 | tf_op jit(solution)/shard_map/stack | solution.py:198
  254.6 6.6 %shard_map.96 = bf16[32,128,256]{2,1,0:T(8,128)(2,1)} custom-call(s32[3]{0:T(128)} %pad_add_fusion.where_ref, bf16[4,8,704,128]{3,2,1,0:T(8,128)(2,1)} %pad_maximum_fusion.blocks_ref, bf16[8,352,128]{2,1,0:T(8,128)(2,1)} %copy-done.6, bf16[8,352,128]{2,1,0:T(8,128)(2,1)} %copy-done.8), custom_call_target="tpu_custom_call" | custom-call | tf_op jit(solution)/shard_map/pallas_call | solution.py:39
  283.4 5.6 %collective-permute-start.17 = (bf16[352,128]{1,0:T(8,128)(2,1)}, bf16[352,128]{1,0:T(8,128)(2,1)}, u32[]{:S(2)}, u32[]{:S(2)}) collective-permute-start(bf16[352,128]{1,0:T(8,128)(2,1)} %get-tuple-element.58), channel_id=1, source_target_pairs={{0,16},{4,20},{8,24},{12,28},{16,0},{20,4},{24,8},{28,12},{1,17},{... | collective-permute-start | bytes 270344 | tf_op jit(solution)/shard_map/ppermute | solution.py:135
  291.8 7.2 %shard_map.97 = bf16[32,256,128]{2,1,0:T(8,128)(2,1)} custom-call(s32[3]{0:T(128)} %pad_add_fusion.where_ref, bf16[4,8,704,128]{3,2,1,0:T(8,128)(2,1)} %pad_maximum_fusion.blocks_ref, bf16[8,352,128]{2,1,0:T(8,128)(2,1)} %all-to-all-done.3.same_ref, bf16[8,352,128]{2,1,0:T(8,128)(2,1)} %copy-done.7), custom_call_target="tpu_custom_call" | custom-call | tf_op jit(solution)/shard_map/pallas_call | solution.py:39
  310.3 9.4 %all-to-all-start.5 = ((f32[16,2,16]{2,1,0:T(2,128)}), f32[16,2,16]{2,1,0:T(2,128)S(1)}, u32[]{:S(2)}, u32[]{:S(2)}) async-start(f32[16,2,16]{2,1,0:T(2,128)} %bitcast.44), calls=%async_computation.5 | async-start | bytes 32768 | tf_op jit(solution)/shard_map/all_to_all | solution.py:130
  327.6 7.6 %all-to-all-start.6 = ((f32[32,2,16]{2,1,0:T(2,128)}), f32[32,2,16]{2,1,0:T(2,128)S(1)}, u32[]{:S(2)}, u32[]{:S(2)}) async-start(f32[32,2,16]{2,1,0:T(2,128)} %broadcast_in_dim.32), calls=%async_computation.6 | async-start | bytes 65536 | tf_op jit(solution)/shard_map/all_to_all | solution.py:130
  338.3 5.6 %all-to-all-done.6 = f32[32,2,16]{2,1,0:T(2,128)S(1)} async-done(((f32[32,2,16]{2,1,0:T(2,128)}), f32[32,2,16]{2,1,0:T(2,128)S(1)}, u32[]{:S(2)}, u32[]{:S(2)}) %all-to-all-start.6) | async-done | bytes 4128 | tf_op jit(solution)/shard_map/all_to_all | solution.py:130
  (107 shorter events, 127.0 us)
Async XLA Ops:
  7.2 133.7 %all-gather.3.cloned.1.call-start = ((), (), s32[]{:S(2)}) async-start(), calls=%async_computation.7 | async-start | bytes 5947392 | tf_op jit(solution)/shard_map/all_gather | solution.py:181
  33.5 91.0 %all-to-all-start.2 = ((bf16[32,256,128]{2,1,0:T(8,128)(2,1)}), bf16[32,256,128]{2,1,0:T(8,128)(2,1)S(1)}, u32[]{:S(2)}, u32[]{:S(2)}) async-start(bf16[32,256,128]{2,1,0:T(8,128)(2,1)} %copy.79), calls=%async_computation.2 | async-start | bytes 4194304 | tf_op jit(solution)/shard_map/all_to_all | solution.py:130
  59.7 22.3 %collective-permute-start.1 = (bf16[704,128]{1,0:T(8,128)(2,1)S(1)}, bf16[704,128]{1,0:T(8,128)(2,1)S(1)}, u32[]{:S(2)}, u32[]{:S(2)}) collective-permute-start(bf16[704,128]{1,0:T(8,128)(2,1)S(1)} %collective-permute-done), channel_id=1, source_target_pairs={{0,4},{4,8},{8,12},{12,16},{16,20},{20,24},{24,28},{28,0},{1,5},{5... | collective-permute-start | bytes 540680 | tf_op jit(solution)/shard_map/ppermute | solution.py:135
  61.6 24.4 %collective-permute-start.2 = (bf16[704,128]{1,0:T(8,128)(2,1)S(1)}, bf16[704,128]{1,0:T(8,128)(2,1)S(1)}, u32[]{:S(2)}, u32[]{:S(2)}) collective-permute-start(bf16[704,128]{1,0:T(8,128)(2,1)S(1)} %collective-permute-done), channel_id=1, source_target_pairs={{0,8},{4,12},{8,16},{12,20},{16,24},{20,28},{24,0},{28,4},{1,9},{5... | collective-permute-start | bytes 540680 | tf_op jit(solution)/shard_map/ppermute | solution.py:135
  68.4 21.7 %collective-permute-start.3 = (bf16[704,128]{1,0:T(8,128)(2,1)S(1)}, bf16[704,128]{1,0:T(8,128)(2,1)S(1)}, u32[]{:S(2)}, u32[]{:S(2)}) collective-permute-start(bf16[704,128]{1,0:T(8,128)(2,1)S(1)} %collective-permute-done), channel_id=1, source_target_pairs={{0,12},{4,16},{8,20},{12,24},{16,28},{20,0},{24,4},{28,8},{1,13},{... | collective-permute-start | bytes 540680 | tf_op jit(solution)/shard_map/ppermute | solution.py:135
  72.5 29.6 %collective-permute-start.4 = (bf16[704,128]{1,0:T(8,128)(2,1)S(1)}, bf16[704,128]{1,0:T(8,128)(2,1)S(1)}, u32[]{:S(2)}, u32[]{:S(2)}) collective-permute-start(bf16[704,128]{1,0:T(8,128)(2,1)S(1)} %collective-permute-done), channel_id=1, source_target_pairs={{0,16},{4,20},{8,24},{12,28},{16,0},{20,4},{24,8},{28,12},{1,17},{... | collective-permute-start | bytes 540680 | tf_op jit(solution)/shard_map/ppermute | solution.py:135
  75.0 27.8 %collective-permute-start.5 = (bf16[704,128]{1,0:T(8,128)(2,1)S(1)}, bf16[704,128]{1,0:T(8,128)(2,1)S(1)}, u32[]{:S(2)}, u32[]{:S(2)}) collective-permute-start(bf16[704,128]{1,0:T(8,128)(2,1)S(1)} %collective-permute-done), channel_id=1, source_target_pairs={{0,20},{4,24},{8,28},{12,0},{16,4},{20,8},{24,12},{28,16},{1,21},{... | collective-permute-start | bytes 540680 | tf_op jit(solution)/shard_map/ppermute | solution.py:135
  82.0 31.9 %collective-permute-start.6 = (bf16[704,128]{1,0:T(8,128)(2,1)S(1)}, bf16[704,128]{1,0:T(8,128)(2,1)S(1)}, u32[]{:S(2)}, u32[]{:S(2)}) collective-permute-start(bf16[704,128]{1,0:T(8,128)(2,1)S(1)} %collective-permute-done), channel_id=1, source_target_pairs={{0,24},{4,28},{8,0},{12,4},{16,8},{20,12},{24,16},{28,20},{1,25},{... | collective-permute-start | bytes 540680 | tf_op jit(solution)/shard_map/ppermute | solution.py:135
  86.0 35.2 %collective-permute-start.7 = (bf16[704,128]{1,0:T(8,128)(2,1)S(1)}, bf16[704,128]{1,0:T(8,128)(2,1)S(1)}, u32[]{:S(2)}, u32[]{:S(2)}) collective-permute-start(bf16[704,128]{1,0:T(8,128)(2,1)S(1)} %collective-permute-done), channel_id=1, source_target_pairs={{0,28},{4,0},{8,4},{12,8},{16,12},{20,16},{24,20},{28,24},{1,29},{... | collective-permute-start | bytes 540680 | tf_op jit(solution)/shard_map/ppermute | solution.py:135
  124.5 59.0 %all-to-all-start.1 = ((bf16[32,128,256]{2,1,0:T(8,128)(2,1)}), bf16[32,128,256]{2,1,0:T(8,128)(2,1)}, u32[]{:S(2)}, u32[]{:S(2)}) async-start(bf16[32,128,256]{2,1,0:T(8,128)(2,1)} %copy.78), calls=%async_computation.1 | async-start | bytes 4194304 | tf_op jit(solution)/shard_map/all_to_all | solution.py:130
  134.4 53.4 %collective-permute-start.8 = (bf16[8,704,128]{2,1,0:T(8,128)(2,1)}, bf16[8,704,128]{2,1,0:T(8,128)(2,1)}, u32[]{:S(2)}, u32[]{:S(2)}) collective-permute-start(bf16[8,704,128]{2,1,0:T(8,128)(2,1)} %bitcast_dynamic-update-slice_fusion), channel_id=1, source_target_pairs={{0,1},{1,2},{2,3},{3,0},{4,5},{5,6},{6,7},{7,4},{8,9},{9,10},{10,1... | collective-permute-start | bytes 4325384 | tf_op jit(solution)/shard_map/ppermute | solution.py:135
  136.9 50.8 %collective-permute-start.9 = (bf16[8,704,128]{2,1,0:T(8,128)(2,1)}, bf16[8,704,128]{2,1,0:T(8,128)(2,1)}, u32[]{:S(2)}, u32[]{:S(2)}) collective-permute-start(bf16[8,704,128]{2,1,0:T(8,128)(2,1)} %bitcast_dynamic-update-slice_fusion), channel_id=1, source_target_pairs={{0,3},{1,0},{2,1},{3,2},{4,7},{5,4},{6,5},{7,6},{8,11},{9,8},{10,9... | collective-permute-start | bytes 4325384 | tf_op jit(solution)/shard_map/ppermute | solution.py:135
  183.5 43.1 %all-to-all-start.4 = ((bf16[8,352,128]{2,1,0:T(8,128)(2,1)}), bf16[8,352,128]{2,1,0:T(8,128)(2,1)S(1)}, u32[]{:S(2)}, u32[]{:S(2)}) async-start(bf16[8,352,128]{2,1,0:T(8,128)(2,1)} %get-tuple-element.24), calls=%async_computation.4 | async-start | bytes 1441792 | tf_op jit(solution)/shard_map/all_to_all | solution.py:130
  189.8 29.0 %collective-permute-start.22 = (bf16[4,704,128]{2,1,0:T(8,128)(2,1)}, bf16[4,704,128]{2,1,0:T(8,128)(2,1)}, u32[]{:S(2)}, u32[]{:S(2)}) collective-permute-start(bf16[4,704,128]{2,1,0:T(8,128)(2,1)} %slice.67), channel_id=1, source_target_pairs={{0,3},{1,0},{2,1},{3,2},{4,7},{5,4},{6,5},{7,6},{8,11},{9,8},{10,9... | collective-permute-start | bytes 2162696 | tf_op jit(solution)/shard_map/ppermute | solution.py:135
  195.7 23.1 %collective-permute-start.21 = (bf16[4,704,128]{2,1,0:T(8,128)(2,1)}, bf16[4,704,128]{2,1,0:T(8,128)(2,1)}, u32[]{:S(2)}, u32[]{:S(2)}) collective-permute-start(bf16[4,704,128]{2,1,0:T(8,128)(2,1)} %slice.66), channel_id=1, source_target_pairs={{0,1},{1,2},{2,3},{3,0},{4,5},{5,6},{6,7},{7,4},{8,9},{9,10},{10,1... | collective-permute-start | bytes 2162696 | tf_op jit(solution)/shard_map/ppermute | solution.py:135
  226.6 42.9 %all-to-all-start.3 = ((bf16[8,352,128]{2,1,0:T(8,128)(2,1)}), bf16[8,352,128]{2,1,0:T(8,128)(2,1)}, u32[]{:S(2)}, u32[]{:S(2)}) async-start(bf16[8,352,128]{2,1,0:T(8,128)(2,1)} %shard_map.94.hid_ref), calls=%async_computation.3 | async-start | bytes 1441792 | tf_op jit(solution)/shard_map/all_to_all | solution.py:130
  239.0 32.8 %collective-permute-start.13 = (bf16[8,352,128]{2,1,0:T(8,128)(2,1)}, bf16[8,352,128]{2,1,0:T(8,128)(2,1)}, u32[]{:S(2)}, u32[]{:S(2)}) collective-permute-start(bf16[8,352,128]{2,1,0:T(8,128)(2,1)} %pad_maximum_fusion.2), channel_id=1, source_target_pairs={{0,3},{1,0},{2,1},{3,2},{4,7},{5,4},{6,5},{7,6},{8,11},{9,8},{10,9... | collective-permute-start | bytes 2162696 | tf_op jit(solution)/shard_map/ppermute | solution.py:135
  246.3 25.4 %collective-permute-start.11 = (bf16[8,352,128]{2,1,0:T(8,128)(2,1)}, bf16[8,352,128]{2,1,0:T(8,128)(2,1)}, u32[]{:S(2)}, u32[]{:S(2)}) collective-permute-start(bf16[8,352,128]{2,1,0:T(8,128)(2,1)} %pad_maximum_fusion.1), channel_id=1, source_target_pairs={{0,1},{1,2},{2,3},{3,0},{4,5},{5,6},{6,7},{7,4},{8,9},{9,10},{10,1... | collective-permute-start | bytes 2162696 | tf_op jit(solution)/shard_map/ppermute | solution.py:135
  275.2 23.8 %collective-permute-start.20 = (bf16[352,128]{1,0:T(8,128)(2,1)S(1)}, bf16[352,128]{1,0:T(8,128)(2,1)S(1)}, u32[]{:S(2)}, u32[]{:S(2)}) collective-permute-start(bf16[352,128]{1,0:T(8,128)(2,1)S(1)} %get-tuple-element.55), channel_id=1, source_target_pairs={{0,28},{4,0},{8,4},{12,8},{16,12},{20,16},{24,20},{28,24},{1,29},{... | collective-permute-start | bytes 270344 | tf_op jit(solution)/shard_map/ppermute | solution.py:135
  277.8 24.8 %collective-permute-start.19 = (bf16[352,128]{1,0:T(8,128)(2,1)S(1)}, bf16[352,128]{1,0:T(8,128)(2,1)S(1)}, u32[]{:S(2)}, u32[]{:S(2)}) collective-permute-start(bf16[352,128]{1,0:T(8,128)(2,1)S(1)} %get-tuple-element.56), channel_id=1, source_target_pairs={{0,24},{4,28},{8,0},{12,4},{16,8},{20,12},{24,16},{28,20},{1,25},{... | collective-permute-start | bytes 270344 | tf_op jit(solution)/shard_map/ppermute | solution.py:135
  279.7 40.0 %collective-permute-start.18 = (bf16[352,128]{1,0:T(8,128)(2,1)}, bf16[352,128]{1,0:T(8,128)(2,1)S(1)}, u32[]{:S(2)}, u32[]{:S(2)}) collective-permute-start(bf16[352,128]{1,0:T(8,128)(2,1)} %get-tuple-element.57), channel_id=1, source_target_pairs={{0,20},{4,24},{8,28},{12,0},{16,4},{20,8},{24,12},{28,16},{1,21},{... | collective-permute-start | bytes 270344 | tf_op jit(solution)/shard_map/ppermute | solution.py:135
  283.4 36.3 %collective-permute-start.17 = (bf16[352,128]{1,0:T(8,128)(2,1)}, bf16[352,128]{1,0:T(8,128)(2,1)}, u32[]{:S(2)}, u32[]{:S(2)}) collective-permute-start(bf16[352,128]{1,0:T(8,128)(2,1)} %get-tuple-element.58), channel_id=1, source_target_pairs={{0,16},{4,20},{8,24},{12,28},{16,0},{20,4},{24,8},{28,12},{1,17},{... | collective-permute-start | bytes 270344 | tf_op jit(solution)/shard_map/ppermute | solution.py:135
  289.0 30.8 %collective-permute-start.16 = (bf16[352,128]{1,0:T(8,128)(2,1)}, bf16[352,128]{1,0:T(8,128)(2,1)}, u32[]{:S(2)}, u32[]{:S(2)}) collective-permute-start(bf16[352,128]{1,0:T(8,128)(2,1)} %get-tuple-element.59), channel_id=1, source_target_pairs={{0,12},{4,16},{8,20},{12,24},{16,28},{20,0},{24,4},{28,8},{1,13},{... | collective-permute-start | bytes 270344 | tf_op jit(solution)/shard_map/ppermute | solution.py:135
  299.0 20.8 %collective-permute-start.15 = (bf16[352,128]{1,0:T(8,128)(2,1)}, bf16[352,128]{1,0:T(8,128)(2,1)}, u32[]{:S(2)}, u32[]{:S(2)}) collective-permute-start(bf16[352,128]{1,0:T(8,128)(2,1)} %get-tuple-element.60), channel_id=1, source_target_pairs={{0,8},{4,12},{8,16},{12,20},{16,24},{20,28},{24,0},{28,4},{1,9},{5... | collective-permute-start | bytes 270344 | tf_op jit(solution)/shard_map/ppermute | solution.py:135
  (18 other events, 242.8 us)
Sparse Core Ops, SparseCore 0:
  11.7 125.8 all-gather.2

commit v2 on v1

v2 whole, which is shorter than its diff:
```python
import functools

import jax
import jax.numpy as jnp
from jax import lax
from jax.experimental import pallas as pl
from jax.experimental.pallas import tpu as pltpu
from jax.sharding import Mesh, PartitionSpec as P

gelu_scale = 0.7978845608
gelu_cubic = 0.044715

DP = ("y", "c")
TENSOR = ("z", "x")


def gelu_pair(inputs):
    inner = gelu_scale * (inputs + gelu_cubic * inputs * inputs * inputs)
    tangent = jnp.tanh(inner)
    activated = 0.5 * inputs * (1.0 + tangent)
    derivative = 0.5 * (1.0 + tangent) + 0.5 * inputs * (1.0 - tangent * tangent) * gelu_scale * (
        1.0 + 3.0 * gelu_cubic * inputs * inputs
    )
    return (activated, derivative)


def dot(lhs, rhs, lhs_dim, rhs_dim):
    return lax.dot_general(
        lhs, rhs, (((lhs_dim,), (rhs_dim,)), ((), ())), preferred_element_type=jnp.float32
    )


def vmem(count):
    return [pl.BlockSpec(memory_space=pltpu.VMEM) for _ in range(count)]


def local_kernel(kernel, out_shapes, scalars, *args):
    smem = [pl.BlockSpec(memory_space=pltpu.SMEM) for _ in range(scalars)]
    return pl.pallas_call(
        kernel,
        out_shape=out_shapes,
        in_specs=smem + vmem(len(args) - scalars),
        out_specs=jax.tree.map(lambda _: vmem(1)[0], out_shapes),
        compiler_params=pltpu.CompilerParams(vmem_limit_bytes=56 * 1024 * 1024),
    )(*args)


def pair(full_ref, i, start, rows):
    return jnp.concatenate(
        [
            full_ref[2 * i, pl.ds(start, rows), :],
            full_ref[2 * i + 1, pl.ds(start, rows), :],
        ],
        axis=1,
    )


def pre_kernel(full_ref, up_ref, slope_ref, term_ref):
    slices, segments = up_ref.shape[0], up_ref.shape[1]
    group_rows = slope_ref.shape[0]
    rows = group_rows // segments
    for s in range(segments):
        pre = jnp.zeros((rows, slope_ref.shape[1]), jnp.float32)
        for i in range(slices):
            pre = pre + dot(pair(full_ref, i, s * rows, rows), up_ref[i, s], 1, 0)
        activated, derivative = gelu_pair(pre)
        activated = activated.astype(jnp.bfloat16)
        slope_ref[pl.ds(s * rows, rows), :] = derivative
        for i in range(slices):
            term_ref[i, s] = dot(
                activated, pair(full_ref, i, group_rows + s * rows, rows), 0, 0
            ).astype(jnp.bfloat16)


def back_kernel(full_ref, down_ref, slope_ref, hid_ref, term_ref):
    slices, segments = down_ref.shape[0], down_ref.shape[1]
    group_rows = slope_ref.shape[0]
    rows = group_rows // segments
    for s in range(segments):
        back = jnp.zeros((rows, slope_ref.shape[1]), jnp.float32)
        for i in range(slices):
            back = back + dot(pair(full_ref, i, group_rows + s * rows, rows), down_ref[i, s], 1, 1)
        hidden = (back * slope_ref[pl.ds(s * rows, rows), :]).astype(jnp.bfloat16)
        hid_ref[pl.ds(s * rows, rows), :] = hidden
        for i in range(slices):
            term_ref[i, s] = dot(pair(full_ref, i, s * rows, rows), hidden, 0, 0).astype(
                jnp.bfloat16
            )


def input_kernel(where_ref, hid_ref, up_ref, out_ref):
    slices, segments = up_ref.shape[0], up_ref.shape[1]
    n_x, n_z, group_rows = out_ref.shape[0], out_ref.shape[1], out_ref.shape[2]
    rows = group_rows // segments
    z, x = where_ref[0], where_ref[1]
    for s in range(segments):
        hidden = hid_ref[pl.ds(s * rows, rows), :]
        for i in range(slices):
            part = dot(hidden, up_ref[i, s], 1, 1).astype(jnp.bfloat16)
            for half in range(2):
                t = 2 * i + half
                to_x = lax.rem(t % n_x - x + n_x, n_x)
                to_z = lax.rem(t // n_x - z + n_z, n_z)
                out_ref[to_x, to_z, pl.ds(s * rows, rows), :] = part[
                    :, half * 128 : (half + 1) * 128
                ]


def exchange(value, axes):
    return lax.all_to_all(value, axes, split_axis=0, concat_axis=0, tiled=True)


def shift(value, axis, by):
    size = lax.axis_size(axis)
    return lax.ppermute(value, axis, [(i, (i + by) % size) for i in range(size)])


def add(*values):
    return functools.reduce(lambda a, b: a + b, [v.astype(jnp.float32) for v in values])


def start_sum(parts):
    half = parts.shape[1] // 2
    bf16 = jnp.bfloat16
    from_left = shift(parts[2, :half], "x", 1)
    from_right = shift(parts[2, half:], "x", -1)
    right = jnp.concatenate([add(parts[1, :half], from_left).astype(bf16), parts[1, half:]])
    left = jnp.concatenate([parts[3, :half], add(parts[3, half:], from_right).astype(bf16)])
    return right, left


def finish_sum(own, right, left):
    bf16 = jnp.bfloat16
    near = add(own, shift(right, "x", 1), shift(left, "x", -1)).astype(bf16)
    hops = [shift(near[k], "z", k) for k in range(1, near.shape[0])]
    return add(near[0], *hops).astype(bf16)


def body(tokens, grad_out, routes, counts, up_weight, down_weight):
    group_rows, lanes = tokens.shape
    experts, width, hidden = up_weight.shape
    segments = routes.shape[1]
    high = lax.Precision.HIGHEST
    n_y = lax.axis_size("y")
    n_dp = n_y * lax.axis_size("c")
    n_z, n_x = lax.axis_size("z"), lax.axis_size("x")
    bf16 = jnp.bfloat16
    shape = jax.ShapeDtypeStruct
    here = jnp.stack([lax.axis_index(a).astype(jnp.int32) for a in ("z", "x")])
    routes_out = jnp.broadcast_to(routes, (n_dp,) + routes.shape[1:])
    all_routes = exchange(routes_out, DP)
    flat_routes = all_routes.reshape(-1, experts)
    valid = (jnp.arange(group_rows, dtype=jnp.int32) < counts[0])[:, None]
    masked = jnp.where(valid, grad_out, jnp.zeros_like(grad_out))
    both = jnp.concatenate([tokens, masked], axis=0)
    full = lax.all_gather(both, TENSOR)
    local_up = jnp.einsum(
        "ke,edh->kdh", flat_routes, up_weight.astype(jnp.float32), precision=high
    ).astype(bf16)
    merged_up = exchange(local_up, DP).reshape(n_dp, segments, width, hidden)
    local_down = jnp.einsum(
        "ke,ehd->khd", flat_routes, down_weight.astype(jnp.float32), precision=high
    ).astype(bf16)
    merged_down = exchange(local_down, DP).reshape(n_dp, segments, hidden, width)

    slope, down_terms = local_kernel(
        pre_kernel,
        (
            shape((group_rows, hidden), jnp.float32),
            shape((n_dp, segments, hidden, width), bf16),
        ),
        0,
        full,
        merged_up,
    )
    down_terms = exchange(down_terms.reshape(-1, hidden, width), DP)
    hid, up_terms = local_kernel(
        back_kernel,
        (shape((group_rows, hidden), bf16), shape((n_dp, segments, width, hidden), bf16)),
        0,
        full,
        merged_down,
        slope,
    )
    parts = local_kernel(
        input_kernel, shape((n_x, n_z, group_rows, lanes), bf16), 1, here, hid, merged_up
    )
    right, left = start_sum(parts)
    up_terms, right, left = lax.optimization_barrier((up_terms, right, left))
    summed = finish_sum(parts[0], right, left)
    down_grad = jnp.einsum(
        "ke,khd->ehd", flat_routes, down_terms.astype(jnp.float32), precision=high
    ).astype(bf16)
    down_inner = jnp.einsum(
        "khd,ehd->ke", down_terms, down_weight, preferred_element_type=jnp.float32
    )
    up_terms = exchange(up_terms.reshape(-1, width, hidden), DP)
    up_terms, down_grad, down_inner, summed = lax.optimization_barrier(
        (up_terms, down_grad, down_inner, summed)
    )
    up_grad = jnp.einsum(
        "ke,kdh->edh", flat_routes, up_terms.astype(jnp.float32), precision=high
    ).astype(bf16)
    inner = down_inner + jnp.einsum(
        "kdh,edh->ke", up_terms, up_weight, preferred_element_type=jnp.float32
    )
    own = jnp.sum(exchange(inner.reshape(all_routes.shape), DP), axis=0)
    pieces = exchange(jnp.broadcast_to(own[None], (n_z * n_x,) + own.shape), TENSOR)
    route_grad = jnp.sum(pieces, axis=0)[None]
    return (summed, up_grad, down_grad, route_grad)


def solution(mesh):
    fine = Mesh(mesh.devices.reshape(8, 2, 8, 4), DP + TENSOR)
    return jax.shard_map(
        body,
        mesh=fine,
        in_specs=(
            P(DP, TENSOR),
            P(DP, TENSOR),
            P(DP, None, None),
            P(DP),
            P(None, DP, TENSOR),
            P(None, TENSOR, DP),
        ),
        out_specs=(
            P(DP, TENSOR),
            P(None, DP, TENSOR),
            P(None, TENSOR, DP),
            P(DP, None, None),
        ),
        check_vma=False,
    )
```

time: 353 us -> 317 us (0.90)
  starting transfers between devices: 158 us -> 70.8 us
  waiting for transfers between devices: 82.7 us -> 134 us
  blocking collectives: 0 us -> 33.5 us
  local copies, waits for them, and re-layouts: 30.8 us -> 17.5 us
  other arithmetic: 20.9 us -> 9.47 us
  Pallas kernels: 28.3 us -> 18.2 us
    all_to_all x7 -> x5, starting transfers between devices: 71 us -> 26.4 us  [exchange(): return lax.all_to_all(value, axes, split_axis=0, concat_axis=0, tiled=True)]
    ppermute x24 -> x11, starting transfers between devices: 84 us -> 44.4 us  [shift(): lax.ppermute(value, axis, [(i, (i + by) % size) for i in range(size)])]
    all_to_all x7 -> x5, waiting for transfers between devices: 50.2 us -> 88.3 us  [exchange(): return lax.all_to_all(value, axes, split_axis=0, concat_axis=0, tiled=True)]
    all_to_all x0 -> x2, blocking collectives: none -> 33.5 us  [exchange(): return lax.all_to_all(value, axes, split_axis=0, concat_axis=0, tiled=True)]
    all_gather x1, waiting for transfers between devices: 0.02 us -> 18.8 us  [body(): full = lax.all_gather(both, TENSOR)]
    pallas_call x5 -> x3, Pallas kernels: 28.3 us -> 18.2 us  [local_kernel(): pl.pallas_call(kernel, out_shape=out_shapes, in_specs=smem + vmem(len(arg...]
    another operation x3 -> x1, other arithmetic: 7.65 us -> 0.58 us  [body(): here = jnp.stack([lax.axis_index(a).astype(jnp.int32) for a in ('z', 'x')])]
    unnamed x28 -> x11, local copies, waits for them, and re-layouts: 12.1 us -> 6.09 us
  transfers between devices with their start and end apart: 33 -> 17, of which waited for: 8 -> 10; matrix products, arithmetic and copies ran while one was open for 17% -> 11% of each run, Pallas kernels for 8% -> 6%
where the time goes in v2:
time: 317 us; the launch traced here: 316 us
  waiting for transfers between devices  134 us (42%)
  starting transfers between devices  70.8 us (22%)
  blocking collectives  33.5 us (11%)
  Pallas kernels  18.2 us (6%)
  local copies, waits for them, and re-layouts  17.5 us (6%)
  matrix products  17.2 us (5%)
  between operations  15 us (5%)
  other arithmetic  9.47 us (3%)
    all_to_all x5, waiting for transfers between devices, exchange(): return lax.all_to_all(value, axes, split_axis=0, concat_axis=0, tiled=True)  88.3 us
    ppermute x11, starting transfers between devices, shift(): lax.ppermute(value, axis, [(i, (i + by) % size) for i in range(size)])  44.4 us
    all_to_all x2, blocking collectives, exchange(): return lax.all_to_all(value, axes, split_axis=0, concat_axis=0, tiled=True)  33.5 us
    ppermute x11, waiting for transfers between devices, shift(): lax.ppermute(value, axis, [(i, (i + by) % size) for i in range(size)])  27.1 us
    all_to_all x5, starting transfers between devices, exchange(): return lax.all_to_all(value, axes, split_axis=0, concat_axis=0, tiled=True)  26.4 us
    all_gather x1, waiting for transfers between devices, body(): full = lax.all_gather(both, TENSOR)  18.8 us
    pallas_call x3, Pallas kernels, local_kernel(): pl.pallas_call(kernel, out_shape=out_shapes, in_specs=smem + vmem(len(arg...  18.2 us
  transfers between devices with their start and end apart: 17, of which 10 were waited for; matrix products, arithmetic and copies ran while one was open for 11% of the time, Pallas kernels for 6%

profile of v2, /device:TPU:1, one launch (start us, length us, event | category | flops | bytes accessed | tf_op | source)
XLA Modules:
  0.0 315.9 jit_solution(13898068844888318846)
XLA Ops:
  11.3 16.7 %all_to_all.35 = f32[16,2,16]{2,1,0:T(2,128)S(1)} all-to-all(f32[16,2,16]{2,1,0:T(2,128)S(1)} %broadcast_in_dim.31), channel_id=1, replica_groups=mesh['y'=8,'c'=2,'z'=8,'x'=4] {'y','c'}, dimensions={0} | all-to-all | bytes 4096 | tf_op jit(solution)/shard_map/all_to_all | solution.py:110
  32.0 3.9 %all-to-all-start.2 = ((bf16[32,256,128]{2,1,0:T(8,128)(2,1)}), bf16[32,256,128]{2,1,0:T(8,128)(2,1)S(1)}, u32[]{:S(2)}, u32[]{:S(2)}) async-start(bf16[32,256,128]{2,1,0:T(8,128)(2,1)} %copy.77), calls=%async_computation.2 | async-start | bytes 4194304 | tf_op jit(solution)/shard_map/all_to_all | solution.py:110
  41.6 43.3 %all-to-all-done.2 = bf16[32,256,128]{2,1,0:T(8,128)(2,1)S(1)} async-done(((bf16[32,256,128]{2,1,0:T(8,128)(2,1)}), bf16[32,256,128]{2,1,0:T(8,128)(2,1)S(1)}, u32[]{:S(2)}, u32[]{:S(2)}) %all-to-all-start.2) | async-done | bytes 2097184 | tf_op jit(solution)/shard_map/all_to_all | solution.py:110
  84.9 5.0 %all-to-all-start.1 = ((bf16[32,128,256]{2,1,0:T(8,128)(2,1)}), bf16[32,128,256]{2,1,0:T(8,128)(2,1)}, u32[]{:S(2)}, u32[]{:S(2)}) async-start(bf16[32,128,256]{2,1,0:T(8,128)(2,1)} %copy.74), calls=%async_computation.1 | async-start | bytes 4194304 | tf_op jit(solution)/shard_map/all_to_all | solution.py:110
  89.9 18.8 %all-gather.3.cloned.1.call-done = bf16[22528,128]{1,0:T(8,128)(2,1)} async-done(((bf16[704,128]{1,0:T(8,128)(2,1)}), bf16[22528,128]{1,0:T(8,128)(2,1)}) %all-gather.3.cloned.1.call-update) | async-done | bytes 5767184 | tf_op jit(solution)/shard_map/all_gather | solution.py:156
  108.7 6.4 %shard_map.93 = (f32[352,128]{1,0:T(8,128)}, bf16[16,2,128,256]{3,2,1,0:T(8,128)(2,1)}) custom-call(bf16[32,704,128]{2,1,0:T(8,128)(2,1)} %bitcast.76, bf16[16,2,256,128]{3,2,1,0:T(8,128)(2,1)} %bitcast.78), custom_call_target="tpu_custom_call" | custom-call | tf_op jit(solution)/shard_map/pallas_call | solution.py:39
  115.2 23.8 %all-to-all-done.1 = bf16[32,128,256]{2,1,0:T(8,128)(2,1)} async-done(((bf16[32,128,256]{2,1,0:T(8,128)(2,1)}), bf16[32,128,256]{2,1,0:T(8,128)(2,1)}, u32[]{:S(2)}, u32[]{:S(2)}) %all-to-all-start.1) | async-done | bytes 2097184 | tf_op jit(solution)/shard_map/all_to_all | solution.py:110
  139.0 5.0 %all-to-all-start.4 = ((bf16[32,128,256]{2,1,0:T(8,128)(2,1)}), bf16[32,128,256]{2,1,0:T(8,128)(2,1)S(1)}, u32[]{:S(2)}, u32[]{:S(2)}) async-start(bf16[32,128,256]{2,1,0:T(8,128)(2,1)} %bitcast.81), calls=%async_computation.4 | async-start | bytes 4194304 | tf_op jit(solution)/shard_map/all_to_all | solution.py:110
  144.5 7.6 %shard_map.94 = (bf16[352,128]{1,0:T(8,128)(2,1)}, bf16[16,2,256,128]{3,2,1,0:T(8,128)(2,1)}) custom-call(bf16[32,704,128]{2,1,0:T(8,128)(2,1)} %bitcast.77, bf16[16,2,128,256]{3,2,1,0:T(8,128)(2,1)} %bitcast.5.down_ref, f32[352,128]{1,0:T(8,128)} %get-tuple-element.15.slope_ref), custom_call_target="tpu_custom_call" | custom-call | tf_op jit(solution)/shard_map/pallas_call | solution.py:39
  152.1 4.1 %shard_map.95 = bf16[4,8,352,128]{3,2,1,0:T(8,128)(2,1)} custom-call(s32[2]{0:T(128)} %pad_add_fusion.where_ref, bf16[352,128]{1,0:T(8,128)(2,1)} %get-tuple-element.17.hid_ref, bf16[16,2,256,128]{3,2,1,0:T(8,128)(2,1)} %bitcast.79), custom_call_target="tpu_custom_call" | custom-call | tf_op jit(solution)/shard_map/pallas_call | solution.py:39
  159.9 4.3 %collective-permute-start.1 = (bf16[4,352,128]{2,1,0:T(8,128)(2,1)S(1)}, bf16[4,352,128]{2,1,0:T(8,128)(2,1)S(1)}, u32[]{:S(2)}, u32[]{:S(2)}) collective-permute-start(bf16[4,352,128]{2,1,0:T(8,128)(2,1)S(1)} %get-tuple-element.47), channel_id=1, source_target_pairs={{0,3},{1,0},{2,1},{3,2},{4,7},{5,4},{6,5},{7,6},{8,11},{9,8},{10,9... | collective-permute-start | bytes 1081352 | tf_op jit(solution)/shard_map/ppermute | solution.py:115
  164.2 6.5 %collective-permute-done = bf16[4,352,128]{2,1,0:T(8,128)(2,1)S(1)} collective-permute-done((bf16[4,352,128]{2,1,0:T(8,128)(2,1)S(1)}, bf16[4,352,128]{2,1,0:T(8,128)(2,1)S(1)}, u32[]{:S(2)}, u32[]{:S(2)}) %collective-permute-start) | collective-permute-done | bytes 360480 | tf_op jit(solution)/shard_map/ppermute | solution.py:115
  174.0 18.9 %all-to-all-done.4 = bf16[32,128,256]{2,1,0:T(8,128)(2,1)S(1)} async-done(((bf16[32,128,256]{2,1,0:T(8,128)(2,1)}), bf16[32,128,256]{2,1,0:T(8,128)(2,1)S(1)}, u32[]{:S(2)}, u32[]{:S(2)}) %all-to-all-start.4) | async-done | bytes 2097184 | tf_op jit(solution)/shard_map/all_to_all | solution.py:110
  192.9 5.0 %all-to-all-start.3 = ((bf16[32,256,128]{2,1,0:T(8,128)(2,1)}), bf16[32,256,128]{2,1,0:T(8,128)(2,1)}, u32[]{:S(2)}, u32[]{:S(2)}) async-start(bf16[32,256,128]{2,1,0:T(8,128)(2,1)} %bitcast.80), calls=%async_computation.3 | async-start | bytes 4194304 | tf_op jit(solution)/shard_map/all_to_all | solution.py:110
  200.1 4.3 %collective-permute-start.3 = (bf16[8,352,128]{2,1,0:T(8,128)(2,1)}, bf16[8,352,128]{2,1,0:T(8,128)(2,1)S(1)}, u32[]{:S(2)}, u32[]{:S(2)}) collective-permute-start(bf16[8,352,128]{2,1,0:T(8,128)(2,1)} %get-tuple-element.21), channel_id=1, source_target_pairs={{0,3},{1,0},{2,1},{3,2},{4,7},{5,4},{6,5},{7,6},{8,11},{9,8},{10,9... | collective-permute-start | bytes 2162696 | tf_op jit(solution)/shard_map/ppermute | solution.py:115
  204.4 14.5 %collective-permute-done.2 = bf16[8,352,128]{2,1,0:T(8,128)(2,1)S(1)} collective-permute-done((bf16[8,352,128]{2,1,0:T(8,128)(2,1)}, bf16[8,352,128]{2,1,0:T(8,128)(2,1)S(1)}, u32[]{:S(2)}, u32[]{:S(2)}) %collective-permute-start.2) | collective-permute-done | bytes 720928 | tf_op jit(solution)/shard_map/ppermute | solution.py:115
  222.8 10.4 %collective-permute-start.10 = (bf16[352,128]{1,0:T(8,128)(2,1)S(1)}, bf16[352,128]{1,0:T(8,128)(2,1)S(1)}, u32[]{:S(2)}, u32[]{:S(2)}) collective-permute-start(bf16[352,128]{1,0:T(8,128)(2,1)S(1)} %get-tuple-element.53), channel_id=1, source_target_pairs={{0,28},{4,0},{8,4},{12,8},{16,12},{20,16},{24,20},{28,24},{1,29},{... | collective-permute-start | bytes 270344 | tf_op jit(solution)/shard_map/ppermute | solution.py:115
  237.1 4.5 %collective-permute-start.6 = (bf16[352,128]{1,0:T(8,128)(2,1)}, bf16[352,128]{1,0:T(8,128)(2,1)S(1)}, u32[]{:S(2)}, u32[]{:S(2)}) collective-permute-start(bf16[352,128]{1,0:T(8,128)(2,1)} %get-tuple-element.57), channel_id=1, source_target_pairs={{0,12},{4,16},{8,20},{12,24},{16,28},{20,0},{24,4},{28,8},{1,13},{... | collective-permute-start | bytes 270344 | tf_op jit(solution)/shard_map/ppermute | solution.py:115
  241.6 4.9 %collective-permute-start.7 = (bf16[352,128]{1,0:T(8,128)(2,1)}, bf16[352,128]{1,0:T(8,128)(2,1)}, u32[]{:S(2)}, u32[]{:S(2)}) collective-permute-start(bf16[352,128]{1,0:T(8,128)(2,1)} %get-tuple-element.56), channel_id=1, source_target_pairs={{0,16},{4,20},{8,24},{12,28},{16,0},{20,4},{24,8},{28,12},{1,17},{... | collective-permute-start | bytes 270344 | tf_op jit(solution)/shard_map/ppermute | solution.py:115
  246.6 4.3 %collective-permute-start.8 = (bf16[352,128]{1,0:T(8,128)(2,1)}, bf16[352,128]{1,0:T(8,128)(2,1)}, u32[]{:S(2)}, u32[]{:S(2)}) collective-permute-start(bf16[352,128]{1,0:T(8,128)(2,1)} %get-tuple-element.55), channel_id=1, source_target_pairs={{0,20},{4,24},{8,28},{12,0},{16,4},{20,8},{24,12},{28,16},{1,21},{... | collective-permute-start | bytes 270344 | tf_op jit(solution)/shard_map/ppermute | solution.py:115
  256.9 4.4 %collective-permute-done.9 = bf16[352,128]{1,0:T(8,128)(2,1)} collective-permute-done((bf16[352,128]{1,0:T(8,128)(2,1)}, bf16[352,128]{1,0:T(8,128)(2,1)}, u32[]{:S(2)}, u32[]{:S(2)}) %collective-permute-start.9) | collective-permute-done | bytes 90144 | tf_op jit(solution)/shard_map/ppermute | solution.py:115
  275.0 16.8 %all_to_all.36 = f32[16,2,16]{2,1,0:T(2,128)S(1)} all-to-all(f32[16,2,16]{2,1,0:T(2,128)S(1)} %bitcast.86), channel_id=1, replica_groups=mesh['y'=8,'c'=2,'z'=8,'x'=4] {'y','c'}, dimensions={0} | all-to-all | bytes 4096 | tf_op jit(solution)/shard_map/all_to_all | solution.py:110
  292.5 7.5 %all-to-all-start.6 = ((f32[32,2,16]{2,1,0:T(2,128)}), f32[32,2,16]{2,1,0:T(2,128)S(1)}, u32[]{:S(2)}, u32[]{:S(2)}) async-start(f32[32,2,16]{2,1,0:T(2,128)} %broadcast_in_dim.32), calls=%async_computation.6 | async-start | bytes 65536 | tf_op jit(solution)/shard_map/all_to_all | solution.py:110
  300.0 3.5 %fusion.17 = bf16[16,256,128]{2,0,1:T(8,128)(2,1)S(1)} fusion(f32[32,16,1]{1,0,2:T(8,128)S(1)} %bitcast.85, bf16[32,256,128]{2,1,0:T(8,128)(2,1)} %all-to-all-done.3), kind=kOutput, calls=%fused_computation.14 | convolution fusion | flops 201850880 | bytes 3147776 | tf_op jit(solution)/shard_map/ke,kdh->edh/dot_general | solution.py:201
  (51 shorter events, 56.4 us)
Async XLA Ops:
  7.2 20.8 %copy-start = (bf16[16,256,128]{2,1,0:T(8,128)(2,1)S(1)}, bf16[16,256,128]{2,1,0:T(8,128)(2,1)}, u32[]{:S(2)}) copy-start(bf16[16,256,128]{2,1,0:T(8,128)(2,1)} %param.10) | copy-start | bytes 3145732
  7.2 101.5 %all-gather.3.cloned.1.call-start = ((), (), s32[]{:S(2)}) async-start(), calls=%async_computation.7 | async-start | bytes 5947392 | tf_op jit(solution)/shard_map/all_gather | solution.py:156
  32.0 52.9 %all-to-all-start.2 = ((bf16[32,256,128]{2,1,0:T(8,128)(2,1)}), bf16[32,256,128]{2,1,0:T(8,128)(2,1)S(1)}, u32[]{:S(2)}, u32[]{:S(2)}) async-start(bf16[32,256,128]{2,1,0:T(8,128)(2,1)} %copy.77), calls=%async_computation.2 | async-start | bytes 4194304 | tf_op jit(solution)/shard_map/all_to_all | solution.py:110
  84.9 23.8 %copy-start.1 = (bf16[32,256,128]{2,1,0:T(8,128)(2,1)}, bf16[32,256,128]{2,1,0:T(8,128)(2,1)S(1)}, u32[]{:S(2)}) copy-start(bf16[32,256,128]{2,1,0:T(8,128)(2,1)S(1)} %all-to-all-done.2) | copy-start | bytes 6291460
  84.9 54.0 %all-to-all-start.1 = ((bf16[32,128,256]{2,1,0:T(8,128)(2,1)}), bf16[32,128,256]{2,1,0:T(8,128)(2,1)}, u32[]{:S(2)}, u32[]{:S(2)}) async-start(bf16[32,128,256]{2,1,0:T(8,128)(2,1)} %copy.74), calls=%async_computation.1 | async-start | bytes 4194304 | tf_op jit(solution)/shard_map/all_to_all | solution.py:110
  139.0 53.9 %all-to-all-start.4 = ((bf16[32,128,256]{2,1,0:T(8,128)(2,1)}), bf16[32,128,256]{2,1,0:T(8,128)(2,1)S(1)}, u32[]{:S(2)}, u32[]{:S(2)}) async-start(bf16[32,128,256]{2,1,0:T(8,128)(2,1)} %bitcast.81), calls=%async_computation.4 | async-start | bytes 4194304 | tf_op jit(solution)/shard_map/all_to_all | solution.py:110
  157.7 13.0 %collective-permute-start = (bf16[4,352,128]{2,1,0:T(8,128)(2,1)S(1)}, bf16[4,352,128]{2,1,0:T(8,128)(2,1)S(1)}, u32[]{:S(2)}, u32[]{:S(2)}) collective-permute-start(bf16[4,352,128]{2,1,0:T(8,128)(2,1)S(1)} %get-tuple-element.49), channel_id=1, source_target_pairs={{0,1},{1,2},{2,3},{3,0},{4,5},{5,6},{6,7},{7,4},{8,9},{9,10},{10,1... | collective-permute-start | bytes 1081352 | tf_op jit(solution)/shard_map/ppermute | solution.py:115
  159.9 11.7 %collective-permute-start.1 = (bf16[4,352,128]{2,1,0:T(8,128)(2,1)S(1)}, bf16[4,352,128]{2,1,0:T(8,128)(2,1)S(1)}, u32[]{:S(2)}, u32[]{:S(2)}) collective-permute-start(bf16[4,352,128]{2,1,0:T(8,128)(2,1)S(1)} %get-tuple-element.47), channel_id=1, source_target_pairs={{0,3},{1,0},{2,1},{3,2},{4,7},{5,4},{6,5},{7,6},{8,11},{9,8},{10,9... | collective-permute-start | bytes 1081352 | tf_op jit(solution)/shard_map/ppermute | solution.py:115
  192.9 78.6 %all-to-all-start.3 = ((bf16[32,256,128]{2,1,0:T(8,128)(2,1)}), bf16[32,256,128]{2,1,0:T(8,128)(2,1)}, u32[]{:S(2)}, u32[]{:S(2)}) async-start(bf16[32,256,128]{2,1,0:T(8,128)(2,1)} %bitcast.80), calls=%async_computation.3 | async-start | bytes 4194304 | tf_op jit(solution)/shard_map/all_to_all | solution.py:110
  197.9 21.0 %collective-permute-start.2 = (bf16[8,352,128]{2,1,0:T(8,128)(2,1)}, bf16[8,352,128]{2,1,0:T(8,128)(2,1)S(1)}, u32[]{:S(2)}, u32[]{:S(2)}) collective-permute-start(bf16[8,352,128]{2,1,0:T(8,128)(2,1)} %get-tuple-element.20), channel_id=1, source_target_pairs={{0,1},{1,2},{2,3},{3,0},{4,5},{5,6},{6,7},{7,4},{8,9},{9,10},{10,1... | collective-permute-start | bytes 2162696 | tf_op jit(solution)/shard_map/ppermute | solution.py:115
  200.1 19.7 %collective-permute-start.3 = (bf16[8,352,128]{2,1,0:T(8,128)(2,1)}, bf16[8,352,128]{2,1,0:T(8,128)(2,1)S(1)}, u32[]{:S(2)}, u32[]{:S(2)}) collective-permute-start(bf16[8,352,128]{2,1,0:T(8,128)(2,1)} %get-tuple-element.21), channel_id=1, source_target_pairs={{0,3},{1,0},{2,1},{3,2},{4,7},{5,4},{6,5},{7,6},{8,11},{9,8},{10,9... | collective-permute-start | bytes 2162696 | tf_op jit(solution)/shard_map/ppermute | solution.py:115
  221.1 0.9 copy-start.3
  222.8 23.8 %collective-permute-start.10 = (bf16[352,128]{1,0:T(8,128)(2,1)S(1)}, bf16[352,128]{1,0:T(8,128)(2,1)S(1)}, u32[]{:S(2)}, u32[]{:S(2)}) collective-permute-start(bf16[352,128]{1,0:T(8,128)(2,1)S(1)} %get-tuple-element.53), channel_id=1, source_target_pairs={{0,28},{4,0},{8,4},{12,8},{16,12},{20,16},{24,20},{28,24},{1,29},{... | collective-permute-start | bytes 270344 | tf_op jit(solution)/shard_map/ppermute | solution.py:115
  233.2 17.6 %collective-permute-start.4 = (bf16[352,128]{1,0:T(8,128)(2,1)S(1)}, bf16[352,128]{1,0:T(8,128)(2,1)S(1)}, u32[]{:S(2)}, u32[]{:S(2)}) collective-permute-start(bf16[352,128]{1,0:T(8,128)(2,1)S(1)} %get-tuple-element.52), channel_id=1, source_target_pairs={{0,4},{4,8},{8,12},{12,16},{16,20},{20,24},{24,28},{28,0},{1,5},{5... | collective-permute-start | bytes 270344 | tf_op jit(solution)/shard_map/ppermute | solution.py:115
  235.2 21.7 %collective-permute-start.5 = (bf16[352,128]{1,0:T(8,128)(2,1)}, bf16[352,128]{1,0:T(8,128)(2,1)S(1)}, u32[]{:S(2)}, u32[]{:S(2)}) collective-permute-start(bf16[352,128]{1,0:T(8,128)(2,1)} %get-tuple-element.58), channel_id=1, source_target_pairs={{0,8},{4,12},{8,16},{12,20},{16,24},{20,28},{24,0},{28,4},{1,9},{5... | collective-permute-start | bytes 270344 | tf_op jit(solution)/shard_map/ppermute | solution.py:115
  237.1 19.8 %collective-permute-start.6 = (bf16[352,128]{1,0:T(8,128)(2,1)}, bf16[352,128]{1,0:T(8,128)(2,1)S(1)}, u32[]{:S(2)}, u32[]{:S(2)}) collective-permute-start(bf16[352,128]{1,0:T(8,128)(2,1)} %get-tuple-element.57), channel_id=1, source_target_pairs={{0,12},{4,16},{8,20},{12,24},{16,28},{20,0},{24,4},{28,8},{1,13},{... | collective-permute-start | bytes 270344 | tf_op jit(solution)/shard_map/ppermute | solution.py:115
  241.6 15.3 %collective-permute-start.7 = (bf16[352,128]{1,0:T(8,128)(2,1)}, bf16[352,128]{1,0:T(8,128)(2,1)}, u32[]{:S(2)}, u32[]{:S(2)}) collective-permute-start(bf16[352,128]{1,0:T(8,128)(2,1)} %get-tuple-element.56), channel_id=1, source_target_pairs={{0,16},{4,20},{8,24},{12,28},{16,0},{20,4},{24,8},{28,12},{1,17},{... | collective-permute-start | bytes 270344 | tf_op jit(solution)/shard_map/ppermute | solution.py:115
  246.6 10.3 %collective-permute-start.8 = (bf16[352,128]{1,0:T(8,128)(2,1)}, bf16[352,128]{1,0:T(8,128)(2,1)}, u32[]{:S(2)}, u32[]{:S(2)}) collective-permute-start(bf16[352,128]{1,0:T(8,128)(2,1)} %get-tuple-element.55), channel_id=1, source_target_pairs={{0,20},{4,24},{8,28},{12,0},{16,4},{20,8},{24,12},{28,16},{1,21},{... | collective-permute-start | bytes 270344 | tf_op jit(solution)/shard_map/ppermute | solution.py:115
  250.9 10.5 %collective-permute-start.9 = (bf16[352,128]{1,0:T(8,128)(2,1)}, bf16[352,128]{1,0:T(8,128)(2,1)}, u32[]{:S(2)}, u32[]{:S(2)}) collective-permute-start(bf16[352,128]{1,0:T(8,128)(2,1)} %get-tuple-element.54), channel_id=1, source_target_pairs={{0,24},{4,28},{8,0},{12,4},{16,8},{20,12},{24,16},{28,20},{1,25},{... | collective-permute-start | bytes 270344 | tf_op jit(solution)/shard_map/ppermute | solution.py:115
  292.5 15.9 %all-to-all-start.6 = ((f32[32,2,16]{2,1,0:T(2,128)}), f32[32,2,16]{2,1,0:T(2,128)S(1)}, u32[]{:S(2)}, u32[]{:S(2)}) async-start(f32[32,2,16]{2,1,0:T(2,128)} %broadcast_in_dim.32), calls=%async_computation.6 | async-start | bytes 65536 | tf_op jit(solution)/shard_map/all_to_all | solution.py:110
  300.0 4.8 %copy-start.2 = (bf16[16,128,256]{2,0,1:T(8,128)(2,1)S(1)}, bf16[16,128,256]{2,0,1:T(8,128)(2,1)}, u32[]{:S(2)}) copy-start(bf16[16,128,256]{2,0,1:T(8,128)(2,1)} %fusion.14) | copy-start | bytes 3145732
Sparse Core Ops, SparseCore 0:
  11.7 96.9 all-gather.2

commit v3 on v2

--- a/solution.py
+++ b/solution.py
@@ -129,11 +129,13 @@
     return right, left
 
 
-def finish_sum(own, right, left):
-    bf16 = jnp.bfloat16
-    near = add(own, shift(right, "x", 1), shift(left, "x", -1)).astype(bf16)
+def second_hop(own, right, left):
+    return add(own, shift(right, "x", 1), shift(left, "x", -1)).astype(jnp.bfloat16)
+
+
+def finish_sum(near):
     hops = [shift(near[k], "z", k) for k in range(1, near.shape[0])]
-    return add(near[0], *hops).astype(bf16)
+    return add(near[0], *hops).astype(jnp.bfloat16)
 
 
 def body(tokens, grad_out, routes, counts, up_weight, down_weight):
@@ -149,11 +151,12 @@
     here = jnp.stack([lax.axis_index(a).astype(jnp.int32) for a in ("z", "x")])
     routes_out = jnp.broadcast_to(routes, (n_dp,) + routes.shape[1:])
     all_routes = exchange(routes_out, DP)
-    flat_routes = all_routes.reshape(-1, experts)
     valid = (jnp.arange(group_rows, dtype=jnp.int32) < counts[0])[:, None]
     masked = jnp.where(valid, grad_out, jnp.zeros_like(grad_out))
     both = jnp.concatenate([tokens, masked], axis=0)
+    both, all_routes = lax.optimization_barrier((both, all_routes))
     full = lax.all_gather(both, TENSOR)
+    flat_routes = all_routes.reshape(-1, experts)
     local_up = jnp.einsum(
         "ke,edh->kdh", flat_routes, up_weight.astype(jnp.float32), precision=high
     ).astype(bf16)
@@ -186,8 +189,9 @@
         input_kernel, shape((n_x, n_z, group_rows, lanes), bf16), 1, here, hid, merged_up
     )
     right, left = start_sum(parts)
-    up_terms, right, left = lax.optimization_barrier((up_terms, right, left))
-    summed = finish_sum(parts[0], right, left)
+    near = second_hop(parts[0], right, left)
+    up_terms, near = lax.optimization_barrier((up_terms, near))
+    summed = finish_sum(near)
     down_grad = jnp.einsum(
         "ke,khd->ehd", flat_routes, down_terms.astype(jnp.float32), precision=high
     ).astype(bf16)

time: 317 us -> 297 us (0.937)
  blocking collectives: 33.5 us -> 15.3 us
  waiting for transfers between devices: 134 us -> 120 us
  starting transfers between devices: 70.8 us -> 84.5 us
    all_to_all x5 -> x6, waiting for transfers between devices: 88.3 us -> 63.3 us  [exchange(): return lax.all_to_all(value, axes, split_axis=0, concat_axis=0, tiled=True)]
    all_to_all x2 -> x1, blocking collectives: 33.5 us -> 15.3 us  [exchange(): return lax.all_to_all(value, axes, split_axis=0, concat_axis=0, tiled=True)]
    all_to_all x5 -> x6, starting transfers between devices: 26.4 us -> 40 us  [exchange(): return lax.all_to_all(value, axes, split_axis=0, concat_axis=0, tiled=True)]
    all_gather x1, waiting for transfers between devices: 18.8 us -> 29 us  [body(): full = lax.all_gather(both, TENSOR)]
  transfers between devices with their start and end apart: 17 -> 18, of which waited for: 10 -> 10; matrix products, arithmetic and copies ran while one was open for 11% -> 12% of each run, Pallas kernels for 6% -> 6%
where the time goes in v3:
time: 297 us; the launch traced here: 296 us
  waiting for transfers between devices  120 us (40%)
  starting transfers between devices  84.5 us (28%)
  local copies, waits for them, and re-layouts  18.6 us (6%)
  Pallas kernels  18.2 us (6%)
  matrix products  17.2 us (6%)
  blocking collectives  15.3 us (5%)
  between operations  14.9 us (5%)
  other arithmetic  7.03 us (2%)
    all_to_all x6, waiting for transfers between devices, exchange(): return lax.all_to_all(value, axes, split_axis=0, concat_axis=0, tiled=True)  63.3 us
    ppermute x11, starting transfers between devices, shift(): lax.ppermute(value, axis, [(i, (i + by) % size) for i in range(size)])  44.5 us
    all_to_all x6, starting transfers between devices, exchange(): return lax.all_to_all(value, axes, split_axis=0, concat_axis=0, tiled=True)  40 us
    all_gather x1, waiting for transfers between devices, body(): full = lax.all_gather(both, TENSOR)  29 us
    ppermute x11, waiting for transfers between devices, shift(): lax.ppermute(value, axis, [(i, (i + by) % size) for i in range(size)])  27.7 us
    pallas_call x3, Pallas kernels, local_kernel(): pl.pallas_call(kernel, out_shape=out_shapes, in_specs=smem + vmem(len(arg...  18.2 us
    all_to_all x1, blocking collectives, exchange(): return lax.all_to_all(value, axes, split_axis=0, concat_axis=0, tiled=True)  15.3 us
  transfers between devices with their start and end apart: 18, of which 10 were waited for; matrix products, arithmetic and copies ran while one was open for 12% of the time, Pallas kernels for 6%

profile of v3, /device:TPU:1, one launch (start us, length us, event | category | flops | bytes accessed | tf_op | source)
XLA Modules:
  0.0 295.9 jit_solution(4587003196747653949)
XLA Ops:
  8.6 10.2 %all-to-all-start = ((f32[16,2,16]{2,1,0:T(2,128)}), f32[16,2,16]{2,1,0:T(2,128)S(1)}, u32[]{:S(2)}, u32[]{:S(2)}) async-start(f32[16,2,16]{2,1,0:T(2,128)} %broadcast_in_dim.31), calls=%async_computation | async-start | bytes 32768 | tf_op jit(solution)/shard_map/all_to_all | solution.py:110
  22.0 4.1 %all-to-all-done = f32[16,2,16]{2,1,0:T(2,128)S(1)} async-done(((f32[16,2,16]{2,1,0:T(2,128)}), f32[16,2,16]{2,1,0:T(2,128)S(1)}, u32[]{:S(2)}, u32[]{:S(2)}) %all-to-all-start) | async-done | bytes 2080 | tf_op jit(solution)/shard_map/all_to_all | solution.py:110
  30.3 3.9 %all-to-all-start.2 = ((bf16[32,256,128]{2,1,0:T(8,128)(2,1)}), bf16[32,256,128]{2,1,0:T(8,128)(2,1)S(1)}, u32[]{:S(2)}, u32[]{:S(2)}) async-start(bf16[32,256,128]{2,1,0:T(8,128)(2,1)} %copy.77), calls=%async_computation.2 | async-start | bytes 4194304 | tf_op jit(solution)/shard_map/all_to_all | solution.py:110
  39.8 43.4 %all-to-all-done.2 = bf16[32,256,128]{2,1,0:T(8,128)(2,1)S(1)} async-done(((bf16[32,256,128]{2,1,0:T(8,128)(2,1)}), bf16[32,256,128]{2,1,0:T(8,128)(2,1)S(1)}, u32[]{:S(2)}, u32[]{:S(2)}) %all-to-all-start.2) | async-done | bytes 2097184 | tf_op jit(solution)/shard_map/all_to_all | solution.py:110
  83.2 5.0 %all-to-all-start.1 = ((bf16[32,128,256]{2,1,0:T(8,128)(2,1)}), bf16[32,128,256]{2,1,0:T(8,128)(2,1)}, u32[]{:S(2)}, u32[]{:S(2)}) async-start(bf16[32,128,256]{2,1,0:T(8,128)(2,1)} %copy.74), calls=%async_computation.1 | async-start | bytes 4194304 | tf_op jit(solution)/shard_map/all_to_all | solution.py:110
  88.1 29.0 %all-gather.3.cloned.1.call-done = bf16[22528,128]{1,0:T(8,128)(2,1)} async-done(((bf16[704,128]{1,0:T(8,128)(2,1)}), bf16[22528,128]{1,0:T(8,128)(2,1)}) %all-gather.3.cloned.1.call-update) | async-done | bytes 5767184 | tf_op jit(solution)/shard_map/all_gather | solution.py:158
  117.2 6.5 %shard_map.93 = (f32[352,128]{1,0:T(8,128)}, bf16[16,2,128,256]{3,2,1,0:T(8,128)(2,1)}) custom-call(bf16[32,704,128]{2,1,0:T(8,128)(2,1)} %bitcast.70, bf16[16,2,256,128]{3,2,1,0:T(8,128)(2,1)} %bitcast.72), custom_call_target="tpu_custom_call" | custom-call | tf_op jit(solution)/shard_map/pallas_call | solution.py:39
  123.7 13.6 %all-to-all-done.1 = bf16[32,128,256]{2,1,0:T(8,128)(2,1)} async-done(((bf16[32,128,256]{2,1,0:T(8,128)(2,1)}), bf16[32,128,256]{2,1,0:T(8,128)(2,1)}, u32[]{:S(2)}, u32[]{:S(2)}) %all-to-all-start.1) | async-done | bytes 2097184 | tf_op jit(solution)/shard_map/all_to_all | solution.py:110
  137.2 5.0 %all-to-all-start.4 = ((bf16[32,128,256]{2,1,0:T(8,128)(2,1)}), bf16[32,128,256]{2,1,0:T(8,128)(2,1)S(1)}, u32[]{:S(2)}, u32[]{:S(2)}) async-start(bf16[32,128,256]{2,1,0:T(8,128)(2,1)} %bitcast.75), calls=%async_computation.4 | async-start | bytes 4194304 | tf_op jit(solution)/shard_map/all_to_all | solution.py:110
  142.8 7.6 %shard_map.94 = (bf16[352,128]{1,0:T(8,128)(2,1)}, bf16[16,2,256,128]{3,2,1,0:T(8,128)(2,1)}) custom-call(bf16[32,704,128]{2,1,0:T(8,128)(2,1)} %bitcast.71, bf16[16,2,128,256]{3,2,1,0:T(8,128)(2,1)} %bitcast.5.down_ref, f32[352,128]{1,0:T(8,128)} %get-tuple-element.18.slope_ref), custom_call_target="tpu_custom_call" | custom-call | tf_op jit(solution)/shard_map/pallas_call | solution.py:39
  150.4 4.1 %shard_map.95 = bf16[4,8,352,128]{3,2,1,0:T(8,128)(2,1)} custom-call(s32[2]{0:T(128)} %pad_add_fusion.where_ref, bf16[352,128]{1,0:T(8,128)(2,1)} %get-tuple-element.20.hid_ref, bf16[16,2,256,128]{3,2,1,0:T(8,128)(2,1)} %bitcast.73), custom_call_target="tpu_custom_call" | custom-call | tf_op jit(solution)/shard_map/pallas_call | solution.py:39
  158.0 4.6 %collective-permute-start.2 = (bf16[4,352,128]{2,1,0:T(8,128)(2,1)S(1)}, bf16[4,352,128]{2,1,0:T(8,128)(2,1)S(1)}, u32[]{:S(2)}, u32[]{:S(2)}) collective-permute-start(bf16[4,352,128]{2,1,0:T(8,128)(2,1)S(1)} %get-tuple-element.51), channel_id=1, source_target_pairs={{0,3},{1,0},{2,1},{3,2},{4,7},{5,4},{6,5},{7,6},{8,11},{9,8},{10,9... | collective-permute-start | bytes 1081352 | tf_op jit(solution)/shard_map/ppermute | solution.py:115
  162.6 6.6 %collective-permute-done = bf16[4,352,128]{2,1,0:T(8,128)(2,1)S(1)} collective-permute-done((bf16[4,352,128]{2,1,0:T(8,128)(2,1)S(1)}, bf16[4,352,128]{2,1,0:T(8,128)(2,1)S(1)}, u32[]{:S(2)}, u32[]{:S(2)}) %collective-permute-start) | collective-permute-done | bytes 360480 | tf_op jit(solution)/shard_map/ppermute | solution.py:115
  172.6 5.0 %collective-permute-start.3 = (bf16[8,352,128]{2,1,0:T(8,128)(2,1)S(1)}, bf16[8,352,128]{2,1,0:T(8,128)(2,1)S(1)}, u32[]{:S(2)}, u32[]{:S(2)}) collective-permute-start(bf16[8,352,128]{2,1,0:T(8,128)(2,1)S(1)} %pad_maximum_fusion.1), channel_id=1, source_target_pairs={{0,3},{1,0},{2,1},{3,2},{4,7},{5,4},{6,5},{7,6},{8,11},{9,8},{10,9... | collective-permute-start | bytes 2162696 | tf_op jit(solution)/shard_map/ppermute | solution.py:115
  177.6 13.3 %collective-permute-done.1 = bf16[8,352,128]{2,1,0:T(8,128)(2,1)S(1)} collective-permute-done((bf16[8,352,128]{2,1,0:T(8,128)(2,1)S(1)}, bf16[8,352,128]{2,1,0:T(8,128)(2,1)S(1)}, u32[]{:S(2)}, u32[]{:S(2)}) %collective-permute-start.1) | collective-permute-done | bytes 720928 | tf_op jit(solution)/shard_map/ppermute | solution.py:115
  193.0 8.6 %all-to-all-start.3 = ((bf16[32,256,128]{2,1,0:T(8,128)(2,1)}), bf16[32,256,128]{2,1,0:T(8,128)(2,1)}, u32[]{:S(2)}, u32[]{:S(2)}) async-start(bf16[32,256,128]{2,1,0:T(8,128)(2,1)} %bitcast.74), calls=%async_computation.3 | async-start | bytes 4194304 | tf_op jit(solution)/shard_map/all_to_all | solution.py:110
  203.5 9.8 %collective-permute-start.10 = (bf16[352,128]{1,0:T(8,128)(2,1)S(1)}, bf16[352,128]{1,0:T(8,128)(2,1)S(1)}, u32[]{:S(2)}, u32[]{:S(2)}) collective-permute-start(bf16[352,128]{1,0:T(8,128)(2,1)S(1)} %get-tuple-element.55), channel_id=1, source_target_pairs={{0,28},{4,0},{8,4},{12,8},{16,12},{20,16},{24,20},{28,24},{1,29},{... | collective-permute-start | bytes 270344 | tf_op jit(solution)/shard_map/ppermute | solution.py:115
  217.1 4.5 %collective-permute-start.6 = (bf16[352,128]{1,0:T(8,128)(2,1)}, bf16[352,128]{1,0:T(8,128)(2,1)S(1)}, u32[]{:S(2)}, u32[]{:S(2)}) collective-permute-start(bf16[352,128]{1,0:T(8,128)(2,1)} %get-tuple-element.59), channel_id=1, source_target_pairs={{0,12},{4,16},{8,20},{12,24},{16,28},{20,0},{24,4},{28,8},{1,13},{... | collective-permute-start | bytes 270344 | tf_op jit(solution)/shard_map/ppermute | solution.py:115
  221.7 5.0 %collective-permute-start.7 = (bf16[352,128]{1,0:T(8,128)(2,1)}, bf16[352,128]{1,0:T(8,128)(2,1)}, u32[]{:S(2)}, u32[]{:S(2)}) collective-permute-start(bf16[352,128]{1,0:T(8,128)(2,1)} %get-tuple-element.58), channel_id=1, source_target_pairs={{0,16},{4,20},{8,24},{12,28},{16,0},{20,4},{24,8},{28,12},{1,17},{... | collective-permute-start | bytes 270344 | tf_op jit(solution)/shard_map/ppermute | solution.py:115
  226.6 4.3 %collective-permute-start.8 = (bf16[352,128]{1,0:T(8,128)(2,1)}, bf16[352,128]{1,0:T(8,128)(2,1)}, u32[]{:S(2)}, u32[]{:S(2)}) collective-permute-start(bf16[352,128]{1,0:T(8,128)(2,1)} %get-tuple-element.57), channel_id=1, source_target_pairs={{0,20},{4,24},{8,28},{12,0},{16,4},{20,8},{24,12},{28,16},{1,21},{... | collective-permute-start | bytes 270344 | tf_op jit(solution)/shard_map/ppermute | solution.py:115
  236.9 6.1 %collective-permute-done.9 = bf16[352,128]{1,0:T(8,128)(2,1)} collective-permute-done((bf16[352,128]{1,0:T(8,128)(2,1)}, bf16[352,128]{1,0:T(8,128)(2,1)}, u32[]{:S(2)}, u32[]{:S(2)}) %collective-permute-start.9) | collective-permute-done | bytes 90144 | tf_op jit(solution)/shard_map/ppermute | solution.py:115
  256.7 15.3 %all_to_all.35 = f32[16,2,16]{2,1,0:T(2,128)S(1)} all-to-all(f32[16,2,16]{2,1,0:T(2,128)S(1)} %bitcast.80), channel_id=1, replica_groups=mesh['y'=8,'c'=2,'z'=8,'x'=4] {'y','c'}, dimensions={0} | all-to-all | bytes 4096 | tf_op jit(solution)/shard_map/all_to_all | solution.py:110
  272.7 7.3 %all-to-all-start.6 = ((f32[32,2,16]{2,1,0:T(2,128)}), f32[32,2,16]{2,1,0:T(2,128)S(1)}, u32[]{:S(2)}, u32[]{:S(2)}) async-start(f32[32,2,16]{2,1,0:T(2,128)} %broadcast_in_dim.32), calls=%async_computation.6 | async-start | bytes 65536 | tf_op jit(solution)/shard_map/all_to_all | solution.py:110
  280.1 3.5 %fusion.6 = bf16[16,256,128]{2,0,1:T(8,128)(2,1)S(1)} fusion(f32[32,16,1]{1,0,2:T(8,128)S(1)} %bitcast.79, bf16[32,256,128]{2,1,0:T(8,128)(2,1)} %all-to-all-done.3), kind=kOutput, calls=%fused_computation.8 | convolution fusion | flops 201850880 | bytes 3147776 | tf_op jit(solution)/shard_map/ke,kdh->edh/dot_general | solution.py:205
  (53 shorter events, 54.9 us)
Async XLA Ops:
  7.2 19.0 %copy-start = (bf16[16,256,128]{2,1,0:T(8,128)(2,1)S(1)}, bf16[16,256,128]{2,1,0:T(8,128)(2,1)}, u32[]{:S(2)}) copy-start(bf16[16,256,128]{2,1,0:T(8,128)(2,1)} %param.10) | copy-start | bytes 3145732
  8.6 17.6 %all-to-all-start = ((f32[16,2,16]{2,1,0:T(2,128)}), f32[16,2,16]{2,1,0:T(2,128)S(1)}, u32[]{:S(2)}, u32[]{:S(2)}) async-start(f32[16,2,16]{2,1,0:T(2,128)} %broadcast_in_dim.31), calls=%async_computation | async-start | bytes 32768 | tf_op jit(solution)/shard_map/all_to_all | solution.py:110
  18.7 98.5 %all-gather.3.cloned.1.call-start = ((), (), s32[]{:S(2)}) async-start(), calls=%async_computation.7 | async-start | bytes 5947392 | tf_op jit(solution)/shard_map/all_gather | solution.py:158
  30.3 52.9 %all-to-all-start.2 = ((bf16[32,256,128]{2,1,0:T(8,128)(2,1)}), bf16[32,256,128]{2,1,0:T(8,128)(2,1)S(1)}, u32[]{:S(2)}, u32[]{:S(2)}) async-start(bf16[32,256,128]{2,1,0:T(8,128)(2,1)} %copy.77), calls=%async_computation.2 | async-start | bytes 4194304 | tf_op jit(solution)/shard_map/all_to_all | solution.py:110
  83.2 34.0 %copy-start.1 = (bf16[32,256,128]{2,1,0:T(8,128)(2,1)}, bf16[32,256,128]{2,1,0:T(8,128)(2,1)S(1)}, u32[]{:S(2)}) copy-start(bf16[32,256,128]{2,1,0:T(8,128)(2,1)S(1)} %all-to-all-done.2) | copy-start | bytes 6291460
  83.2 54.0 %all-to-all-start.1 = ((bf16[32,128,256]{2,1,0:T(8,128)(2,1)}), bf16[32,128,256]{2,1,0:T(8,128)(2,1)}, u32[]{:S(2)}, u32[]{:S(2)}) async-start(bf16[32,128,256]{2,1,0:T(8,128)(2,1)} %copy.74), calls=%async_computation.1 | async-start | bytes 4194304 | tf_op jit(solution)/shard_map/all_to_all | solution.py:110
  137.2 55.8 %all-to-all-start.4 = ((bf16[32,128,256]{2,1,0:T(8,128)(2,1)}), bf16[32,128,256]{2,1,0:T(8,128)(2,1)S(1)}, u32[]{:S(2)}, u32[]{:S(2)}) async-start(bf16[32,128,256]{2,1,0:T(8,128)(2,1)} %bitcast.75), calls=%async_computation.4 | async-start | bytes 4194304 | tf_op jit(solution)/shard_map/all_to_all | solution.py:110
  154.5 15.5 %copy-start.2 = (bf16[4,8,352,128]{3,2,1,0:T(8,128)(2,1)S(1)}, bf16[4,8,352,128]{3,2,1,0:T(8,128)(2,1)}, u32[]{:S(2)}) copy-start(bf16[4,8,352,128]{3,2,1,0:T(8,128)(2,1)} %shard_map.95) | copy-start | bytes 8650756
  156.1 13.1 %collective-permute-start = (bf16[4,352,128]{2,1,0:T(8,128)(2,1)S(1)}, bf16[4,352,128]{2,1,0:T(8,128)(2,1)S(1)}, u32[]{:S(2)}, u32[]{:S(2)}) collective-permute-start(bf16[4,352,128]{2,1,0:T(8,128)(2,1)S(1)} %get-tuple-element.50), channel_id=1, source_target_pairs={{0,1},{1,2},{2,3},{3,0},{4,5},{5,6},{6,7},{7,4},{8,9},{9,10},{10,1... | collective-permute-start | bytes 1081352 | tf_op jit(solution)/shard_map/ppermute | solution.py:115
  158.0 12.0 %collective-permute-start.2 = (bf16[4,352,128]{2,1,0:T(8,128)(2,1)S(1)}, bf16[4,352,128]{2,1,0:T(8,128)(2,1)S(1)}, u32[]{:S(2)}, u32[]{:S(2)}) collective-permute-start(bf16[4,352,128]{2,1,0:T(8,128)(2,1)S(1)} %get-tuple-element.51), channel_id=1, source_target_pairs={{0,3},{1,0},{2,1},{3,2},{4,7},{5,4},{6,5},{7,6},{8,11},{9,8},{10,9... | collective-permute-start | bytes 1081352 | tf_op jit(solution)/shard_map/ppermute | solution.py:115
  170.3 20.6 %collective-permute-start.1 = (bf16[8,352,128]{2,1,0:T(8,128)(2,1)S(1)}, bf16[8,352,128]{2,1,0:T(8,128)(2,1)S(1)}, u32[]{:S(2)}, u32[]{:S(2)}) collective-permute-start(bf16[8,352,128]{2,1,0:T(8,128)(2,1)S(1)} %pad_maximum_fusion), channel_id=1, source_target_pairs={{0,1},{1,2},{2,3},{3,0},{4,5},{5,6},{6,7},{7,4},{8,9},{9,10},{10,1... | collective-permute-start | bytes 2162696 | tf_op jit(solution)/shard_map/ppermute | solution.py:115
  172.6 19.2 %collective-permute-start.3 = (bf16[8,352,128]{2,1,0:T(8,128)(2,1)S(1)}, bf16[8,352,128]{2,1,0:T(8,128)(2,1)S(1)}, u32[]{:S(2)}, u32[]{:S(2)}) collective-permute-start(bf16[8,352,128]{2,1,0:T(8,128)(2,1)S(1)} %pad_maximum_fusion.1), channel_id=1, source_target_pairs={{0,3},{1,0},{2,1},{3,2},{4,7},{5,4},{6,5},{7,6},{8,11},{9,8},{10,9... | collective-permute-start | bytes 2162696 | tf_op jit(solution)/shard_map/ppermute | solution.py:115
  193.0 60.3 %all-to-all-start.3 = ((bf16[32,256,128]{2,1,0:T(8,128)(2,1)}), bf16[32,256,128]{2,1,0:T(8,128)(2,1)}, u32[]{:S(2)}, u32[]{:S(2)}) async-start(bf16[32,256,128]{2,1,0:T(8,128)(2,1)} %bitcast.74), calls=%async_computation.3 | async-start | bytes 4194304 | tf_op jit(solution)/shard_map/all_to_all | solution.py:110
  203.5 23.1 %collective-permute-start.10 = (bf16[352,128]{1,0:T(8,128)(2,1)S(1)}, bf16[352,128]{1,0:T(8,128)(2,1)S(1)}, u32[]{:S(2)}, u32[]{:S(2)}) collective-permute-start(bf16[352,128]{1,0:T(8,128)(2,1)S(1)} %get-tuple-element.55), channel_id=1, source_target_pairs={{0,28},{4,0},{8,4},{12,8},{16,12},{20,16},{24,20},{28,24},{1,29},{... | collective-permute-start | bytes 270344 | tf_op jit(solution)/shard_map/ppermute | solution.py:115
  213.3 17.6 %collective-permute-start.4 = (bf16[352,128]{1,0:T(8,128)(2,1)S(1)}, bf16[352,128]{1,0:T(8,128)(2,1)S(1)}, u32[]{:S(2)}, u32[]{:S(2)}) collective-permute-start(bf16[352,128]{1,0:T(8,128)(2,1)S(1)} %get-tuple-element.54), channel_id=1, source_target_pairs={{0,4},{4,8},{8,12},{12,16},{16,20},{20,24},{24,28},{28,0},{1,5},{5... | collective-permute-start | bytes 270344 | tf_op jit(solution)/shard_map/ppermute | solution.py:115
  215.2 21.7 %collective-permute-start.5 = (bf16[352,128]{1,0:T(8,128)(2,1)}, bf16[352,128]{1,0:T(8,128)(2,1)S(1)}, u32[]{:S(2)}, u32[]{:S(2)}) collective-permute-start(bf16[352,128]{1,0:T(8,128)(2,1)} %get-tuple-element.60), channel_id=1, source_target_pairs={{0,8},{4,12},{8,16},{12,20},{16,24},{20,28},{24,0},{28,4},{1,9},{5... | collective-permute-start | bytes 270344 | tf_op jit(solution)/shard_map/ppermute | solution.py:115
  217.1 19.8 %collective-permute-start.6 = (bf16[352,128]{1,0:T(8,128)(2,1)}, bf16[352,128]{1,0:T(8,128)(2,1)S(1)}, u32[]{:S(2)}, u32[]{:S(2)}) collective-permute-start(bf16[352,128]{1,0:T(8,128)(2,1)} %get-tuple-element.59), channel_id=1, source_target_pairs={{0,12},{4,16},{8,20},{12,24},{16,28},{20,0},{24,4},{28,8},{1,13},{... | collective-permute-start | bytes 270344 | tf_op jit(solution)/shard_map/ppermute | solution.py:115
  221.7 15.3 %collective-permute-start.7 = (bf16[352,128]{1,0:T(8,128)(2,1)}, bf16[352,128]{1,0:T(8,128)(2,1)}, u32[]{:S(2)}, u32[]{:S(2)}) collective-permute-start(bf16[352,128]{1,0:T(8,128)(2,1)} %get-tuple-element.58), channel_id=1, source_target_pairs={{0,16},{4,20},{8,24},{12,28},{16,0},{20,4},{24,8},{28,12},{1,17},{... | collective-permute-start | bytes 270344 | tf_op jit(solution)/shard_map/ppermute | solution.py:115
  226.6 10.3 %collective-permute-start.8 = (bf16[352,128]{1,0:T(8,128)(2,1)}, bf16[352,128]{1,0:T(8,128)(2,1)}, u32[]{:S(2)}, u32[]{:S(2)}) collective-permute-start(bf16[352,128]{1,0:T(8,128)(2,1)} %get-tuple-element.57), channel_id=1, source_target_pairs={{0,20},{4,24},{8,28},{12,0},{16,4},{20,8},{24,12},{28,16},{1,21},{... | collective-permute-start | bytes 270344 | tf_op jit(solution)/shard_map/ppermute | solution.py:115
  230.9 12.1 %collective-permute-start.9 = (bf16[352,128]{1,0:T(8,128)(2,1)}, bf16[352,128]{1,0:T(8,128)(2,1)}, u32[]{:S(2)}, u32[]{:S(2)}) collective-permute-start(bf16[352,128]{1,0:T(8,128)(2,1)} %get-tuple-element.56), channel_id=1, source_target_pairs={{0,24},{4,28},{8,0},{12,4},{16,8},{20,12},{24,16},{28,20},{1,25},{... | collective-permute-start | bytes 270344 | tf_op jit(solution)/shard_map/ppermute | solution.py:115
  272.7 15.7 %all-to-all-start.6 = ((f32[32,2,16]{2,1,0:T(2,128)}), f32[32,2,16]{2,1,0:T(2,128)S(1)}, u32[]{:S(2)}, u32[]{:S(2)}) async-start(f32[32,2,16]{2,1,0:T(2,128)} %broadcast_in_dim.32), calls=%async_computation.6 | async-start | bytes 65536 | tf_op jit(solution)/shard_map/all_to_all | solution.py:110
  280.0 4.8 %copy-start.3 = (bf16[16,128,256]{2,0,1:T(8,128)(2,1)S(1)}, bf16[16,128,256]{2,0,1:T(8,128)(2,1)}, u32[]{:S(2)}) copy-start(bf16[16,128,256]{2,0,1:T(8,128)(2,1)} %fusion.9) | copy-start | bytes 3145732
Sparse Core Ops, SparseCore 0:
  26.3 90.8 all-gather.2

commit v4 on v3

--- a/solution.py
+++ b/solution.py
@@ -56,7 +56,7 @@
 
 
 def pre_kernel(full_ref, up_ref, slope_ref, term_ref):
-    slices, segments = up_ref.shape[0], up_ref.shape[1]
+    slices, segments = term_ref.shape[0], term_ref.shape[1]
     group_rows = slope_ref.shape[0]
     rows = group_rows // segments
     for s in range(segments):
@@ -64,24 +64,33 @@
         for i in range(slices):
             pre = pre + dot(pair(full_ref, i, s * rows, rows), up_ref[i, s], 1, 0)
         activated, derivative = gelu_pair(pre)
-        activated = activated.astype(jnp.bfloat16)
+        turned = activated.astype(jnp.bfloat16).T
         slope_ref[pl.ds(s * rows, rows), :] = derivative
         for i in range(slices):
-            term_ref[i, s] = dot(
-                activated, pair(full_ref, i, group_rows + s * rows, rows), 0, 0
-            ).astype(jnp.bfloat16)
-
-
-def back_kernel(full_ref, down_ref, slope_ref, hid_ref, term_ref):
+            term = dot(turned, pair(full_ref, i, group_rows + s * rows, rows), 1, 0)
+            for half in range(2):
+                at = slice(half * 128, (half + 1) * 128)
+                term_ref[i, s, at, :] = term[:, at].astype(jnp.bfloat16)
+
+
+def back_kernel(full_ref, down_ref, slope_ref, hid_ref):
     slices, segments = down_ref.shape[0], down_ref.shape[1]
-    group_rows = slope_ref.shape[0]
+    group_rows, hidden = slope_ref.shape
     rows = group_rows // segments
     for s in range(segments):
-        back = jnp.zeros((rows, slope_ref.shape[1]), jnp.float32)
+        back = jnp.zeros((rows, hidden), jnp.float32)
         for i in range(slices):
             back = back + dot(pair(full_ref, i, group_rows + s * rows, rows), down_ref[i, s], 1, 1)
-        hidden = (back * slope_ref[pl.ds(s * rows, rows), :]).astype(jnp.bfloat16)
-        hid_ref[pl.ds(s * rows, rows), :] = hidden
+        hid_ref[pl.ds(s * rows, rows), :] = (
+            back * slope_ref[pl.ds(s * rows, rows), :]
+        ).astype(jnp.bfloat16)
+
+
+def up_kernel(full_ref, hid_ref, term_ref):
+    slices, segments = term_ref.shape[0], term_ref.shape[1]
+    rows = hid_ref.shape[0] // segments
+    for s in range(segments):
+        hidden = hid_ref[pl.ds(s * rows, rows), :]
         for i in range(slices):
             term_ref[i, s] = dot(pair(full_ref, i, s * rows, rows), hidden, 0, 0).astype(
                 jnp.bfloat16
@@ -157,51 +166,49 @@
     both, all_routes = lax.optimization_barrier((both, all_routes))
     full = lax.all_gather(both, TENSOR)
     flat_routes = all_routes.reshape(-1, experts)
-    local_up = jnp.einsum(
-        "ke,edh->kdh", flat_routes, up_weight.astype(jnp.float32), precision=high
-    ).astype(bf16)
-    merged_up = exchange(local_up, DP).reshape(n_dp, segments, width, hidden)
-    local_down = jnp.einsum(
-        "ke,ehd->khd", flat_routes, down_weight.astype(jnp.float32), precision=high
-    ).astype(bf16)
-    merged_down = exchange(local_down, DP).reshape(n_dp, segments, hidden, width)
+    def merge(weight):
+        return jnp.einsum(
+            "ke,eab->kab", flat_routes, weight.astype(jnp.float32), precision=high
+        ).astype(bf16)
+
+    merged_up = exchange(merge(up_weight), DP).reshape(n_dp, segments, width, hidden)
+    merged_down = exchange(merge(down_weight), DP).reshape(n_dp, segments, hidden, width)
+    down_halves = jnp.concatenate([down_weight[:, :, :lanes], down_weight[:, :, lanes:]], axis=1)
+    merged_up, down_halves = lax.optimization_barrier((merged_up, down_halves))
 
     slope, down_terms = local_kernel(
         pre_kernel,
         (
             shape((group_rows, hidden), jnp.float32),
-            shape((n_dp, segments, hidden, width), bf16),
+            shape((n_dp, segments, width, hidden), bf16),
         ),
         0,
         full,
         merged_up,
     )
-    down_terms = exchange(down_terms.reshape(-1, hidden, width), DP)
-    hid, up_terms = local_kernel(
-        back_kernel,
-        (shape((group_rows, hidden), bf16), shape((n_dp, segments, width, hidden), bf16)),
-        0,
-        full,
-        merged_down,
-        slope,
+    down_terms = exchange(down_terms.reshape(-1, 2 * hidden, lanes), DP)
+    hid = local_kernel(
+        back_kernel, shape((group_rows, hidden), bf16), 0, full, merged_down, slope
     )
     parts = local_kernel(
         input_kernel, shape((n_x, n_z, group_rows, lanes), bf16), 1, here, hid, merged_up
+    )
+    up_terms = local_kernel(
+        up_kernel, shape((n_dp, segments, width, hidden), bf16), 0, full, hid
     )
     right, left = start_sum(parts)
     near = second_hop(parts[0], right, left)
     up_terms, near = lax.optimization_barrier((up_terms, near))
     summed = finish_sum(near)
     down_grad = jnp.einsum(
-        "ke,khd->ehd", flat_routes, down_terms.astype(jnp.float32), precision=high
+        "ke,kab->eab", flat_routes, down_terms.astype(jnp.float32), precision=high
     ).astype(bf16)
+    down_grad = jnp.concatenate([down_grad[:, :hidden], down_grad[:, hidden:]], axis=2)
     down_inner = jnp.einsum(
-        "khd,ehd->ke", down_terms, down_weight, preferred_element_type=jnp.float32
+        "kab,eab->ke", down_terms, down_halves, preferred_element_type=jnp.float32
     )
     up_terms = exchange(up_terms.reshape(-1, width, hidden), DP)
-    up_terms, down_grad, down_inner, summed = lax.optimization_barrier(
-        (up_terms, down_grad, down_inner, summed)
-    )
+    up_terms, down_inner = lax.optimization_barrier((up_terms, down_inner))
     up_grad = jnp.einsum(
         "ke,kdh->edh", flat_routes, up_terms.astype(jnp.float32), precision=high
     ).astype(bf16)

time: 297 us -> 296 us (level)
  blocking collectives: 15.3 us -> 0 us
  waiting for transfers between devices: 120 us -> 129 us
  starting transfers between devices: 84.5 us -> 89.5 us
  local copies, waits for them, and re-layouts: 18.6 us -> 15.2 us
  other arithmetic: 7.03 us -> 10.1 us
    all_to_all x1 -> x0, blocking collectives: 15.3 us -> none  [exchange(): return lax.all_to_all(value, axes, split_axis=0, concat_axis=0, tiled=True)]
    all_to_all x6 -> x7, waiting for transfers between devices: 63.3 us -> 74.8 us  [exchange(): return lax.all_to_all(value, axes, split_axis=0, concat_axis=0, tiled=True)]
    all_to_all x6 -> x7, starting transfers between devices: 40 us -> 46.7 us  [exchange(): return lax.all_to_all(value, axes, split_axis=0, concat_axis=0, tiled=True)]
    all_to_all x1 -> x0, local copies, waits for them, and re-layouts: 3.11 us -> none  [exchange(): return lax.all_to_all(value, axes, split_axis=0, concat_axis=0, tiled=True)]
    pallas_call x3 -> x4, Pallas kernels: 18.2 us -> 20.9 us  [local_kernel(): pl.pallas_call(kernel, out_shape=out_shapes, in_specs=smem + vmem(len(arg...]
  transfers between devices with their start and end apart: 18 -> 19, of which waited for: 10 -> 14; matrix products, arithmetic and copies ran while one was open for 12% -> 12% of each run, Pallas kernels for 6% -> 7%
where the time goes in v4:
time: 296 us; the launch traced here: 295 us
  waiting for transfers between devices  129 us (44%)
  starting transfers between devices  89.5 us (30%)
  Pallas kernels  20.9 us (7%)
  matrix products  15.7 us (5%)
  local copies, waits for them, and re-layouts  15.2 us (5%)
  between operations  14.9 us (5%)
  other arithmetic  10.1 us (3%)
    all_to_all x7, waiting for transfers between devices, exchange(): return lax.all_to_all(value, axes, split_axis=0, concat_axis=0, tiled=True)  74.8 us
    all_to_all x7, starting transfers between devices, exchange(): return lax.all_to_all(value, axes, split_axis=0, concat_axis=0, tiled=True)  46.7 us
    ppermute x11, starting transfers between devices, shift(): lax.ppermute(value, axis, [(i, (i + by) % size) for i in range(size)])  42.7 us
    ppermute x11, waiting for transfers between devices, shift(): lax.ppermute(value, axis, [(i, (i + by) % size) for i in range(size)])  27.6 us
    all_gather x1, waiting for transfers between devices, body(): full = lax.all_gather(both, TENSOR)  26.7 us
    pallas_call x4, Pallas kernels, local_kernel(): pl.pallas_call(kernel, out_shape=out_shapes, in_specs=smem + vmem(len(arg...  20.9 us
  transfers between devices with their start and end apart: 19, of which 14 were waited for; matrix products, arithmetic and copies ran while one was open for 12% of the time, Pallas kernels for 7%

profile of v4, /device:TPU:1, one launch (start us, length us, event | category | flops | bytes accessed | tf_op | source)
XLA Modules:
  0.0 295.3 jit_solution(5434260895584010408)
XLA Ops:
  8.6 10.2 %all-to-all-start = ((f32[16,2,16]{2,1,0:T(2,128)}), f32[16,2,16]{2,1,0:T(2,128)S(1)}, u32[]{:S(2)}, u32[]{:S(2)}) async-start(f32[16,2,16]{2,1,0:T(2,128)} %broadcast_in_dim.31), calls=%async_computation | async-start | bytes 32768 | tf_op jit(solution)/shard_map/all_to_all | solution.py:119
  22.0 4.1 %all-to-all-done = f32[16,2,16]{2,1,0:T(2,128)S(1)} async-done(((f32[16,2,16]{2,1,0:T(2,128)}), f32[16,2,16]{2,1,0:T(2,128)S(1)}, u32[]{:S(2)}, u32[]{:S(2)}) %all-to-all-start) | async-done | bytes 2080 | tf_op jit(solution)/shard_map/all_to_all | solution.py:119
  39.7 43.4 %all-to-all-done.2 = bf16[32,256,128]{2,1,0:T(8,128)(2,1)S(1)} async-done(((bf16[32,256,128]{2,1,0:T(8,128)(2,1)}), bf16[32,256,128]{2,1,0:T(8,128)(2,1)S(1)}, u32[]{:S(2)}, u32[]{:S(2)}) %all-to-all-start.2) | async-done | bytes 2097184 | tf_op jit(solution)/shard_map/all_to_all | solution.py:119
  83.1 5.0 %all-to-all-start.1 = ((bf16[32,128,256]{2,1,0:T(8,128)(2,1)}), bf16[32,128,256]{2,1,0:T(8,128)(2,1)}, u32[]{:S(2)}, u32[]{:S(2)}) async-start(bf16[32,128,256]{2,1,0:T(8,128)(2,1)} %copy.72), calls=%async_computation.1 | async-start | bytes 4194304 | tf_op jit(solution)/shard_map/all_to_all | solution.py:119
  90.5 26.7 %all-gather.3.cloned.1.call-done = bf16[22528,128]{1,0:T(8,128)(2,1)} async-done(((bf16[704,128]{1,0:T(8,128)(2,1)}), bf16[22528,128]{1,0:T(8,128)(2,1)}) %all-gather.3.cloned.1.call-update) | async-done | bytes 5767184 | tf_op jit(solution)/shard_map/all_gather | solution.py:167
  117.2 6.5 %shard_map.93 = (f32[352,128]{1,0:T(8,128)}, bf16[16,2,256,128]{3,2,1,0:T(8,128)(2,1)}) custom-call(bf16[32,704,128]{2,1,0:T(8,128)(2,1)} %bitcast.68, bf16[16,2,256,128]{3,2,1,0:T(8,128)(2,1)} %bitcast.71), custom_call_target="tpu_custom_call" | custom-call | tf_op jit(solution)/shard_map/pallas_call | solution.py:39
  123.7 13.5 %all-to-all-done.1 = bf16[32,128,256]{2,1,0:T(8,128)(2,1)} async-done(((bf16[32,128,256]{2,1,0:T(8,128)(2,1)}), bf16[32,128,256]{2,1,0:T(8,128)(2,1)}, u32[]{:S(2)}, u32[]{:S(2)}) %all-to-all-start.1) | async-done | bytes 2097184 | tf_op jit(solution)/shard_map/all_to_all | solution.py:119
  137.2 5.0 %all-to-all-start.4 = ((bf16[32,256,128]{2,1,0:T(8,128)(2,1)}), bf16[32,256,128]{2,1,0:T(8,128)(2,1)S(1)}, u32[]{:S(2)}, u32[]{:S(2)}) async-start(bf16[32,256,128]{2,1,0:T(8,128)(2,1)} %bitcast.73), calls=%async_computation.4 | async-start | bytes 4194304 | tf_op jit(solution)/shard_map/all_to_all | solution.py:119
  142.8 4.8 %shard_map.94.hid_ref = bf16[352,128]{1,0:T(8,128)(2,1)} custom-call(bf16[32,704,128]{2,1,0:T(8,128)(2,1)} %bitcast.69, bf16[16,2,128,256]{3,2,1,0:T(8,128)(2,1)} %bitcast.5.down_ref, f32[352,128]{1,0:T(8,128)} %get-tuple-element.17.slope_ref), custom_call_target="tpu_custom_call" | custom-call | tf_op jit(solution)/shard_map/pallas_call | solution.py:39
  147.6 4.2 %shard_map.96 = bf16[4,8,352,128]{3,2,1,0:T(8,128)(2,1)} custom-call(s32[2]{0:T(128)} %pad_add_fusion.where_ref, bf16[352,128]{1,0:T(8,128)(2,1)} %shard_map.94.hid_ref, bf16[16,2,256,128]{3,2,1,0:T(8,128)(2,1)} %bitcast.72), custom_call_target="tpu_custom_call" | custom-call | tf_op jit(solution)/shard_map/pallas_call | solution.py:39
  155.3 4.6 %collective-permute-start.2 = (bf16[4,352,128]{2,1,0:T(8,128)(2,1)S(1)}, bf16[4,352,128]{2,1,0:T(8,128)(2,1)S(1)}, u32[]{:S(2)}, u32[]{:S(2)}) collective-permute-start(bf16[4,352,128]{2,1,0:T(8,128)(2,1)S(1)} %get-tuple-element.47), channel_id=1, source_target_pairs={{0,3},{1,0},{2,1},{3,2},{4,7},{5,4},{6,5},{7,6},{8,11},{9,8},{10,9... | collective-permute-start | bytes 1081352 | tf_op jit(solution)/shard_map/ppermute | solution.py:124
  159.9 6.6 %collective-permute-done = bf16[4,352,128]{2,1,0:T(8,128)(2,1)S(1)} collective-permute-done((bf16[4,352,128]{2,1,0:T(8,128)(2,1)S(1)}, bf16[4,352,128]{2,1,0:T(8,128)(2,1)S(1)}, u32[]{:S(2)}, u32[]{:S(2)}) %collective-permute-start) | collective-permute-done | bytes 360480 | tf_op jit(solution)/shard_map/ppermute | solution.py:124
  168.5 5.3 %collective-permute-start.3 = (bf16[8,352,128]{2,1,0:T(8,128)(2,1)}, bf16[8,352,128]{2,1,0:T(8,128)(2,1)}, u32[]{:S(2)}, u32[]{:S(2)}) collective-permute-start(bf16[8,352,128]{2,1,0:T(8,128)(2,1)} %pad_maximum_fusion.3), channel_id=1, source_target_pairs={{0,3},{1,0},{2,1},{3,2},{4,7},{5,4},{6,5},{7,6},{8,11},{9,8},{10,9... | collective-permute-start | bytes 2162696 | tf_op jit(solution)/shard_map/ppermute | solution.py:124
  176.0 5.4 %shard_map.95 = bf16[16,2,256,128]{3,2,1,0:T(8,128)(2,1)} custom-call(bf16[32,704,128]{2,1,0:T(8,128)(2,1)} %bitcast.70, bf16[352,128]{1,0:T(8,128)(2,1)} %shard_map.94.hid_ref), custom_call_target="tpu_custom_call" | custom-call | tf_op jit(solution)/shard_map/pallas_call | solution.py:39
  181.3 7.0 %collective-permute-done.3 = bf16[8,352,128]{2,1,0:T(8,128)(2,1)} collective-permute-done((bf16[8,352,128]{2,1,0:T(8,128)(2,1)}, bf16[8,352,128]{2,1,0:T(8,128)(2,1)}, u32[]{:S(2)}, u32[]{:S(2)}) %collective-permute-start.3) | collective-permute-done | bytes 720928 | tf_op jit(solution)/shard_map/ppermute | solution.py:124
  188.3 4.8 %collective-permute-done.1 = bf16[8,352,128]{2,1,0:T(8,128)(2,1)S(1)} collective-permute-done((bf16[8,352,128]{2,1,0:T(8,128)(2,1)S(1)}, bf16[8,352,128]{2,1,0:T(8,128)(2,1)S(1)}, u32[]{:S(2)}, u32[]{:S(2)}) %collective-permute-start.1) | collective-permute-done | bytes 720928 | tf_op jit(solution)/shard_map/ppermute | solution.py:124
  195.4 8.9 %all-to-all-start.3 = ((bf16[32,256,128]{2,1,0:T(8,128)(2,1)}), bf16[32,256,128]{2,1,0:T(8,128)(2,1)}, u32[]{:S(2)}, u32[]{:S(2)}) async-start(bf16[32,256,128]{2,1,0:T(8,128)(2,1)} %bitcast.26), calls=%async_computation.3 | async-start | bytes 4194304 | tf_op jit(solution)/shard_map/all_to_all | solution.py:119
  205.5 9.0 %collective-permute-start.10 = (bf16[352,128]{1,0:T(8,128)(2,1)S(1)}, bf16[352,128]{1,0:T(8,128)(2,1)S(1)}, u32[]{:S(2)}, u32[]{:S(2)}) collective-permute-start(bf16[352,128]{1,0:T(8,128)(2,1)S(1)} %get-tuple-element.55), channel_id=1, source_target_pairs={{0,28},{4,0},{8,4},{12,8},{16,12},{20,16},{24,20},{28,24},{1,29},{... | collective-permute-start | bytes 270344 | tf_op jit(solution)/shard_map/ppermute | solution.py:124
  218.6 7.3 %collective-permute-start.7 = (bf16[352,128]{1,0:T(8,128)(2,1)S(1)}, bf16[352,128]{1,0:T(8,128)(2,1)S(1)}, u32[]{:S(2)}, u32[]{:S(2)}) collective-permute-start(bf16[352,128]{1,0:T(8,128)(2,1)S(1)} %get-tuple-element.58), channel_id=1, source_target_pairs={{0,16},{4,20},{8,24},{12,28},{16,0},{20,4},{24,8},{28,12},{1,17},{... | collective-permute-start | bytes 270344 | tf_op jit(solution)/shard_map/ppermute | solution.py:124
  236.0 5.7 %collective-permute-done.5 = bf16[352,128]{1,0:T(8,128)(2,1)S(1)} collective-permute-done((bf16[352,128]{1,0:T(8,128)(2,1)S(1)}, bf16[352,128]{1,0:T(8,128)(2,1)S(1)}, u32[]{:S(2)}, u32[]{:S(2)}) %collective-permute-start.5) | collective-permute-done | bytes 90144 | tf_op jit(solution)/shard_map/ppermute | solution.py:124
  257.4 5.0 %all-to-all-start.5 = ((f32[16,2,16]{2,1,0:T(2,128)}), f32[16,2,16]{2,1,0:T(2,128)S(1)}, u32[]{:S(2)}, u32[]{:S(2)}) async-start(f32[16,2,16]{2,1,0:T(2,128)} %bitcast.31), calls=%async_computation.5 | async-start | bytes 32768 | tf_op jit(solution)/shard_map/all_to_all | solution.py:119
  263.8 5.8 %all-to-all-done.5 = f32[16,2,16]{2,1,0:T(2,128)S(1)} async-done(((f32[16,2,16]{2,1,0:T(2,128)}), f32[16,2,16]{2,1,0:T(2,128)S(1)}, u32[]{:S(2)}, u32[]{:S(2)}) %all-to-all-start.5) | async-done | bytes 2080 | tf_op jit(solution)/shard_map/all_to_all | solution.py:119
  270.3 8.8 %all-to-all-start.6 = ((f32[32,2,16]{2,1,0:T(2,128)}), f32[32,2,16]{2,1,0:T(2,128)S(1)}, u32[]{:S(2)}, u32[]{:S(2)}) async-start(f32[32,2,16]{2,1,0:T(2,128)} %broadcast_in_dim.32), calls=%async_computation.6 | async-start | bytes 65536 | tf_op jit(solution)/shard_map/all_to_all | solution.py:119
  283.8 4.0 %all-to-all-done.6 = f32[32,2,16]{2,1,0:T(2,128)S(1)} async-done(((f32[32,2,16]{2,1,0:T(2,128)}), f32[32,2,16]{2,1,0:T(2,128)S(1)}, u32[]{:S(2)}, u32[]{:S(2)}) %all-to-all-start.6) | async-done | bytes 4128 | tf_op jit(solution)/shard_map/all_to_all | solution.py:119
  (61 shorter events, 68.8 us)
Async XLA Ops:
  7.2 19.0 %copy-start = (bf16[16,256,128]{2,1,0:T(8,128)(2,1)S(1)}, bf16[16,256,128]{2,1,0:T(8,128)(2,1)}, u32[]{:S(2)}) copy-start(bf16[16,256,128]{2,1,0:T(8,128)(2,1)} %param.10) | copy-start | bytes 3145732
  8.6 17.6 %all-to-all-start = ((f32[16,2,16]{2,1,0:T(2,128)}), f32[16,2,16]{2,1,0:T(2,128)S(1)}, u32[]{:S(2)}, u32[]{:S(2)}) async-start(f32[16,2,16]{2,1,0:T(2,128)} %broadcast_in_dim.31), calls=%async_computation | async-start | bytes 32768 | tf_op jit(solution)/shard_map/all_to_all | solution.py:119
  18.7 98.5 %all-gather.3.cloned.1.call-start = ((), (), s32[]{:S(2)}) async-start(), calls=%async_computation.7 | async-start | bytes 5947392 | tf_op jit(solution)/shard_map/all_gather | solution.py:167
  30.2 52.9 %all-to-all-start.2 = ((bf16[32,256,128]{2,1,0:T(8,128)(2,1)}), bf16[32,256,128]{2,1,0:T(8,128)(2,1)S(1)}, u32[]{:S(2)}, u32[]{:S(2)}) async-start(bf16[32,256,128]{2,1,0:T(8,128)(2,1)} %copy.75), calls=%async_computation.2 | async-start | bytes 4194304 | tf_op jit(solution)/shard_map/all_to_all | solution.py:119
  83.1 6.3 %copy-start.1 = (bf16[32,256,128]{2,1,0:T(8,128)(2,1)}, bf16[32,256,128]{2,1,0:T(8,128)(2,1)S(1)}, u32[]{:S(2)}) copy-start(bf16[32,256,128]{2,1,0:T(8,128)(2,1)S(1)} %all-to-all-done.2) | copy-start | bytes 6291460
  83.1 54.0 %all-to-all-start.1 = ((bf16[32,128,256]{2,1,0:T(8,128)(2,1)}), bf16[32,128,256]{2,1,0:T(8,128)(2,1)}, u32[]{:S(2)}, u32[]{:S(2)}) async-start(bf16[32,128,256]{2,1,0:T(8,128)(2,1)} %copy.72), calls=%async_computation.1 | async-start | bytes 4194304 | tf_op jit(solution)/shard_map/all_to_all | solution.py:119
  137.2 58.2 %all-to-all-start.4 = ((bf16[32,256,128]{2,1,0:T(8,128)(2,1)}), bf16[32,256,128]{2,1,0:T(8,128)(2,1)S(1)}, u32[]{:S(2)}, u32[]{:S(2)}) async-start(bf16[32,256,128]{2,1,0:T(8,128)(2,1)} %bitcast.73), calls=%async_computation.4 | async-start | bytes 4194304 | tf_op jit(solution)/shard_map/all_to_all | solution.py:119
  151.8 15.5 %copy-start.2 = (bf16[4,8,352,128]{3,2,1,0:T(8,128)(2,1)S(1)}, bf16[4,8,352,128]{3,2,1,0:T(8,128)(2,1)}, u32[]{:S(2)}) copy-start(bf16[4,8,352,128]{3,2,1,0:T(8,128)(2,1)} %shard_map.96) | copy-start | bytes 8650756
  153.4 13.1 %collective-permute-start = (bf16[4,352,128]{2,1,0:T(8,128)(2,1)S(1)}, bf16[4,352,128]{2,1,0:T(8,128)(2,1)S(1)}, u32[]{:S(2)}, u32[]{:S(2)}) collective-permute-start(bf16[4,352,128]{2,1,0:T(8,128)(2,1)S(1)} %get-tuple-element.46), channel_id=1, source_target_pairs={{0,1},{1,2},{2,3},{3,0},{4,5},{5,6},{6,7},{7,4},{8,9},{9,10},{10,1... | collective-permute-start | bytes 1081352 | tf_op jit(solution)/shard_map/ppermute | solution.py:124
  155.3 12.0 %collective-permute-start.2 = (bf16[4,352,128]{2,1,0:T(8,128)(2,1)S(1)}, bf16[4,352,128]{2,1,0:T(8,128)(2,1)S(1)}, u32[]{:S(2)}, u32[]{:S(2)}) collective-permute-start(bf16[4,352,128]{2,1,0:T(8,128)(2,1)S(1)} %get-tuple-element.47), channel_id=1, source_target_pairs={{0,3},{1,0},{2,1},{3,2},{4,7},{5,4},{6,5},{7,6},{8,11},{9,8},{10,9... | collective-permute-start | bytes 1081352 | tf_op jit(solution)/shard_map/ppermute | solution.py:124
  168.5 19.9 %collective-permute-start.3 = (bf16[8,352,128]{2,1,0:T(8,128)(2,1)}, bf16[8,352,128]{2,1,0:T(8,128)(2,1)}, u32[]{:S(2)}, u32[]{:S(2)}) collective-permute-start(bf16[8,352,128]{2,1,0:T(8,128)(2,1)} %pad_maximum_fusion.3), channel_id=1, source_target_pairs={{0,3},{1,0},{2,1},{3,2},{4,7},{5,4},{6,5},{7,6},{8,11},{9,8},{10,9... | collective-permute-start | bytes 2162696 | tf_op jit(solution)/shard_map/ppermute | solution.py:124
  173.8 19.3 %collective-permute-start.1 = (bf16[8,352,128]{2,1,0:T(8,128)(2,1)S(1)}, bf16[8,352,128]{2,1,0:T(8,128)(2,1)S(1)}, u32[]{:S(2)}, u32[]{:S(2)}) collective-permute-start(bf16[8,352,128]{2,1,0:T(8,128)(2,1)S(1)} %pad_maximum_fusion.2), channel_id=1, source_target_pairs={{0,1},{1,2},{2,3},{3,0},{4,5},{5,6},{6,7},{7,4},{8,9},{9,10},{10,1... | collective-permute-start | bytes 2162696 | tf_op jit(solution)/shard_map/ppermute | solution.py:124
  195.4 58.0 %all-to-all-start.3 = ((bf16[32,256,128]{2,1,0:T(8,128)(2,1)}), bf16[32,256,128]{2,1,0:T(8,128)(2,1)}, u32[]{:S(2)}, u32[]{:S(2)}) async-start(bf16[32,256,128]{2,1,0:T(8,128)(2,1)} %bitcast.26), calls=%async_computation.3 | async-start | bytes 4194304 | tf_op jit(solution)/shard_map/all_to_all | solution.py:119
  205.5 22.4 %collective-permute-start.10 = (bf16[352,128]{1,0:T(8,128)(2,1)S(1)}, bf16[352,128]{1,0:T(8,128)(2,1)S(1)}, u32[]{:S(2)}, u32[]{:S(2)}) collective-permute-start(bf16[352,128]{1,0:T(8,128)(2,1)S(1)} %get-tuple-element.55), channel_id=1, source_target_pairs={{0,28},{4,0},{8,4},{12,8},{16,12},{20,16},{24,20},{28,24},{1,29},{... | collective-permute-start | bytes 270344 | tf_op jit(solution)/shard_map/ppermute | solution.py:124
  214.5 16.4 %collective-permute-start.9 = (bf16[352,128]{1,0:T(8,128)(2,1)S(1)}, bf16[352,128]{1,0:T(8,128)(2,1)S(1)}, u32[]{:S(2)}, u32[]{:S(2)}) collective-permute-start(bf16[352,128]{1,0:T(8,128)(2,1)S(1)} %get-tuple-element.56), channel_id=1, source_target_pairs={{0,24},{4,28},{8,0},{12,4},{16,8},{20,12},{24,16},{28,20},{1,25},{... | collective-permute-start | bytes 270344 | tf_op jit(solution)/shard_map/ppermute | solution.py:124
  216.7 17.6 %collective-permute-start.8 = (bf16[352,128]{1,0:T(8,128)(2,1)S(1)}, bf16[352,128]{1,0:T(8,128)(2,1)S(1)}, u32[]{:S(2)}, u32[]{:S(2)}) collective-permute-start(bf16[352,128]{1,0:T(8,128)(2,1)S(1)} %get-tuple-element.57), channel_id=1, source_target_pairs={{0,20},{4,24},{8,28},{12,0},{16,4},{20,8},{24,12},{28,16},{1,21},{... | collective-permute-start | bytes 270344 | tf_op jit(solution)/shard_map/ppermute | solution.py:124
  218.6 15.7 %collective-permute-start.7 = (bf16[352,128]{1,0:T(8,128)(2,1)S(1)}, bf16[352,128]{1,0:T(8,128)(2,1)S(1)}, u32[]{:S(2)}, u32[]{:S(2)}) collective-permute-start(bf16[352,128]{1,0:T(8,128)(2,1)S(1)} %get-tuple-element.58), channel_id=1, source_target_pairs={{0,16},{4,20},{8,24},{12,28},{16,0},{20,4},{24,8},{28,12},{1,17},{... | collective-permute-start | bytes 270344 | tf_op jit(solution)/shard_map/ppermute | solution.py:124
  225.9 10.0 %collective-permute-start.6 = (bf16[352,128]{1,0:T(8,128)(2,1)S(1)}, bf16[352,128]{1,0:T(8,128)(2,1)S(1)}, u32[]{:S(2)}, u32[]{:S(2)}) collective-permute-start(bf16[352,128]{1,0:T(8,128)(2,1)S(1)} %get-tuple-element.59), channel_id=1, source_target_pairs={{0,12},{4,16},{8,20},{12,24},{16,28},{20,0},{24,4},{28,8},{1,13},{... | collective-permute-start | bytes 270344 | tf_op jit(solution)/shard_map/ppermute | solution.py:124
  227.9 13.8 %collective-permute-start.5 = (bf16[352,128]{1,0:T(8,128)(2,1)S(1)}, bf16[352,128]{1,0:T(8,128)(2,1)S(1)}, u32[]{:S(2)}, u32[]{:S(2)}) collective-permute-start(bf16[352,128]{1,0:T(8,128)(2,1)S(1)} %get-tuple-element.60), channel_id=1, source_target_pairs={{0,8},{4,12},{8,16},{12,20},{16,24},{20,28},{24,0},{28,4},{1,9},{5... | collective-permute-start | bytes 270344 | tf_op jit(solution)/shard_map/ppermute | solution.py:124
  231.0 11.7 %collective-permute-start.4 = (bf16[352,128]{1,0:T(8,128)(2,1)S(1)}, bf16[352,128]{1,0:T(8,128)(2,1)S(1)}, u32[]{:S(2)}, u32[]{:S(2)}) collective-permute-start(bf16[352,128]{1,0:T(8,128)(2,1)S(1)} %get-tuple-element.54), channel_id=1, source_target_pairs={{0,4},{4,8},{8,12},{12,16},{16,20},{20,24},{24,28},{28,0},{1,5},{5... | collective-permute-start | bytes 270344 | tf_op jit(solution)/shard_map/ppermute | solution.py:124
  249.3 13.0 %copy-start.3 = (bf16[16,128,128]{2,0,1:T(8,128)(2,1)S(1)}, bf16[16,128,128]{2,0,1:T(8,128)(2,1)}, u32[]{:S(2)}) copy-start(bf16[16,128,128]{2,0,1:T(8,128)(2,1)} %get-tuple-element.50) | copy-start | bytes 1572868
  249.4 13.0 %copy-start.4 = (bf16[16,128,128]{2,0,1:T(8,128)(2,1)S(1)}, bf16[16,128,128]{2,0,1:T(8,128)(2,1)}, u32[]{:S(2)}) copy-start(bf16[16,128,128]{2,0,1:T(8,128)(2,1)} %get-tuple-element.51) | copy-start | bytes 1572868
  257.4 12.3 %all-to-all-start.5 = ((f32[16,2,16]{2,1,0:T(2,128)}), f32[16,2,16]{2,1,0:T(2,128)S(1)}, u32[]{:S(2)}, u32[]{:S(2)}) async-start(f32[16,2,16]{2,1,0:T(2,128)} %bitcast.31), calls=%async_computation.5 | async-start | bytes 32768 | tf_op jit(solution)/shard_map/all_to_all | solution.py:119
  270.3 17.5 %all-to-all-start.6 = ((f32[32,2,16]{2,1,0:T(2,128)}), f32[32,2,16]{2,1,0:T(2,128)S(1)}, u32[]{:S(2)}, u32[]{:S(2)}) async-start(f32[32,2,16]{2,1,0:T(2,128)} %broadcast_in_dim.32), calls=%async_computation.6 | async-start | bytes 65536 | tf_op jit(solution)/shard_map/all_to_all | solution.py:119
  (1 other events, 3.0 us)
Sparse Core Ops, SparseCore 0:
  26.3 90.8 all-gather.2

commit v5 on v4

--- a/solution.py
+++ b/solution.py
@@ -73,14 +73,19 @@
                 term_ref[i, s, at, :] = term[:, at].astype(jnp.bfloat16)
 
 
-def back_kernel(full_ref, down_ref, slope_ref, hid_ref):
-    slices, segments = down_ref.shape[0], down_ref.shape[1]
+def back_kernel(where_ref, full_ref, slope_ref, *refs):
+    downs, hid_ref = refs[:-1], refs[-1]
+    n_y, segments = len(downs), downs[0].shape[1]
     group_rows, hidden = slope_ref.shape
     rows = group_rows // segments
+    y, core = where_ref[2], where_ref[3]
     for s in range(segments):
         back = jnp.zeros((rows, hidden), jnp.float32)
-        for i in range(slices):
-            back = back + dot(pair(full_ref, i, group_rows + s * rows, rows), down_ref[i, s], 1, 1)
+        for k in range(n_y):
+            for other in range(2):
+                i = 2 * lax.rem(y - k + n_y, n_y) + (1 - core if other else core)
+                grads = pair(full_ref, i, group_rows + s * rows, rows)
+                back = back + dot(grads, downs[k][other, s], 1, 1)
         hid_ref[pl.ds(s * rows, rows), :] = (
             back * slope_ref[pl.ds(s * rows, rows), :]
         ).astype(jnp.bfloat16)
@@ -122,6 +127,11 @@
 def shift(value, axis, by):
     size = lax.axis_size(axis)
     return lax.ppermute(value, axis, [(i, (i + by) % size) for i in range(size)])
+
+
+def from_here(value, dim, axis):
+    twice = jnp.concatenate([value, value], axis=dim)
+    return lax.dynamic_slice_in_dim(twice, lax.axis_index(axis), value.shape[dim], dim)
 
 
 def add(*values):
@@ -157,22 +167,29 @@
     n_z, n_x = lax.axis_size("z"), lax.axis_size("x")
     bf16 = jnp.bfloat16
     shape = jax.ShapeDtypeStruct
-    here = jnp.stack([lax.axis_index(a).astype(jnp.int32) for a in ("z", "x")])
+    here = jnp.stack([lax.axis_index(a).astype(jnp.int32) for a in ("z", "x", "y", "c")])
     routes_out = jnp.broadcast_to(routes, (n_dp,) + routes.shape[1:])
     all_routes = exchange(routes_out, DP)
     valid = (jnp.arange(group_rows, dtype=jnp.int32) < counts[0])[:, None]
     masked = jnp.where(valid, grad_out, jnp.zeros_like(grad_out))
     both = jnp.concatenate([tokens, masked], axis=0)
-    both, all_routes = lax.optimization_barrier((both, all_routes))
     full = lax.all_gather(both, TENSOR)
     flat_routes = all_routes.reshape(-1, experts)
-    def merge(weight):
+    def merge(rows, weight):
         return jnp.einsum(
-            "ke,eab->kab", flat_routes, weight.astype(jnp.float32), precision=high
+            "ke,eab->kab", rows, weight.astype(jnp.float32), precision=high
         ).astype(bf16)
 
-    merged_up = exchange(merge(up_weight), DP).reshape(n_dp, segments, width, hidden)
-    merged_down = exchange(merge(down_weight), DP).reshape(n_dp, segments, hidden, width)
+    merged_up = exchange(merge(flat_routes, up_weight), DP)
+    merged_up = merged_up.reshape(n_dp, segments, width, hidden)
+    turned_routes = from_here(from_here(all_routes.reshape(n_y, 2, segments, experts), 0, "y"), 1, "c")
+    local_down = merge(turned_routes.swapaxes(0, 1).reshape(-1, experts), down_weight)
+    local_down = local_down.reshape(2, n_y, segments, hidden, width)
+    crossed = shift(local_down[1], "c", 1)
+    downs = []
+    for k in range(n_y):
+        out = jnp.stack([local_down[0, k], crossed[k]])
+        downs.append(shift(out, "y", k) if k else out)
     down_halves = jnp.concatenate([down_weight[:, :, :lanes], down_weight[:, :, lanes:]], axis=1)
     merged_up, down_halves = lax.optimization_barrier((merged_up, down_halves))
 
@@ -186,9 +203,10 @@
         full,
         merged_up,
     )
+    down_terms, *downs = lax.optimization_barrier((down_terms, *downs))
     down_terms = exchange(down_terms.reshape(-1, 2 * hidden, lanes), DP)
     hid = local_kernel(
-        back_kernel, shape((group_rows, hidden), bf16), 0, full, merged_down, slope
+        back_kernel, shape((group_rows, hidden), bf16), 1, here, full, slope, *downs
     )
     parts = local_kernel(
         input_kernel, shape((n_x, n_z, group_rows, lanes), bf16), 1, here, hid, merged_up

time: 296 us -> 290 us (0.980)
  waiting for transfers between devices: 129 us -> 82 us
  starting transfers between devices: 89.5 us -> 109 us
  blocking collectives: 0 us -> 16.7 us
  other arithmetic: 10.1 us -> 14.7 us
    all_to_all x7 -> x5, waiting for transfers between devices: 74.8 us -> 12.5 us  [exchange(): return lax.all_to_all(value, axes, split_axis=0, concat_axis=0, tiled=True)]
    ppermute x11 -> x19, waiting for transfers between devices: 27.6 us -> 69.1 us  [shift(): lax.ppermute(value, axis, [(i, (i + by) % size) for i in range(size)])]
    ppermute x11 -> x19, starting transfers between devices: 42.7 us -> 75.3 us  [shift(): lax.ppermute(value, axis, [(i, (i + by) % size) for i in range(size)])]
    all_gather x1, waiting for transfers between devices: 26.7 us -> 0.38 us  [body(): full = lax.all_gather(both, TENSOR)]
    all_to_all x0 -> x1, blocking collectives: none -> 16.7 us  [exchange(): return lax.all_to_all(value, axes, split_axis=0, concat_axis=0, tiled=True)]
    all_to_all x7 -> x5, starting transfers between devices: 46.7 us -> 34.1 us  [exchange(): return lax.all_to_all(value, axes, split_axis=0, concat_axis=0, tiled=True)]
    another operation x1 -> x9, other arithmetic: 0.62 us -> 5.14 us  [the longest x8 4.48 us: body(): out = jnp.stack([local_down[0, k], crossed[k]])]
  transfers between devices with their start and end apart: 19 -> 25, of which waited for: 14 -> 16; matrix products, arithmetic and copies ran while one was open for 12% -> 12% of each run, Pallas kernels for 7% -> 7%
where the time goes in v5:
time: 290 us; the launch traced here: 289 us
  starting transfers between devices  109 us (38%)
  waiting for transfers between devices  82 us (28%)
  Pallas kernels  20.8 us (7%)
  blocking collectives  16.7 us (6%)
  matrix products  15.7 us (5%)
  between operations  15.2 us (5%)
  other arithmetic  14.7 us (5%)
  local copies, waits for them, and re-layouts  14.4 us (5%)
    ppermute x19, starting transfers between devices, shift(): lax.ppermute(value, axis, [(i, (i + by) % size) for i in range(size)])  75.3 us
    ppermute x19, waiting for transfers between devices, shift(): lax.ppermute(value, axis, [(i, (i + by) % size) for i in range(size)])  69.1 us
    all_to_all x5, starting transfers between devices, exchange(): return lax.all_to_all(value, axes, split_axis=0, concat_axis=0, tiled=True)  34.1 us
    pallas_call x4, Pallas kernels, local_kernel(): pl.pallas_call(kernel, out_shape=out_shapes, in_specs=smem + vmem(len(arg...  20.8 us
    all_to_all x1, blocking collectives, exchange(): return lax.all_to_all(value, axes, split_axis=0, concat_axis=0, tiled=True)  16.7 us
    all_to_all x5, waiting for transfers between devices, exchange(): return lax.all_to_all(value, axes, split_axis=0, concat_axis=0, tiled=True)  12.5 us
  transfers between devices with their start and end apart: 25, of which 16 were waited for; matrix products, arithmetic and copies ran while one was open for 12% of the time, Pallas kernels for 7%

profile of v5, /device:TPU:1, one launch (start us, length us, event | category | flops | bytes accessed | tf_op | source)
XLA Modules:
  0.0 288.8 jit_solution(14776245376833990686)
XLA Ops:
  11.3 16.7 %all_to_all.30 = f32[16,2,16]{2,1,0:T(2,128)S(1)} all-to-all(f32[16,2,16]{2,1,0:T(2,128)S(1)} %broadcast_in_dim.31), channel_id=1, replica_groups=mesh['y'=8,'c'=2,'z'=8,'x'=4] {'y','c'}, dimensions={0} | all-to-all | bytes 4096 | tf_op jit(solution)/shard_map/all_to_all | solution.py:124
  52.5 4.3 %collective-permute-start.3 = (bf16[2,2,128,256]{3,2,1,0:T(8,128)(2,1)}, bf16[2,2,128,256]{3,2,1,0:T(8,128)(2,1)}, u32[]{:S(2)}, u32[]{:S(2)}) collective-permute-start(bf16[2,2,128,256]{3,2,1,0:T(8,128)(2,1)} %pad_maximum_fusion.7), channel_id=1, source_target_pairs={{0,192},{64,256},{128,320},{192,384},{256,448},{320,0},{384,64},{4... | collective-permute-start | bytes 786440 | tf_op jit(solution)/shard_map/ppermute | solution.py:129
  62.3 4.4 %collective-permute-start.5 = (bf16[2,2,128,256]{3,2,1,0:T(8,128)(2,1)}, bf16[2,2,128,256]{3,2,1,0:T(8,128)(2,1)}, u32[]{:S(2)}, u32[]{:S(2)}) collective-permute-start(bf16[2,2,128,256]{3,2,1,0:T(8,128)(2,1)} %pad_maximum_fusion.9), channel_id=1, source_target_pairs={{0,320},{64,384},{128,448},{192,0},{256,64},{320,128},{384,192},{4... | collective-permute-start | bytes 786440 | tf_op jit(solution)/shard_map/ppermute | solution.py:129
  68.1 22.1 %collective-permute-done.1.refs_1_ = bf16[2,2,128,256]{3,2,1,0:T(8,128)(2,1)S(1)} collective-permute-done((bf16[2,2,128,256]{3,2,1,0:T(8,128)(2,1)S(1)}, bf16[2,2,128,256]{3,2,1,0:T(8,128)(2,1)S(1)}, u32[]{:S(2)}, u32[]{:S(2)}) %collective-permute-start.1) | collective-permute-done | bytes 262176 | tf_op jit(solution)/shard_map/ppermute | solution.py:129
  94.2 6.0 %collective-permute-done.2.refs_2_ = bf16[2,2,128,256]{3,2,1,0:T(8,128)(2,1)S(1)} collective-permute-done((bf16[2,2,128,256]{3,2,1,0:T(8,128)(2,1)S(1)}, bf16[2,2,128,256]{3,2,1,0:T(8,128)(2,1)S(1)}, u32[]{:S(2)}, u32[]{:S(2)}) %collective-permute-start.2) | collective-permute-done | bytes 262176 | tf_op jit(solution)/shard_map/ppermute | solution.py:129
  100.8 4.8 %collective-permute-start.7 = (bf16[2,2,128,256]{3,2,1,0:T(8,128)(2,1)}, bf16[2,2,128,256]{3,2,1,0:T(8,128)(2,1)}, u32[]{:S(2)}, u32[]{:S(2)}) collective-permute-start(bf16[2,2,128,256]{3,2,1,0:T(8,128)(2,1)} %pad_maximum_fusion.11), channel_id=1, source_target_pairs={{0,448},{64,0},{128,64},{192,128},{256,192},{320,256},{384,320},{4... | collective-permute-start | bytes 786440 | tf_op jit(solution)/shard_map/ppermute | solution.py:129
  109.1 6.5 %shard_map.93 = (f32[352,128]{1,0:T(8,128)}, bf16[16,2,256,128]{3,2,1,0:T(8,128)(2,1)}) custom-call(bf16[32,704,128]{2,1,0:T(8,128)(2,1)} %bitcast.96, bf16[16,2,256,128]{3,2,1,0:T(8,128)(2,1)} %bitcast.99), custom_call_target="tpu_custom_call" | custom-call | tf_op jit(solution)/shard_map/pallas_call | solution.py:39
  117.9 10.1 %collective-permute-done.4.refs_4_ = bf16[2,2,128,256]{3,2,1,0:T(8,128)(2,1)} collective-permute-done((bf16[2,2,128,256]{3,2,1,0:T(8,128)(2,1)}, bf16[2,2,128,256]{3,2,1,0:T(8,128)(2,1)}, u32[]{:S(2)}, u32[]{:S(2)}) %collective-permute-start.4) | collective-permute-done | bytes 262176 | tf_op jit(solution)/shard_map/ppermute | solution.py:129
  128.4 6.6 %all-to-all-start.3 = ((bf16[32,256,128]{2,1,0:T(8,128)(2,1)}), bf16[32,256,128]{2,1,0:T(8,128)(2,1)S(1)}, u32[]{:S(2)}, u32[]{:S(2)}) async-start(bf16[32,256,128]{2,1,0:T(8,128)(2,1)} %bitcast.102), calls=%async_computation.3 | async-start | bytes 4194304 | tf_op jit(solution)/shard_map/all_to_all | solution.py:124
  135.7 4.8 %shard_map.94.hid_ref = bf16[352,128]{1,0:T(8,128)(2,1)} custom-call(s32[4]{0:T(128)} %pad_add_fusion.where_ref, bf16[32,704,128]{2,1,0:T(8,128)(2,1)} %bitcast.97, f32[352,128]{1,0:T(8,128)} %get-tuple-element.22.slope_ref, bf16[2,2,128,256]{3,2,1,0:T(8,128)(2,1)} %pad_maximum_fusion.4.refs_0_, bf16[2,2,128,256]{3,2,1,0:T(8,128)(2,1)} %copy-done.7, ...), custom_call_target="tpu_custom_call" | custom-call | tf_op jit(solution)/shard_map/pallas_call | solution.py:39
  148.4 4.3 %collective-permute-start.10 = (bf16[4,352,128]{2,1,0:T(8,128)(2,1)S(1)}, bf16[4,352,128]{2,1,0:T(8,128)(2,1)S(1)}, u32[]{:S(2)}, u32[]{:S(2)}) collective-permute-start(bf16[4,352,128]{2,1,0:T(8,128)(2,1)S(1)} %get-tuple-element.65), channel_id=1, source_target_pairs={{0,3},{1,0},{2,1},{3,2},{4,7},{5,4},{6,5},{7,6},{8,11},{9,8},{10,9... | collective-permute-start | bytes 1081352 | tf_op jit(solution)/shard_map/ppermute | solution.py:129
  152.7 6.5 %collective-permute-done.8 = bf16[4,352,128]{2,1,0:T(8,128)(2,1)S(1)} collective-permute-done((bf16[4,352,128]{2,1,0:T(8,128)(2,1)S(1)}, bf16[4,352,128]{2,1,0:T(8,128)(2,1)S(1)}, u32[]{:S(2)}, u32[]{:S(2)}) %collective-permute-start.8) | collective-permute-done | bytes 360480 | tf_op jit(solution)/shard_map/ppermute | solution.py:129
  161.1 5.3 %collective-permute-start.11 = (bf16[8,352,128]{2,1,0:T(8,128)(2,1)}, bf16[8,352,128]{2,1,0:T(8,128)(2,1)}, u32[]{:S(2)}, u32[]{:S(2)}) collective-permute-start(bf16[8,352,128]{2,1,0:T(8,128)(2,1)} %pad_maximum_fusion.3), channel_id=1, source_target_pairs={{0,3},{1,0},{2,1},{3,2},{4,7},{5,4},{6,5},{7,6},{8,11},{9,8},{10,9... | collective-permute-start | bytes 2162696 | tf_op jit(solution)/shard_map/ppermute | solution.py:129
  168.5 5.3 %shard_map.95 = bf16[16,2,256,128]{3,2,1,0:T(8,128)(2,1)} custom-call(bf16[32,704,128]{2,1,0:T(8,128)(2,1)} %bitcast.98, bf16[352,128]{1,0:T(8,128)(2,1)} %shard_map.94.hid_ref), custom_call_target="tpu_custom_call" | custom-call | tf_op jit(solution)/shard_map/pallas_call | solution.py:39
  173.8 7.1 %collective-permute-done.11 = bf16[8,352,128]{2,1,0:T(8,128)(2,1)} collective-permute-done((bf16[8,352,128]{2,1,0:T(8,128)(2,1)}, bf16[8,352,128]{2,1,0:T(8,128)(2,1)}, u32[]{:S(2)}, u32[]{:S(2)}) %collective-permute-start.11) | collective-permute-done | bytes 720928 | tf_op jit(solution)/shard_map/ppermute | solution.py:129
  180.9 4.8 %collective-permute-done.9 = bf16[8,352,128]{2,1,0:T(8,128)(2,1)S(1)} collective-permute-done((bf16[8,352,128]{2,1,0:T(8,128)(2,1)S(1)}, bf16[8,352,128]{2,1,0:T(8,128)(2,1)S(1)}, u32[]{:S(2)}, u32[]{:S(2)}) %collective-permute-start.9) | collective-permute-done | bytes 720928 | tf_op jit(solution)/shard_map/ppermute | solution.py:129
  188.0 9.1 %all-to-all-start.2 = ((bf16[32,256,128]{2,1,0:T(8,128)(2,1)}), bf16[32,256,128]{2,1,0:T(8,128)(2,1)}, u32[]{:S(2)}, u32[]{:S(2)}) async-start(bf16[32,256,128]{2,1,0:T(8,128)(2,1)} %bitcast.39), calls=%async_computation.2 | async-start | bytes 4194304 | tf_op jit(solution)/shard_map/all_to_all | solution.py:124
  201.3 8.6 %collective-permute-start.18 = (bf16[352,128]{1,0:T(8,128)(2,1)S(1)}, bf16[352,128]{1,0:T(8,128)(2,1)S(1)}, u32[]{:S(2)}, u32[]{:S(2)}) collective-permute-start(bf16[352,128]{1,0:T(8,128)(2,1)S(1)} %get-tuple-element.89), channel_id=1, source_target_pairs={{0,28},{4,0},{8,4},{12,8},{16,12},{20,16},{24,20},{28,24},{1,29},{... | collective-permute-start | bytes 270344 | tf_op jit(solution)/shard_map/ppermute | solution.py:129
  216.4 6.1 %collective-permute-start.15 = (bf16[352,128]{1,0:T(8,128)(2,1)S(1)}, bf16[352,128]{1,0:T(8,128)(2,1)S(1)}, u32[]{:S(2)}, u32[]{:S(2)}) collective-permute-start(bf16[352,128]{1,0:T(8,128)(2,1)S(1)} %get-tuple-element.92), channel_id=1, source_target_pairs={{0,16},{4,20},{8,24},{12,28},{16,0},{20,4},{24,8},{28,12},{1,17},{... | collective-permute-start | bytes 270344 | tf_op jit(solution)/shard_map/ppermute | solution.py:129
  224.5 4.5 %collective-permute-start.13 = (bf16[352,128]{1,0:T(8,128)(2,1)S(1)}, bf16[352,128]{1,0:T(8,128)(2,1)S(1)}, u32[]{:S(2)}, u32[]{:S(2)}) collective-permute-start(bf16[352,128]{1,0:T(8,128)(2,1)S(1)} %get-tuple-element.94), channel_id=1, source_target_pairs={{0,8},{4,12},{8,16},{12,20},{16,24},{20,28},{24,0},{28,4},{1,9},{5... | collective-permute-start | bytes 270344 | tf_op jit(solution)/shard_map/ppermute | solution.py:129
  232.0 4.9 %collective-permute-done.13 = bf16[352,128]{1,0:T(8,128)(2,1)S(1)} collective-permute-done((bf16[352,128]{1,0:T(8,128)(2,1)S(1)}, bf16[352,128]{1,0:T(8,128)(2,1)S(1)}, u32[]{:S(2)}, u32[]{:S(2)}) %collective-permute-start.13) | collective-permute-done | bytes 90144 | tf_op jit(solution)/shard_map/ppermute | solution.py:129
  250.2 5.5 %all-to-all-start.4 = ((f32[16,2,16]{2,1,0:T(2,128)}), f32[16,2,16]{2,1,0:T(2,128)S(1)}, u32[]{:S(2)}, u32[]{:S(2)}) async-start(f32[16,2,16]{2,1,0:T(2,128)} %bitcast.47), calls=%async_computation.4 | async-start | bytes 32768 | tf_op jit(solution)/shard_map/all_to_all | solution.py:124
  257.2 5.9 %all-to-all-done.4 = f32[16,2,16]{2,1,0:T(2,128)S(1)} async-done(((f32[16,2,16]{2,1,0:T(2,128)}), f32[16,2,16]{2,1,0:T(2,128)S(1)}, u32[]{:S(2)}, u32[]{:S(2)}) %all-to-all-start.4) | async-done | bytes 2080 | tf_op jit(solution)/shard_map/all_to_all | solution.py:124
  263.7 9.0 %all-to-all-start.5 = ((f32[32,2,16]{2,1,0:T(2,128)}), f32[32,2,16]{2,1,0:T(2,128)S(1)}, u32[]{:S(2)}, u32[]{:S(2)}) async-start(f32[32,2,16]{2,1,0:T(2,128)} %broadcast_in_dim.32), calls=%async_computation.5 | async-start | bytes 65536 | tf_op jit(solution)/shard_map/all_to_all | solution.py:124
  (96 shorter events, 100.5 us)
Async XLA Ops:
  7.2 100.9 %all-gather.3.cloned.1.call-start = ((), (), s32[]{:S(2)}) async-start(), calls=%async_computation.6 | async-start | bytes 5947392 | tf_op jit(solution)/shard_map/all_gather | solution.py:176
  32.0 75.8 %all-to-all-start.1 = ((bf16[32,256,128]{2,1,0:T(8,128)(2,1)}), bf16[32,256,128]{2,1,0:T(8,128)(2,1)S(1)}, u32[]{:S(2)}, u32[]{:S(2)}) async-start(bf16[32,256,128]{2,1,0:T(8,128)(2,1)} %copy.100), calls=%async_computation.1 | async-start | bytes 4194304 | tf_op jit(solution)/shard_map/all_to_all | solution.py:124
  44.3 45.9 %collective-permute-start.1 = (bf16[2,2,128,256]{3,2,1,0:T(8,128)(2,1)S(1)}, bf16[2,2,128,256]{3,2,1,0:T(8,128)(2,1)S(1)}, u32[]{:S(2)}, u32[]{:S(2)}) collective-permute-start(bf16[2,2,128,256]{3,2,1,0:T(8,128)(2,1)S(1)} %pad_maximum_fusion.5), channel_id=1, source_target_pairs={{0,64},{64,128},{128,192},{192,256},{256,320},{320,384},{384,448},... | collective-permute-start | bytes 786440 | tf_op jit(solution)/shard_map/ppermute | solution.py:129
  47.7 52.4 %collective-permute-start.2 = (bf16[2,2,128,256]{3,2,1,0:T(8,128)(2,1)S(1)}, bf16[2,2,128,256]{3,2,1,0:T(8,128)(2,1)S(1)}, u32[]{:S(2)}, u32[]{:S(2)}) collective-permute-start(bf16[2,2,128,256]{3,2,1,0:T(8,128)(2,1)S(1)} %pad_maximum_fusion.6), channel_id=1, source_target_pairs={{0,128},{64,192},{128,256},{192,320},{256,384},{320,448},{384,0},{... | collective-permute-start | bytes 786440 | tf_op jit(solution)/shard_map/ppermute | solution.py:129
  52.5 65.4 %collective-permute-start.3 = (bf16[2,2,128,256]{3,2,1,0:T(8,128)(2,1)}, bf16[2,2,128,256]{3,2,1,0:T(8,128)(2,1)}, u32[]{:S(2)}, u32[]{:S(2)}) collective-permute-start(bf16[2,2,128,256]{3,2,1,0:T(8,128)(2,1)} %pad_maximum_fusion.7), channel_id=1, source_target_pairs={{0,192},{64,256},{128,320},{192,384},{256,448},{320,0},{384,64},{4... | collective-permute-start | bytes 786440 | tf_op jit(solution)/shard_map/ppermute | solution.py:129
  57.6 70.5 %collective-permute-start.4 = (bf16[2,2,128,256]{3,2,1,0:T(8,128)(2,1)}, bf16[2,2,128,256]{3,2,1,0:T(8,128)(2,1)}, u32[]{:S(2)}, u32[]{:S(2)}) collective-permute-start(bf16[2,2,128,256]{3,2,1,0:T(8,128)(2,1)} %pad_maximum_fusion.8), channel_id=1, source_target_pairs={{0,256},{64,320},{128,384},{192,448},{256,0},{320,64},{384,128},{4... | collective-permute-start | bytes 786440 | tf_op jit(solution)/shard_map/ppermute | solution.py:129
  62.3 65.8 %collective-permute-start.5 = (bf16[2,2,128,256]{3,2,1,0:T(8,128)(2,1)}, bf16[2,2,128,256]{3,2,1,0:T(8,128)(2,1)}, u32[]{:S(2)}, u32[]{:S(2)}) collective-permute-start(bf16[2,2,128,256]{3,2,1,0:T(8,128)(2,1)} %pad_maximum_fusion.9), channel_id=1, source_target_pairs={{0,320},{64,384},{128,448},{192,0},{256,64},{320,128},{384,192},{4... | collective-permute-start | bytes 786440 | tf_op jit(solution)/shard_map/ppermute | solution.py:129
  90.2 37.8 %collective-permute-start.6 = (bf16[2,2,128,256]{3,2,1,0:T(8,128)(2,1)}, bf16[2,2,128,256]{3,2,1,0:T(8,128)(2,1)}, u32[]{:S(2)}, u32[]{:S(2)}) collective-permute-start(bf16[2,2,128,256]{3,2,1,0:T(8,128)(2,1)} %pad_maximum_fusion.10), channel_id=1, source_target_pairs={{0,384},{64,448},{128,0},{192,64},{256,128},{320,192},{384,256},{4... | collective-permute-start | bytes 786440 | tf_op jit(solution)/shard_map/ppermute | solution.py:129
  100.8 27.6 %collective-permute-start.7 = (bf16[2,2,128,256]{3,2,1,0:T(8,128)(2,1)}, bf16[2,2,128,256]{3,2,1,0:T(8,128)(2,1)}, u32[]{:S(2)}, u32[]{:S(2)}) collective-permute-start(bf16[2,2,128,256]{3,2,1,0:T(8,128)(2,1)} %pad_maximum_fusion.11), channel_id=1, source_target_pairs={{0,448},{64,0},{128,64},{192,128},{256,192},{320,256},{384,320},{4... | collective-permute-start | bytes 786440 | tf_op jit(solution)/shard_map/ppermute | solution.py:129
  128.4 59.6 %all-to-all-start.3 = ((bf16[32,256,128]{2,1,0:T(8,128)(2,1)}), bf16[32,256,128]{2,1,0:T(8,128)(2,1)S(1)}, u32[]{:S(2)}, u32[]{:S(2)}) async-start(bf16[32,256,128]{2,1,0:T(8,128)(2,1)} %bitcast.102), calls=%async_computation.3 | async-start | bytes 4194304 | tf_op jit(solution)/shard_map/all_to_all | solution.py:124
  146.2 13.0 %collective-permute-start.8 = (bf16[4,352,128]{2,1,0:T(8,128)(2,1)S(1)}, bf16[4,352,128]{2,1,0:T(8,128)(2,1)S(1)}, u32[]{:S(2)}, u32[]{:S(2)}) collective-permute-start(bf16[4,352,128]{2,1,0:T(8,128)(2,1)S(1)} %get-tuple-element.64), channel_id=1, source_target_pairs={{0,1},{1,2},{2,3},{3,0},{4,5},{5,6},{6,7},{7,4},{8,9},{9,10},{10,1... | collective-permute-start | bytes 1081352 | tf_op jit(solution)/shard_map/ppermute | solution.py:129
  148.4 11.7 %collective-permute-start.10 = (bf16[4,352,128]{2,1,0:T(8,128)(2,1)S(1)}, bf16[4,352,128]{2,1,0:T(8,128)(2,1)S(1)}, u32[]{:S(2)}, u32[]{:S(2)}) collective-permute-start(bf16[4,352,128]{2,1,0:T(8,128)(2,1)S(1)} %get-tuple-element.65), channel_id=1, source_target_pairs={{0,3},{1,0},{2,1},{3,2},{4,7},{5,4},{6,5},{7,6},{8,11},{9,8},{10,9... | collective-permute-start | bytes 1081352 | tf_op jit(solution)/shard_map/ppermute | solution.py:129
  161.1 19.8 %collective-permute-start.11 = (bf16[8,352,128]{2,1,0:T(8,128)(2,1)}, bf16[8,352,128]{2,1,0:T(8,128)(2,1)}, u32[]{:S(2)}, u32[]{:S(2)}) collective-permute-start(bf16[8,352,128]{2,1,0:T(8,128)(2,1)} %pad_maximum_fusion.3), channel_id=1, source_target_pairs={{0,3},{1,0},{2,1},{3,2},{4,7},{5,4},{6,5},{7,6},{8,11},{9,8},{10,9... | collective-permute-start | bytes 2162696 | tf_op jit(solution)/shard_map/ppermute | solution.py:129
  166.5 19.2 %collective-permute-start.9 = (bf16[8,352,128]{2,1,0:T(8,128)(2,1)S(1)}, bf16[8,352,128]{2,1,0:T(8,128)(2,1)S(1)}, u32[]{:S(2)}, u32[]{:S(2)}) collective-permute-start(bf16[8,352,128]{2,1,0:T(8,128)(2,1)S(1)} %pad_maximum_fusion.2), channel_id=1, source_target_pairs={{0,1},{1,2},{2,3},{3,0},{4,5},{5,6},{6,7},{7,4},{8,9},{9,10},{10,1... | collective-permute-start | bytes 2162696 | tf_op jit(solution)/shard_map/ppermute | solution.py:129
  188.0 58.1 %all-to-all-start.2 = ((bf16[32,256,128]{2,1,0:T(8,128)(2,1)}), bf16[32,256,128]{2,1,0:T(8,128)(2,1)}, u32[]{:S(2)}, u32[]{:S(2)}) async-start(bf16[32,256,128]{2,1,0:T(8,128)(2,1)} %bitcast.39), calls=%async_computation.2 | async-start | bytes 4194304 | tf_op jit(solution)/shard_map/all_to_all | solution.py:124
  198.3 24.2 %collective-permute-start.12 = (bf16[352,128]{1,0:T(8,128)(2,1)S(1)}, bf16[352,128]{1,0:T(8,128)(2,1)S(1)}, u32[]{:S(2)}, u32[]{:S(2)}) collective-permute-start(bf16[352,128]{1,0:T(8,128)(2,1)S(1)} %get-tuple-element.88), channel_id=1, source_target_pairs={{0,4},{4,8},{8,12},{12,16},{16,20},{20,24},{24,28},{28,0},{1,5},{5... | collective-permute-start | bytes 270344 | tf_op jit(solution)/shard_map/ppermute | solution.py:129
  201.3 23.1 %collective-permute-start.18 = (bf16[352,128]{1,0:T(8,128)(2,1)S(1)}, bf16[352,128]{1,0:T(8,128)(2,1)S(1)}, u32[]{:S(2)}, u32[]{:S(2)}) collective-permute-start(bf16[352,128]{1,0:T(8,128)(2,1)S(1)} %get-tuple-element.89), channel_id=1, source_target_pairs={{0,28},{4,0},{8,4},{12,8},{16,12},{20,16},{24,20},{28,24},{1,29},{... | collective-permute-start | bytes 270344 | tf_op jit(solution)/shard_map/ppermute | solution.py:129
  209.9 19.1 %collective-permute-start.17 = (bf16[352,128]{1,0:T(8,128)(2,1)S(1)}, bf16[352,128]{1,0:T(8,128)(2,1)S(1)}, u32[]{:S(2)}, u32[]{:S(2)}) collective-permute-start(bf16[352,128]{1,0:T(8,128)(2,1)S(1)} %get-tuple-element.90), channel_id=1, source_target_pairs={{0,24},{4,28},{8,0},{12,4},{16,8},{20,12},{24,16},{28,20},{1,25},{... | collective-permute-start | bytes 270344 | tf_op jit(solution)/shard_map/ppermute | solution.py:129
  213.3 15.7 %collective-permute-start.16 = (bf16[352,128]{1,0:T(8,128)(2,1)S(1)}, bf16[352,128]{1,0:T(8,128)(2,1)S(1)}, u32[]{:S(2)}, u32[]{:S(2)}) collective-permute-start(bf16[352,128]{1,0:T(8,128)(2,1)S(1)} %get-tuple-element.91), channel_id=1, source_target_pairs={{0,20},{4,24},{8,28},{12,0},{16,4},{20,8},{24,12},{28,16},{1,21},{... | collective-permute-start | bytes 270344 | tf_op jit(solution)/shard_map/ppermute | solution.py:129
  216.4 12.6 %collective-permute-start.15 = (bf16[352,128]{1,0:T(8,128)(2,1)S(1)}, bf16[352,128]{1,0:T(8,128)(2,1)S(1)}, u32[]{:S(2)}, u32[]{:S(2)}) collective-permute-start(bf16[352,128]{1,0:T(8,128)(2,1)S(1)} %get-tuple-element.92), channel_id=1, source_target_pairs={{0,16},{4,20},{8,24},{12,28},{16,0},{20,4},{24,8},{28,12},{1,17},{... | collective-permute-start | bytes 270344 | tf_op jit(solution)/shard_map/ppermute | solution.py:129
  222.5 9.4 %collective-permute-start.14 = (bf16[352,128]{1,0:T(8,128)(2,1)S(1)}, bf16[352,128]{1,0:T(8,128)(2,1)S(1)}, u32[]{:S(2)}, u32[]{:S(2)}) collective-permute-start(bf16[352,128]{1,0:T(8,128)(2,1)S(1)} %get-tuple-element.93), channel_id=1, source_target_pairs={{0,12},{4,16},{8,20},{12,24},{16,28},{20,0},{24,4},{28,8},{1,13},{... | collective-permute-start | bytes 270344 | tf_op jit(solution)/shard_map/ppermute | solution.py:129
  224.5 12.4 %collective-permute-start.13 = (bf16[352,128]{1,0:T(8,128)(2,1)S(1)}, bf16[352,128]{1,0:T(8,128)(2,1)S(1)}, u32[]{:S(2)}, u32[]{:S(2)}) collective-permute-start(bf16[352,128]{1,0:T(8,128)(2,1)S(1)} %get-tuple-element.94), channel_id=1, source_target_pairs={{0,8},{4,12},{8,16},{12,20},{16,24},{20,28},{24,0},{28,4},{1,9},{5... | collective-permute-start | bytes 270344 | tf_op jit(solution)/shard_map/ppermute | solution.py:129
  250.2 12.9 %all-to-all-start.4 = ((f32[16,2,16]{2,1,0:T(2,128)}), f32[16,2,16]{2,1,0:T(2,128)S(1)}, u32[]{:S(2)}, u32[]{:S(2)}) async-start(f32[16,2,16]{2,1,0:T(2,128)} %bitcast.47), calls=%async_computation.4 | async-start | bytes 32768 | tf_op jit(solution)/shard_map/all_to_all | solution.py:124
  263.7 17.6 %all-to-all-start.5 = ((f32[32,2,16]{2,1,0:T(2,128)}), f32[32,2,16]{2,1,0:T(2,128)S(1)}, u32[]{:S(2)}, u32[]{:S(2)}) async-start(f32[32,2,16]{2,1,0:T(2,128)} %broadcast_in_dim.32), calls=%async_computation.5 | async-start | bytes 65536 | tf_op jit(solution)/shard_map/all_to_all | solution.py:124
  (10 other events, 148.4 us)
Sparse Core Ops, SparseCore 0:
  11.2 96.9 all-gather.2

commit v6 on v5

--- a/solution.py
+++ b/solution.py
@@ -73,7 +73,7 @@
                 term_ref[i, s, at, :] = term[:, at].astype(jnp.bfloat16)
 
 
-def back_kernel(where_ref, full_ref, slope_ref, *refs):
+def back_kernel(order, where_ref, full_ref, slope_ref, *refs):
     downs, hid_ref = refs[:-1], refs[-1]
     n_y, segments = len(downs), downs[0].shape[1]
     group_rows, hidden = slope_ref.shape
@@ -81,11 +81,11 @@
     y, core = where_ref[2], where_ref[3]
     for s in range(segments):
         back = jnp.zeros((rows, hidden), jnp.float32)
-        for k in range(n_y):
+        for k, down_ref in zip(order, downs):
             for other in range(2):
                 i = 2 * lax.rem(y - k + n_y, n_y) + (1 - core if other else core)
                 grads = pair(full_ref, i, group_rows + s * rows, rows)
-                back = back + dot(grads, downs[k][other, s], 1, 1)
+                back = back + dot(grads, down_ref[other, s], 1, 1)
         hid_ref[pl.ds(s * rows, rows), :] = (
             back * slope_ref[pl.ds(s * rows, rows), :]
         ).astype(jnp.bfloat16)
@@ -148,13 +148,13 @@
     return right, left
 
 
-def second_hop(own, right, left):
-    return add(own, shift(right, "x", 1), shift(left, "x", -1)).astype(jnp.bfloat16)
-
-
-def finish_sum(near):
-    hops = [shift(near[k], "z", k) for k in range(1, near.shape[0])]
-    return add(near[0], *hops).astype(jnp.bfloat16)
+def finish_sum(own, from_left, from_right):
+    bf16 = jnp.bfloat16
+    near = add(own, from_left, from_right).astype(bf16)
+    near = near.reshape((near.shape[0] // 2, 2) + near.shape[1:])
+    hops = [shift(near[k], "z", 2 * k) for k in range(1, near.shape[0])]
+    near = add(near[0], *hops).astype(bf16)
+    return add(near[0], shift(near[1], "z", 1)).astype(bf16)
 
 
 def body(tokens, grad_out, routes, counts, up_weight, down_weight):
@@ -186,10 +186,9 @@
     local_down = merge(turned_routes.swapaxes(0, 1).reshape(-1, experts), down_weight)
     local_down = local_down.reshape(2, n_y, segments, hidden, width)
     crossed = shift(local_down[1], "c", 1)
-    downs = []
-    for k in range(n_y):
-        out = jnp.stack([local_down[0, k], crossed[k]])
-        downs.append(shift(out, "y", k) if k else out)
+    order = sorted(range(n_y), key=lambda k: abs(2 * k - n_y))
+    downs = [jnp.stack([local_down[0, k], crossed[k]]) for k in order]
+    downs = [shift(out, "y", k) if k else out for k, out in zip(order, downs)]
     down_halves = jnp.concatenate([down_weight[:, :, :lanes], down_weight[:, :, lanes:]], axis=1)
     merged_up, down_halves = lax.optimization_barrier((merged_up, down_halves))
 
@@ -206,7 +205,13 @@
     down_terms, *downs = lax.optimization_barrier((down_terms, *downs))
     down_terms = exchange(down_terms.reshape(-1, 2 * hidden, lanes), DP)
     hid = local_kernel(
-        back_kernel, shape((group_rows, hidden), bf16), 1, here, full, slope, *downs
+        functools.partial(back_kernel, order),
+        shape((group_rows, hidden), bf16),
+        1,
+        here,
+        full,
+        slope,
+        *downs,
     )
     parts = local_kernel(
         input_kernel, shape((n_x, n_z, group_rows, lanes), bf16), 1, here, hid, merged_up
@@ -215,9 +220,9 @@
         up_kernel, shape((n_dp, segments, width, hidden), bf16), 0, full, hid
     )
     right, left = start_sum(parts)
-    near = second_hop(parts[0], right, left)
-    up_terms, near = lax.optimization_barrier((up_terms, near))
-    summed = finish_sum(near)
+    from_left, from_right = shift(right, "x", 1), shift(left, "x", -1)
+    up_terms, from_left, from_right = lax.optimization_barrier((up_terms, from_left, from_right))
+    summed = finish_sum(parts[0], from_left, from_right)
     down_grad = jnp.einsum(
         "ke,kab->eab", flat_routes, down_terms.astype(jnp.float32), precision=high
     ).astype(bf16)

time: 290 us -> 290 us (level)
    ppermute x19 -> x16, waiting for transfers between devices: 69.1 us -> 67.1 us  [shift(): lax.ppermute(value, axis, [(i, (i + by) % size) for i in range(size)])]
    ppermute x19 -> x16, starting transfers between devices: 75.3 us -> 74.4 us  [shift(): lax.ppermute(value, axis, [(i, (i + by) % size) for i in range(size)])]
  transfers between devices with their start and end apart: 25 -> 22, of which waited for: 16 -> 14; matrix products, arithmetic and copies ran while one was open for 12% -> 11% of each run, Pallas kernels for 7% -> 7%
where the time goes in v6:
time: 290 us; the launch traced here: 289 us
  starting transfers between devices  111 us (38%)
  waiting for transfers between devices  81.3 us (28%)
  Pallas kernels  20.8 us (7%)
  blocking collectives  16.7 us (6%)
  matrix products  15.7 us (5%)
  between operations  15.1 us (5%)
  local copies, waits for them, and re-layouts  14.3 us (5%)
  other arithmetic  13.6 us (5%)
    ppermute x16, starting transfers between devices, shift(): lax.ppermute(value, axis, [(i, (i + by) % size) for i in range(size)])  74.4 us
    ppermute x16, waiting for transfers between devices, shift(): lax.ppermute(value, axis, [(i, (i + by) % size) for i in range(size)])  67.1 us
    all_to_all x5, starting transfers between devices, exchange(): return lax.all_to_all(value, axes, split_axis=0, concat_axis=0, tiled=True)  36.9 us
    pallas_call x4, Pallas kernels, local_kernel(): pl.pallas_call(kernel, out_shape=out_shapes, in_specs=smem + vmem(len(arg...  20.8 us
    all_to_all x1, blocking collectives, exchange(): return lax.all_to_all(value, axes, split_axis=0, concat_axis=0, tiled=True)  16.7 us
    all_to_all x5, waiting for transfers between devices, exchange(): return lax.all_to_all(value, axes, split_axis=0, concat_axis=0, tiled=True)  14.1 us
  transfers between devices with their start and end apart: 22, of which 14 were waited for; matrix products, arithmetic and copies ran while one was open for 11% of the time, Pallas kernels for 7%

profile of v6, /device:TPU:1, one launch (start us, length us, event | category | flops | bytes accessed | tf_op | source)
XLA Modules:
  0.0 288.8 jit_solution(13538602545722399426)
XLA Ops:
  11.2 16.7 %all_to_all.30 = f32[16,2,16]{2,1,0:T(2,128)S(1)} all-to-all(f32[16,2,16]{2,1,0:T(2,128)S(1)} %broadcast_in_dim.31), channel_id=1, replica_groups=mesh['y'=8,'c'=2,'z'=8,'x'=4] {'y','c'}, dimensions={0} | all-to-all | bytes 4096 | tf_op jit(solution)/shard_map/all_to_all | solution.py:124
  44.3 7.4 %collective-permute-start.1 = (bf16[2,2,128,256]{3,2,1,0:T(8,128)(2,1)S(1)}, bf16[2,2,128,256]{3,2,1,0:T(8,128)(2,1)S(1)}, u32[]{:S(2)}, u32[]{:S(2)}) collective-permute-start(bf16[2,2,128,256]{3,2,1,0:T(8,128)(2,1)S(1)} %pad_maximum_fusion.4), channel_id=1, source_target_pairs={{0,256},{64,320},{128,384},{192,448},{256,0},{320,64},{384,128},{4... | collective-permute-start | bytes 786440 | tf_op jit(solution)/shard_map/ppermute | solution.py:129
  54.7 6.0 %collective-permute-start.3 = (bf16[2,2,128,256]{3,2,1,0:T(8,128)(2,1)}, bf16[2,2,128,256]{3,2,1,0:T(8,128)(2,1)}, u32[]{:S(2)}, u32[]{:S(2)}) collective-permute-start(bf16[2,2,128,256]{3,2,1,0:T(8,128)(2,1)} %pad_maximum_fusion.6), channel_id=1, source_target_pairs={{0,320},{64,384},{128,448},{192,0},{256,64},{320,128},{384,192},{4... | collective-permute-start | bytes 786440 | tf_op jit(solution)/shard_map/ppermute | solution.py:129
  64.5 5.2 %collective-permute-start.5 = (bf16[2,2,128,256]{3,2,1,0:T(8,128)(2,1)}, bf16[2,2,128,256]{3,2,1,0:T(8,128)(2,1)}, u32[]{:S(2)}, u32[]{:S(2)}) collective-permute-start(bf16[2,2,128,256]{3,2,1,0:T(8,128)(2,1)} %pad_maximum_fusion.8), channel_id=1, source_target_pairs={{0,384},{64,448},{128,0},{192,64},{256,128},{320,192},{384,256},{4... | collective-permute-start | bytes 786440 | tf_op jit(solution)/shard_map/ppermute | solution.py:129
  71.1 23.6 %collective-permute-done.1.refs_0_ = bf16[2,2,128,256]{3,2,1,0:T(8,128)(2,1)S(1)} collective-permute-done((bf16[2,2,128,256]{3,2,1,0:T(8,128)(2,1)S(1)}, bf16[2,2,128,256]{3,2,1,0:T(8,128)(2,1)S(1)}, u32[]{:S(2)}, u32[]{:S(2)}) %collective-permute-start.1) | collective-permute-done | bytes 262176 | tf_op jit(solution)/shard_map/ppermute | solution.py:129
  94.6 6.0 %collective-permute-start.6 = (bf16[2,2,128,256]{3,2,1,0:T(8,128)(2,1)}, bf16[2,2,128,256]{3,2,1,0:T(8,128)(2,1)}, u32[]{:S(2)}, u32[]{:S(2)}) collective-permute-start(bf16[2,2,128,256]{3,2,1,0:T(8,128)(2,1)} %pad_maximum_fusion.9), channel_id=1, source_target_pairs={{0,64},{64,128},{128,192},{192,256},{256,320},{320,384},{384,448},... | collective-permute-start | bytes 786440 | tf_op jit(solution)/shard_map/ppermute | solution.py:129
  100.7 10.9 %collective-permute-done.2.refs_1_ = bf16[2,2,128,256]{3,2,1,0:T(8,128)(2,1)S(1)} collective-permute-done((bf16[2,2,128,256]{3,2,1,0:T(8,128)(2,1)S(1)}, bf16[2,2,128,256]{3,2,1,0:T(8,128)(2,1)S(1)}, u32[]{:S(2)}, u32[]{:S(2)}) %collective-permute-start.2) | collective-permute-done | bytes 262176 | tf_op jit(solution)/shard_map/ppermute | solution.py:129
  112.3 5.7 %collective-permute-start.7 = (bf16[2,2,128,256]{3,2,1,0:T(8,128)(2,1)}, bf16[2,2,128,256]{3,2,1,0:T(8,128)(2,1)}, u32[]{:S(2)}, u32[]{:S(2)}) collective-permute-start(bf16[2,2,128,256]{3,2,1,0:T(8,128)(2,1)} %pad_maximum_fusion.10), channel_id=1, source_target_pairs={{0,448},{64,0},{128,64},{192,128},{256,192},{320,256},{384,320},{4... | collective-permute-start | bytes 786440 | tf_op jit(solution)/shard_map/ppermute | solution.py:129
  121.4 6.5 %shard_map.93 = (f32[352,128]{1,0:T(8,128)}, bf16[16,2,256,128]{3,2,1,0:T(8,128)(2,1)}) custom-call(bf16[32,704,128]{2,1,0:T(8,128)(2,1)} %bitcast.86, bf16[16,2,256,128]{3,2,1,0:T(8,128)(2,1)} %bitcast.89), custom_call_target="tpu_custom_call" | custom-call | tf_op jit(solution)/shard_map/pallas_call | solution.py:39
  129.6 5.4 %all-to-all-start.3 = ((bf16[32,256,128]{2,1,0:T(8,128)(2,1)}), bf16[32,256,128]{2,1,0:T(8,128)(2,1)S(1)}, u32[]{:S(2)}, u32[]{:S(2)}) async-start(bf16[32,256,128]{2,1,0:T(8,128)(2,1)} %bitcast.93), calls=%async_computation.3 | async-start | bytes 4194304 | tf_op jit(solution)/shard_map/all_to_all | solution.py:124
  135.6 4.8 %shard_map.94.hid_ref = bf16[352,128]{1,0:T(8,128)(2,1)} custom-call(s32[4]{0:T(128)} %pad_add_fusion.where_ref, bf16[32,704,128]{2,1,0:T(8,128)(2,1)} %bitcast.87, f32[352,128]{1,0:T(8,128)} %get-tuple-element.23.slope_ref, bf16[2,2,128,256]{3,2,1,0:T(8,128)(2,1)} %copy-done.7, bf16[2,2,128,256]{3,2,1,0:T(8,128)(2,1)} %copy-done.8, ...), custom_call_target="tpu_custom_call" | custom-call | tf_op jit(solution)/shard_map/pallas_call | solution.py:39
  151.4 6.5 %collective-permute-done.10 = bf16[4,352,128]{2,1,0:T(8,128)(2,1)S(1)} collective-permute-done((bf16[4,352,128]{2,1,0:T(8,128)(2,1)S(1)}, bf16[4,352,128]{2,1,0:T(8,128)(2,1)S(1)}, u32[]{:S(2)}, u32[]{:S(2)}) %collective-permute-start.10) | collective-permute-done | bytes 360480 | tf_op jit(solution)/shard_map/ppermute | solution.py:129
  165.6 4.6 %collective-permute-start.11 = (bf16[8,352,128]{2,1,0:T(8,128)(2,1)S(1)}, bf16[8,352,128]{2,1,0:T(8,128)(2,1)}, u32[]{:S(2)}, u32[]{:S(2)}) collective-permute-start(bf16[8,352,128]{2,1,0:T(8,128)(2,1)S(1)} %pad_maximum_fusion.3), channel_id=1, source_target_pairs={{0,3},{1,0},{2,1},{3,2},{4,7},{5,4},{6,5},{7,6},{8,11},{9,8},{10,9... | collective-permute-start | bytes 2162696 | tf_op jit(solution)/shard_map/ppermute | solution.py:129
  170.1 5.4 %shard_map.96 = bf16[16,2,256,128]{3,2,1,0:T(8,128)(2,1)} custom-call(bf16[32,704,128]{2,1,0:T(8,128)(2,1)} %bitcast.88, bf16[352,128]{1,0:T(8,128)(2,1)} %shard_map.94.hid_ref), custom_call_target="tpu_custom_call" | custom-call | tf_op jit(solution)/shard_map/pallas_call | solution.py:39
  175.5 7.6 %collective-permute-done.9 = bf16[8,352,128]{2,1,0:T(8,128)(2,1)S(1)} collective-permute-done((bf16[8,352,128]{2,1,0:T(8,128)(2,1)S(1)}, bf16[8,352,128]{2,1,0:T(8,128)(2,1)S(1)}, u32[]{:S(2)}, u32[]{:S(2)}) %collective-permute-start.9) | collective-permute-done | bytes 720928 | tf_op jit(solution)/shard_map/ppermute | solution.py:129
  184.1 8.9 %all-to-all-start.2 = ((bf16[32,256,128]{2,1,0:T(8,128)(2,1)}), bf16[32,256,128]{2,1,0:T(8,128)(2,1)}, u32[]{:S(2)}, u32[]{:S(2)}) async-start(bf16[32,256,128]{2,1,0:T(8,128)(2,1)} %bitcast.91), calls=%async_computation.2 | async-start | bytes 4194304 | tf_op jit(solution)/shard_map/all_to_all | solution.py:124
  194.9 5.8 %collective-permute-start.12 = (bf16[2,352,128]{2,1,0:T(8,128)(2,1)S(1)}, bf16[2,352,128]{2,1,0:T(8,128)(2,1)S(1)}, u32[]{:S(2)}, u32[]{:S(2)}) collective-permute-start(bf16[2,352,128]{2,1,0:T(8,128)(2,1)S(1)} %get-tuple-element.90), channel_id=1, source_target_pairs={{0,8},{4,12},{8,16},{12,20},{16,24},{20,28},{24,0},{28,4},{1,9},{5... | collective-permute-start | bytes 540680 | tf_op jit(solution)/shard_map/ppermute | solution.py:129
  200.7 6.8 %collective-permute-start.14 = (bf16[2,352,128]{2,1,0:T(8,128)(2,1)S(1)}, bf16[2,352,128]{2,1,0:T(8,128)(2,1)S(1)}, u32[]{:S(2)}, u32[]{:S(2)}) collective-permute-start(bf16[2,352,128]{2,1,0:T(8,128)(2,1)S(1)} %get-tuple-element.91), channel_id=1, source_target_pairs={{0,24},{4,28},{8,0},{12,4},{16,8},{20,12},{24,16},{28,20},{1,25},{... | collective-permute-start | bytes 540680 | tf_op jit(solution)/shard_map/ppermute | solution.py:129
  207.5 5.4 %collective-permute-start.13 = (bf16[2,352,128]{2,1,0:T(8,128)(2,1)S(1)}, bf16[2,352,128]{2,1,0:T(8,128)(2,1)S(1)}, u32[]{:S(2)}, u32[]{:S(2)}) collective-permute-start(bf16[2,352,128]{2,1,0:T(8,128)(2,1)S(1)} %get-tuple-element.92), channel_id=1, source_target_pairs={{0,16},{4,20},{8,24},{12,28},{16,0},{20,4},{24,8},{28,12},{1,17},{... | collective-permute-start | bytes 540680 | tf_op jit(solution)/shard_map/ppermute | solution.py:129
  214.9 8.0 %collective-permute-done.13 = bf16[2,352,128]{2,1,0:T(8,128)(2,1)S(1)} collective-permute-done((bf16[2,352,128]{2,1,0:T(8,128)(2,1)S(1)}, bf16[2,352,128]{2,1,0:T(8,128)(2,1)S(1)}, u32[]{:S(2)}, u32[]{:S(2)}) %collective-permute-start.13) | collective-permute-done | bytes 180256 | tf_op jit(solution)/shard_map/ppermute | solution.py:129
  223.0 7.5 %collective-permute-start.15 = (bf16[352,128]{1,0:T(8,128)(2,1)S(1)}, bf16[352,128]{1,0:T(8,128)(2,1)S(1)}, u32[]{:S(2)}, u32[]{:S(2)}) collective-permute-start(bf16[352,128]{1,0:T(8,128)(2,1)S(1)} %slice_bitcast_fusion.15), channel_id=1, source_target_pairs={{0,4},{4,8},{8,12},{12,16},{16,20},{20,24},{24,28},{28,0},{1,5},{5... | collective-permute-start | bytes 270344 | tf_op jit(solution)/shard_map/ppermute | solution.py:129
  246.1 5.0 %all-to-all-start.4 = ((f32[16,2,16]{2,1,0:T(2,128)}), f32[16,2,16]{2,1,0:T(2,128)S(1)}, u32[]{:S(2)}, u32[]{:S(2)}) async-start(f32[16,2,16]{2,1,0:T(2,128)} %bitcast.41), calls=%async_computation.4 | async-start | bytes 32768 | tf_op jit(solution)/shard_map/all_to_all | solution.py:124
  252.5 5.8 %all-to-all-done.4 = f32[16,2,16]{2,1,0:T(2,128)S(1)} async-done(((f32[16,2,16]{2,1,0:T(2,128)}), f32[16,2,16]{2,1,0:T(2,128)S(1)}, u32[]{:S(2)}, u32[]{:S(2)}) %all-to-all-start.4) | async-done | bytes 2080 | tf_op jit(solution)/shard_map/all_to_all | solution.py:124
  259.0 13.7 %all-to-all-start.5 = ((f32[32,2,16]{2,1,0:T(2,128)}), f32[32,2,16]{2,1,0:T(2,128)S(1)}, u32[]{:S(2)}, u32[]{:S(2)}) async-start(f32[32,2,16]{2,1,0:T(2,128)} %broadcast_in_dim.32), calls=%async_computation.5 | async-start | bytes 65536 | tf_op jit(solution)/shard_map/all_to_all | solution.py:124
  (92 shorter events, 84.5 us)
Async XLA Ops:
  7.2 112.9 %all-gather.3.cloned.1.call-start = ((), (), s32[]{:S(2)}) async-start(), calls=%async_computation.6 | async-start | bytes 5947392 | tf_op jit(solution)/shard_map/all_gather | solution.py:176
  32.0 88.1 %all-to-all-start.1 = ((bf16[32,256,128]{2,1,0:T(8,128)(2,1)}), bf16[32,256,128]{2,1,0:T(8,128)(2,1)S(1)}, u32[]{:S(2)}, u32[]{:S(2)}) async-start(bf16[32,256,128]{2,1,0:T(8,128)(2,1)} %copy.100), calls=%async_computation.1 | async-start | bytes 4194304 | tf_op jit(solution)/shard_map/all_to_all | solution.py:124
  39.6 4.6 %collective-permute-start = (bf16[8,2,128,256]{3,2,1,0:T(8,128)(2,1)S(1)}, bf16[8,2,128,256]{3,2,1,0:T(8,128)(2,1)S(1)}, u32[]{:S(2)}, u32[]{:S(2)}) collective-permute-start(bf16[8,2,128,256]{3,2,1,0:T(8,128)(2,1)S(1)} %bitcast.94), channel_id=1, source_target_pairs={{0,32},{32,0},{1,33},{33,1},{2,34},{34,2},{3,35},{35,3},{4,36},{36... | collective-permute-start | bytes 3145736 | tf_op jit(solution)/shard_map/ppermute | solution.py:129
  44.2 73.8 %copy-start.2 = (bf16[16,128,256]{2,1,0:T(8,128)(2,1)S(1)}, bf16[16,128,256]{2,1,0:T(8,128)(2,1)}, u32[]{:S(2)}) copy-start(bf16[16,128,256]{2,1,0:T(8,128)(2,1)} %param.11) | copy-start | bytes 3145732
  44.3 50.4 %collective-permute-start.1 = (bf16[2,2,128,256]{3,2,1,0:T(8,128)(2,1)S(1)}, bf16[2,2,128,256]{3,2,1,0:T(8,128)(2,1)S(1)}, u32[]{:S(2)}, u32[]{:S(2)}) collective-permute-start(bf16[2,2,128,256]{3,2,1,0:T(8,128)(2,1)S(1)} %pad_maximum_fusion.4), channel_id=1, source_target_pairs={{0,256},{64,320},{128,384},{192,448},{256,0},{320,64},{384,128},{4... | collective-permute-start | bytes 786440 | tf_op jit(solution)/shard_map/ppermute | solution.py:129
  51.7 59.8 %collective-permute-start.2 = (bf16[2,2,128,256]{3,2,1,0:T(8,128)(2,1)S(1)}, bf16[2,2,128,256]{3,2,1,0:T(8,128)(2,1)S(1)}, u32[]{:S(2)}, u32[]{:S(2)}) collective-permute-start(bf16[2,2,128,256]{3,2,1,0:T(8,128)(2,1)S(1)} %pad_maximum_fusion.5), channel_id=1, source_target_pairs={{0,192},{64,256},{128,320},{192,384},{256,448},{320,0},{384,64},{4... | collective-permute-start | bytes 786440 | tf_op jit(solution)/shard_map/ppermute | solution.py:129
  54.7 73.3 %collective-permute-start.3 = (bf16[2,2,128,256]{3,2,1,0:T(8,128)(2,1)}, bf16[2,2,128,256]{3,2,1,0:T(8,128)(2,1)}, u32[]{:S(2)}, u32[]{:S(2)}) collective-permute-start(bf16[2,2,128,256]{3,2,1,0:T(8,128)(2,1)} %pad_maximum_fusion.6), channel_id=1, source_target_pairs={{0,320},{64,384},{128,448},{192,0},{256,64},{320,128},{384,192},{4... | collective-permute-start | bytes 786440 | tf_op jit(solution)/shard_map/ppermute | solution.py:129
  61.5 66.5 %collective-permute-start.4 = (bf16[2,2,128,256]{3,2,1,0:T(8,128)(2,1)}, bf16[2,2,128,256]{3,2,1,0:T(8,128)(2,1)}, u32[]{:S(2)}, u32[]{:S(2)}) collective-permute-start(bf16[2,2,128,256]{3,2,1,0:T(8,128)(2,1)} %pad_maximum_fusion.7), channel_id=1, source_target_pairs={{0,128},{64,192},{128,256},{192,320},{256,384},{320,448},{384,0},{... | collective-permute-start | bytes 786440 | tf_op jit(solution)/shard_map/ppermute | solution.py:129
  64.5 63.5 %collective-permute-start.5 = (bf16[2,2,128,256]{3,2,1,0:T(8,128)(2,1)}, bf16[2,2,128,256]{3,2,1,0:T(8,128)(2,1)}, u32[]{:S(2)}, u32[]{:S(2)}) collective-permute-start(bf16[2,2,128,256]{3,2,1,0:T(8,128)(2,1)} %pad_maximum_fusion.8), channel_id=1, source_target_pairs={{0,384},{64,448},{128,0},{192,64},{256,128},{320,192},{384,256},{4... | collective-permute-start | bytes 786440 | tf_op jit(solution)/shard_map/ppermute | solution.py:129
  94.6 24.7 %copy-start.7 = (bf16[2,2,128,256]{3,2,1,0:T(8,128)(2,1)}, bf16[2,2,128,256]{3,2,1,0:T(8,128)(2,1)S(1)}, u32[]{:S(2)}) copy-start(bf16[2,2,128,256]{3,2,1,0:T(8,128)(2,1)S(1)} %collective-permute-done.1.refs_0_) | copy-start | bytes 786436
  94.6 34.9 %collective-permute-start.6 = (bf16[2,2,128,256]{3,2,1,0:T(8,128)(2,1)}, bf16[2,2,128,256]{3,2,1,0:T(8,128)(2,1)}, u32[]{:S(2)}, u32[]{:S(2)}) collective-permute-start(bf16[2,2,128,256]{3,2,1,0:T(8,128)(2,1)} %pad_maximum_fusion.9), channel_id=1, source_target_pairs={{0,64},{64,128},{128,192},{192,256},{256,320},{320,384},{384,448},... | collective-permute-start | bytes 786440 | tf_op jit(solution)/shard_map/ppermute | solution.py:129
  112.3 17.3 %collective-permute-start.7 = (bf16[2,2,128,256]{3,2,1,0:T(8,128)(2,1)}, bf16[2,2,128,256]{3,2,1,0:T(8,128)(2,1)}, u32[]{:S(2)}, u32[]{:S(2)}) collective-permute-start(bf16[2,2,128,256]{3,2,1,0:T(8,128)(2,1)} %pad_maximum_fusion.10), channel_id=1, source_target_pairs={{0,448},{64,0},{128,64},{192,128},{256,192},{320,256},{384,320},{4... | collective-permute-start | bytes 786440 | tf_op jit(solution)/shard_map/ppermute | solution.py:129
  129.6 54.5 %all-to-all-start.3 = ((bf16[32,256,128]{2,1,0:T(8,128)(2,1)}), bf16[32,256,128]{2,1,0:T(8,128)(2,1)S(1)}, u32[]{:S(2)}, u32[]{:S(2)}) async-start(bf16[32,256,128]{2,1,0:T(8,128)(2,1)} %bitcast.93), calls=%async_computation.3 | async-start | bytes 4194304 | tf_op jit(solution)/shard_map/all_to_all | solution.py:124
  146.0 11.9 %collective-permute-start.10 = (bf16[4,352,128]{2,1,0:T(8,128)(2,1)S(1)}, bf16[4,352,128]{2,1,0:T(8,128)(2,1)S(1)}, u32[]{:S(2)}, u32[]{:S(2)}) collective-permute-start(bf16[4,352,128]{2,1,0:T(8,128)(2,1)S(1)} %get-tuple-element.65), channel_id=1, source_target_pairs={{0,3},{1,0},{2,1},{3,2},{4,7},{5,4},{6,5},{7,6},{8,11},{9,8},{10,9... | collective-permute-start | bytes 1081352 | tf_op jit(solution)/shard_map/ppermute | solution.py:129
  149.5 12.7 %collective-permute-start.8 = (bf16[4,352,128]{2,1,0:T(8,128)(2,1)S(1)}, bf16[4,352,128]{2,1,0:T(8,128)(2,1)S(1)}, u32[]{:S(2)}, u32[]{:S(2)}) collective-permute-start(bf16[4,352,128]{2,1,0:T(8,128)(2,1)S(1)} %get-tuple-element.67), channel_id=1, source_target_pairs={{0,1},{1,2},{2,3},{3,0},{4,5},{5,6},{6,7},{7,4},{8,9},{9,10},{10,1... | collective-permute-start | bytes 1081352 | tf_op jit(solution)/shard_map/ppermute | solution.py:129
  163.6 19.5 %collective-permute-start.9 = (bf16[8,352,128]{2,1,0:T(8,128)(2,1)S(1)}, bf16[8,352,128]{2,1,0:T(8,128)(2,1)S(1)}, u32[]{:S(2)}, u32[]{:S(2)}) collective-permute-start(bf16[8,352,128]{2,1,0:T(8,128)(2,1)S(1)} %pad_maximum_fusion.2), channel_id=1, source_target_pairs={{0,1},{1,2},{2,3},{3,0},{4,5},{5,6},{6,7},{7,4},{8,9},{9,10},{10,1... | collective-permute-start | bytes 2162696 | tf_op jit(solution)/shard_map/ppermute | solution.py:129
  165.6 18.5 %collective-permute-start.11 = (bf16[8,352,128]{2,1,0:T(8,128)(2,1)S(1)}, bf16[8,352,128]{2,1,0:T(8,128)(2,1)}, u32[]{:S(2)}, u32[]{:S(2)}) collective-permute-start(bf16[8,352,128]{2,1,0:T(8,128)(2,1)S(1)} %pad_maximum_fusion.3), channel_id=1, source_target_pairs={{0,3},{1,0},{2,1},{3,2},{4,7},{5,4},{6,5},{7,6},{8,11},{9,8},{10,9... | collective-permute-start | bytes 2162696 | tf_op jit(solution)/shard_map/ppermute | solution.py:129
  184.1 58.0 %all-to-all-start.2 = ((bf16[32,256,128]{2,1,0:T(8,128)(2,1)}), bf16[32,256,128]{2,1,0:T(8,128)(2,1)}, u32[]{:S(2)}, u32[]{:S(2)}) async-start(bf16[32,256,128]{2,1,0:T(8,128)(2,1)} %bitcast.91), calls=%async_computation.2 | async-start | bytes 4194304 | tf_op jit(solution)/shard_map/all_to_all | solution.py:124
  194.9 18.1 %collective-permute-start.12 = (bf16[2,352,128]{2,1,0:T(8,128)(2,1)S(1)}, bf16[2,352,128]{2,1,0:T(8,128)(2,1)S(1)}, u32[]{:S(2)}, u32[]{:S(2)}) collective-permute-start(bf16[2,352,128]{2,1,0:T(8,128)(2,1)S(1)} %get-tuple-element.90), channel_id=1, source_target_pairs={{0,8},{4,12},{8,16},{12,20},{16,24},{20,28},{24,0},{28,4},{1,9},{5... | collective-permute-start | bytes 540680 | tf_op jit(solution)/shard_map/ppermute | solution.py:129
  200.7 14.2 %collective-permute-start.14 = (bf16[2,352,128]{2,1,0:T(8,128)(2,1)S(1)}, bf16[2,352,128]{2,1,0:T(8,128)(2,1)S(1)}, u32[]{:S(2)}, u32[]{:S(2)}) collective-permute-start(bf16[2,352,128]{2,1,0:T(8,128)(2,1)S(1)} %get-tuple-element.91), channel_id=1, source_target_pairs={{0,24},{4,28},{8,0},{12,4},{16,8},{20,12},{24,16},{28,20},{1,25},{... | collective-permute-start | bytes 540680 | tf_op jit(solution)/shard_map/ppermute | solution.py:129
  207.5 15.4 %collective-permute-start.13 = (bf16[2,352,128]{2,1,0:T(8,128)(2,1)S(1)}, bf16[2,352,128]{2,1,0:T(8,128)(2,1)S(1)}, u32[]{:S(2)}, u32[]{:S(2)}) collective-permute-start(bf16[2,352,128]{2,1,0:T(8,128)(2,1)S(1)} %get-tuple-element.92), channel_id=1, source_target_pairs={{0,16},{4,20},{8,24},{12,28},{16,0},{20,4},{24,8},{28,12},{1,17},{... | collective-permute-start | bytes 540680 | tf_op jit(solution)/shard_map/ppermute | solution.py:129
  223.0 9.1 %collective-permute-start.15 = (bf16[352,128]{1,0:T(8,128)(2,1)S(1)}, bf16[352,128]{1,0:T(8,128)(2,1)S(1)}, u32[]{:S(2)}, u32[]{:S(2)}) collective-permute-start(bf16[352,128]{1,0:T(8,128)(2,1)S(1)} %slice_bitcast_fusion.15), channel_id=1, source_target_pairs={{0,4},{4,8},{8,12},{12,16},{16,20},{20,24},{24,28},{28,0},{1,5},{5... | collective-permute-start | bytes 270344 | tf_op jit(solution)/shard_map/ppermute | solution.py:129
  246.1 12.3 %all-to-all-start.4 = ((f32[16,2,16]{2,1,0:T(2,128)}), f32[16,2,16]{2,1,0:T(2,128)S(1)}, u32[]{:S(2)}, u32[]{:S(2)}) async-start(f32[16,2,16]{2,1,0:T(2,128)} %bitcast.41), calls=%async_computation.4 | async-start | bytes 32768 | tf_op jit(solution)/shard_map/all_to_all | solution.py:124
  259.0 22.3 %all-to-all-start.5 = ((f32[32,2,16]{2,1,0:T(2,128)}), f32[32,2,16]{2,1,0:T(2,128)S(1)}, u32[]{:S(2)}, u32[]{:S(2)}) async-start(f32[32,2,16]{2,1,0:T(2,128)} %broadcast_in_dim.32), calls=%async_computation.5 | async-start | bytes 65536 | tf_op jit(solution)/shard_map/all_to_all | solution.py:124
  (7 other events, 53.4 us)
Sparse Core Ops, SparseCore 0:
  11.2 96.9 all-gather.2

commit v7 on v5

--- a/solution.py
+++ b/solution.py
@@ -91,15 +91,16 @@
         ).astype(jnp.bfloat16)
 
 
-def up_kernel(full_ref, hid_ref, term_ref):
-    slices, segments = term_ref.shape[0], term_ref.shape[1]
+def up_kernel(where_ref, full_ref, hid_ref, term_ref):
+    n_y, segments = term_ref.shape[1], term_ref.shape[2]
     rows = hid_ref.shape[0] // segments
+    y, core = where_ref[2], where_ref[3]
     for s in range(segments):
         hidden = hid_ref[pl.ds(s * rows, rows), :]
-        for i in range(slices):
-            term_ref[i, s] = dot(pair(full_ref, i, s * rows, rows), hidden, 0, 0).astype(
-                jnp.bfloat16
-            )
+        for i in range(2 * n_y):
+            to_y = lax.rem(i // 2 - y + n_y, n_y)
+            term = dot(pair(full_ref, i, s * rows, rows), hidden, 0, 0)
+            term_ref[lax.rem(i % 2 + core, 2), to_y, s] = term.astype(jnp.bfloat16)
 
 
 def input_kernel(where_ref, hid_ref, up_ref, out_ref):
@@ -134,6 +135,26 @@
     return lax.dynamic_slice_in_dim(twice, lax.axis_index(axis), value.shape[dim], dim)
 
 
+def backwards(value):
+    return jnp.concatenate([value[:1], jnp.flip(value[1:], 0)], axis=0)
+
+
+def placing(n_y, segments):
+    rows = 2 * n_y * segments
+    a = lax.broadcasted_iota(jnp.int32, (rows, rows), 0)
+    b = lax.broadcasted_iota(jnp.int32, (rows, rows), 1)
+    y, c = lax.axis_index("y"), lax.axis_index("c")
+    at_y = (y - b // (2 * segments) + n_y) % n_y == a // (2 * segments)
+    at_c = (b // segments + c) % 2 == (a // segments) % 2
+    return (at_y & at_c & (a % segments == b % segments)).astype(jnp.float32)
+
+
+def spread(parts):
+    crossed = shift(parts[1], "c", 1)
+    outs = [jnp.stack([parts[0, k], crossed[k]]) for k in range(parts.shape[1])]
+    return [shift(out, "y", k) if k else out for k, out in enumerate(outs)]
+
+
 def add(*values):
     return functools.reduce(lambda a, b: a + b, [v.astype(jnp.float32) for v in values])
 
@@ -153,8 +174,11 @@
 
 
 def finish_sum(near):
-    hops = [shift(near[k], "z", k) for k in range(1, near.shape[0])]
-    return add(near[0], *hops).astype(jnp.bfloat16)
+    bf16 = jnp.bfloat16
+    near = near.reshape((near.shape[0] // 2, 2) + near.shape[1:])
+    hops = [shift(near[k], "z", 2 * k) for k in range(1, near.shape[0])]
+    near = add(near[0], *hops).astype(bf16)
+    return add(near[0], shift(near[1], "z", 1)).astype(bf16)
 
 
 def body(tokens, grad_out, routes, counts, up_weight, down_weight):
@@ -182,16 +206,17 @@
 
     merged_up = exchange(merge(flat_routes, up_weight), DP)
     merged_up = merged_up.reshape(n_dp, segments, width, hidden)
-    turned_routes = from_here(from_here(all_routes.reshape(n_y, 2, segments, experts), 0, "y"), 1, "c")
+    turned_routes = from_here(all_routes.reshape(n_y, 2, segments, experts), 1, "c")
+    turned_routes = from_here(turned_routes, 0, "y")
     local_down = merge(turned_routes.swapaxes(0, 1).reshape(-1, experts), down_weight)
     local_down = local_down.reshape(2, n_y, segments, hidden, width)
-    crossed = shift(local_down[1], "c", 1)
-    downs = []
-    for k in range(n_y):
-        out = jnp.stack([local_down[0, k], crossed[k]])
-        downs.append(shift(out, "y", k) if k else out)
+    downs = spread(local_down)
     down_halves = jnp.concatenate([down_weight[:, :, :lanes], down_weight[:, :, lanes:]], axis=1)
-    merged_up, down_halves = lax.optimization_barrier((merged_up, down_halves))
+    place = placing(n_y, segments)
+    back_routes = backwards(turned_routes).reshape(-1, experts)
+    merged_up, down_halves, place, back_routes, here = lax.optimization_barrier(
+        (merged_up, down_halves, place, back_routes, here)
+    )
 
     slope, down_terms = local_kernel(
         pre_kernel,
@@ -212,11 +237,13 @@
         input_kernel, shape((n_x, n_z, group_rows, lanes), bf16), 1, here, hid, merged_up
     )
     up_terms = local_kernel(
-        up_kernel, shape((n_dp, segments, width, hidden), bf16), 0, full, hid
+        up_kernel, shape((2, n_y, segments, width, hidden), bf16), 1, here, full, hid
     )
     right, left = start_sum(parts)
     near = second_hop(parts[0], right, left)
-    up_terms, near = lax.optimization_barrier((up_terms, near))
+    up_terms = spread(up_terms)
+    near, early, down_terms = lax.optimization_barrier((near, up_terms[: n_y // 2], down_terms))
+    up_terms = jnp.stack(early + up_terms[n_y // 2 :]).reshape(-1, width, hidden)
     summed = finish_sum(near)
     down_grad = jnp.einsum(
         "ke,kab->eab", flat_routes, down_terms.astype(jnp.float32), precision=high
@@ -225,14 +252,15 @@
     down_inner = jnp.einsum(
         "kab,eab->ke", down_terms, down_halves, preferred_element_type=jnp.float32
     )
-    up_terms = exchange(up_terms.reshape(-1, width, hidden), DP)
     up_terms, down_inner = lax.optimization_barrier((up_terms, down_inner))
     up_grad = jnp.einsum(
-        "ke,kdh->edh", flat_routes, up_terms.astype(jnp.float32), precision=high
+        "ke,kdh->edh",
+        back_routes,
+        up_terms.astype(jnp.float32),
+        precision=high,
     ).astype(bf16)
-    inner = down_inner + jnp.einsum(
-        "kdh,edh->ke", up_terms, up_weight, preferred_element_type=jnp.float32
-    )
+    up_inner = jnp.einsum("kdh,edh->ke", up_terms, up_weight, preferred_element_type=jnp.float32)
+    inner = down_inner + jnp.einsum("ab,be->ae", place, up_inner, precision=high)
     own = jnp.sum(exchange(inner.reshape(all_routes.shape), DP), axis=0)
     pieces = exchange(jnp.broadcast_to(own[None], (n_z * n_x,) + own.shape), TENSOR)
     route_grad = jnp.sum(pieces, axis=0)[None]

time: 290 us -> 295 us (1.017)
  starting transfers between devices: 109 us -> 125 us
  waiting for transfers between devices: 82 us -> 66.9 us
  local copies, waits for them, and re-layouts: 14.4 us -> 17.6 us
    ppermute x19 -> x24, starting transfers between devices: 75.3 us -> 96 us  [shift(): lax.ppermute(value, axis, [(i, (i + by) % size) for i in range(size)])]
    ppermute x19 -> x24, waiting for transfers between devices: 69.1 us -> 57.9 us  [shift(): lax.ppermute(value, axis, [(i, (i + by) % size) for i in range(size)])]
    all_to_all x5 -> x4, waiting for transfers between devices: 12.5 us -> 6.7 us  [exchange(): return lax.all_to_all(value, axes, split_axis=0, concat_axis=0, tiled=True)]
    all_to_all x5 -> x4, starting transfers between devices: 34.1 us -> 28.7 us  [exchange(): return lax.all_to_all(value, axes, split_axis=0, concat_axis=0, tiled=True)]
    another operation x8 -> x16, other arithmetic: 4.48 us -> 7.51 us  [spread(): outs = [jnp.stack([parts[0, k], crossed[k]]) for k in range(parts.shape[1])]]
    unnamed x20 -> x33, local copies, waits for them, and re-layouts: 4.23 us -> 6.65 us
  transfers between devices with their start and end apart: 25 -> 29, of which waited for: 16 -> 11; matrix products, arithmetic and copies ran while one was open for 12% -> 15% of each run, Pallas kernels for 7% -> 7%
where the time goes in v7:
time: 295 us; the launch traced here: 293 us
  starting transfers between devices  125 us (42%)
  waiting for transfers between devices  66.9 us (23%)
  Pallas kernels  20.9 us (7%)
  local copies, waits for them, and re-layouts  17.6 us (6%)
  other arithmetic  17.3 us (6%)
  blocking collectives  16.7 us (6%)
  between operations  15.5 us (5%)
  matrix products  13.8 us (5%)
    ppermute x24, starting transfers between devices, shift(): lax.ppermute(value, axis, [(i, (i + by) % size) for i in range(size)])  96 us
    ppermute x24, waiting for transfers between devices, shift(): lax.ppermute(value, axis, [(i, (i + by) % size) for i in range(size)])  57.9 us
    all_to_all x4, starting transfers between devices, exchange(): return lax.all_to_all(value, axes, split_axis=0, concat_axis=0, tiled=True)  28.7 us
    pallas_call x4, Pallas kernels, local_kernel(): pl.pallas_call(kernel, out_shape=out_shapes, in_specs=smem + vmem(len(arg...  20.9 us
    all_to_all x1, blocking collectives, exchange(): return lax.all_to_all(value, axes, split_axis=0, concat_axis=0, tiled=True)  16.7 us
    another operation x16, other arithmetic, spread(): outs = [jnp.stack([parts[0, k], crossed[k]]) for k in range(parts.shape[1])]  7.51 us
    all_to_all x4, waiting for transfers between devices, exchange(): return lax.all_to_all(value, axes, split_axis=0, concat_axis=0, tiled=True)  6.7 us
    unnamed x33, local copies, waits for them, and re-layouts  6.65 us
  transfers between devices with their start and end apart: 29, of which 11 were waited for; matrix products, arithmetic and copies ran while one was open for 15% of the time, Pallas kernels for 7%

profile of v7, /device:TPU:1, one launch (start us, length us, event | category | flops | bytes accessed | tf_op | source)
XLA Modules:
  0.0 293.3 jit_solution(7467470295154975588)
XLA Ops:
  11.3 16.7 %all_to_all.25 = f32[16,2,16]{2,1,0:T(2,128)S(1)} all-to-all(f32[16,2,16]{2,1,0:T(2,128)S(1)} %broadcast_in_dim.29), channel_id=1, replica_groups=mesh['y'=8,'c'=2,'z'=8,'x'=4] {'y','c'}, dimensions={0} | all-to-all | bytes 4096 | tf_op jit(solution)/shard_map/all_to_all | solution.py:125
  53.6 4.3 %collective-permute-start.3 = (bf16[2,2,128,256]{3,2,1,0:T(8,128)(2,1)}, bf16[2,2,128,256]{3,2,1,0:T(8,128)(2,1)}, u32[]{:S(2)}, u32[]{:S(2)}) collective-permute-start(bf16[2,2,128,256]{3,2,1,0:T(8,128)(2,1)} %pad_maximum_fusion.7), channel_id=1, source_target_pairs={{0,192},{64,256},{128,320},{192,384},{256,448},{320,0},{384,64},{4... | collective-permute-start | bytes 786440 | tf_op jit(solution)/shard_map/ppermute | solution.py:130
  63.3 4.4 %collective-permute-start.5 = (bf16[2,2,128,256]{3,2,1,0:T(8,128)(2,1)}, bf16[2,2,128,256]{3,2,1,0:T(8,128)(2,1)}, u32[]{:S(2)}, u32[]{:S(2)}) collective-permute-start(bf16[2,2,128,256]{3,2,1,0:T(8,128)(2,1)} %pad_maximum_fusion.9), channel_id=1, source_target_pairs={{0,320},{64,384},{128,448},{192,0},{256,64},{320,128},{384,192},{4... | collective-permute-start | bytes 786440 | tf_op jit(solution)/shard_map/ppermute | solution.py:130
  69.2 21.1 %collective-permute-done.1.refs_1_ = bf16[2,2,128,256]{3,2,1,0:T(8,128)(2,1)} collective-permute-done((bf16[2,2,128,256]{3,2,1,0:T(8,128)(2,1)S(1)}, bf16[2,2,128,256]{3,2,1,0:T(8,128)(2,1)}, u32[]{:S(2)}, u32[]{:S(2)}) %collective-permute-start.1) | collective-permute-done | bytes 262176 | tf_op jit(solution)/shard_map/ppermute | solution.py:130
  94.2 6.1 %collective-permute-done.2.refs_2_ = bf16[2,2,128,256]{3,2,1,0:T(8,128)(2,1)} collective-permute-done((bf16[2,2,128,256]{3,2,1,0:T(8,128)(2,1)S(1)}, bf16[2,2,128,256]{3,2,1,0:T(8,128)(2,1)}, u32[]{:S(2)}, u32[]{:S(2)}) %collective-permute-start.2) | collective-permute-done | bytes 262176 | tf_op jit(solution)/shard_map/ppermute | solution.py:130
  100.3 4.7 %collective-permute-start.7 = (bf16[2,2,128,256]{3,2,1,0:T(8,128)(2,1)}, bf16[2,2,128,256]{3,2,1,0:T(8,128)(2,1)}, u32[]{:S(2)}, u32[]{:S(2)}) collective-permute-start(bf16[2,2,128,256]{3,2,1,0:T(8,128)(2,1)} %pad_maximum_fusion.11), channel_id=1, source_target_pairs={{0,448},{64,0},{128,64},{192,128},{256,192},{320,256},{384,320},{4... | collective-permute-start | bytes 786440 | tf_op jit(solution)/shard_map/ppermute | solution.py:130
  108.1 6.5 %shard_map.93 = (f32[352,128]{1,0:T(8,128)}, bf16[16,2,256,128]{3,2,1,0:T(8,128)(2,1)}) custom-call(bf16[32,704,128]{2,1,0:T(8,128)(2,1)} %bitcast.120, bf16[16,2,256,128]{3,2,1,0:T(8,128)(2,1)} %bitcast.123), custom_call_target="tpu_custom_call" | custom-call | tf_op jit(solution)/shard_map/pallas_call | solution.py:39
  117.9 10.1 %collective-permute-done.4.refs_4_ = bf16[2,2,128,256]{3,2,1,0:T(8,128)(2,1)} collective-permute-done((bf16[2,2,128,256]{3,2,1,0:T(8,128)(2,1)}, bf16[2,2,128,256]{3,2,1,0:T(8,128)(2,1)}, u32[]{:S(2)}, u32[]{:S(2)}) %collective-permute-start.4) | collective-permute-done | bytes 262176 | tf_op jit(solution)/shard_map/ppermute | solution.py:130
  128.4 6.6 %all-to-all-start.2 = ((bf16[32,256,128]{2,1,0:T(8,128)(2,1)}), bf16[32,256,128]{2,1,0:T(8,128)(2,1)S(1)}, u32[]{:S(2)}, u32[]{:S(2)}) async-start(bf16[32,256,128]{2,1,0:T(8,128)(2,1)} %bitcast.128), calls=%async_computation.2 | async-start | bytes 4194304 | tf_op jit(solution)/shard_map/all_to_all | solution.py:125
  135.1 4.8 %shard_map.94.hid_ref = bf16[352,128]{1,0:T(8,128)(2,1)} custom-call(s32[4]{0:T(128)} %pad_add_fusion.where_ref, bf16[32,704,128]{2,1,0:T(8,128)(2,1)} %bitcast.121, f32[352,128]{1,0:T(8,128)} %get-tuple-element.30.slope_ref, bf16[2,2,128,256]{3,2,1,0:T(8,128)(2,1)} %pad_maximum_fusion.4.refs_0_, bf16[2,2,128,256]{3,2,1,0:T(8,128)(2,1)} %collective-permute-done.1.refs_1_, ...), custom_call_target="tpu_custom_call" | custom-call | tf_op jit(solution)/shard_map/pallas_call | solution.py:39
  139.8 5.3 %shard_map.96 = bf16[2,8,2,256,128]{4,3,2,1,0:T(8,128)(2,1)} custom-call(s32[4]{0:T(128)} %pad_add_fusion.where_ref, bf16[32,704,128]{2,1,0:T(8,128)(2,1)} %bitcast.122, bf16[352,128]{1,0:T(8,128)(2,1)} %shard_map.94.hid_ref), custom_call_target="tpu_custom_call" | custom-call | tf_op jit(solution)/shard_map/pallas_call | solution.py:39
  145.2 4.3 %shard_map.95 = bf16[4,8,352,128]{3,2,1,0:T(8,128)(2,1)} custom-call(s32[4]{0:T(128)} %pad_add_fusion.where_ref, bf16[352,128]{1,0:T(8,128)(2,1)} %shard_map.94.hid_ref, bf16[16,2,256,128]{3,2,1,0:T(8,128)(2,1)} %bitcast.124), custom_call_target="tpu_custom_call" | custom-call | tf_op jit(solution)/shard_map/pallas_call | solution.py:39
  155.4 4.3 %collective-permute-start.10 = (bf16[4,352,128]{2,1,0:T(8,128)(2,1)S(1)}, bf16[4,352,128]{2,1,0:T(8,128)(2,1)S(1)}, u32[]{:S(2)}, u32[]{:S(2)}) collective-permute-start(bf16[4,352,128]{2,1,0:T(8,128)(2,1)S(1)} %get-tuple-element.79), channel_id=1, source_target_pairs={{0,3},{1,0},{2,1},{3,2},{4,7},{5,4},{6,5},{7,6},{8,11},{9,8},{10,9... | collective-permute-start | bytes 1081352 | tf_op jit(solution)/shard_map/ppermute | solution.py:130
  159.8 6.1 %collective-permute-done.8 = bf16[4,352,128]{2,1,0:T(8,128)(2,1)S(1)} collective-permute-done((bf16[4,352,128]{2,1,0:T(8,128)(2,1)S(1)}, bf16[4,352,128]{2,1,0:T(8,128)(2,1)S(1)}, u32[]{:S(2)}, u32[]{:S(2)}) %collective-permute-start.8) | collective-permute-done | bytes 360480 | tf_op jit(solution)/shard_map/ppermute | solution.py:130
  167.1 5.3 %collective-permute-start.11 = (bf16[8,352,128]{2,1,0:T(8,128)(2,1)S(1)}, bf16[8,352,128]{2,1,0:T(8,128)(2,1)S(1)}, u32[]{:S(2)}, u32[]{:S(2)}) collective-permute-start(bf16[8,352,128]{2,1,0:T(8,128)(2,1)S(1)} %pad_maximum_fusion.3), channel_id=1, source_target_pairs={{0,3},{1,0},{2,1},{3,2},{4,7},{5,4},{6,5},{7,6},{8,11},{9,8},{10,9... | collective-permute-start | bytes 2162696 | tf_op jit(solution)/shard_map/ppermute | solution.py:130
  182.4 4.3 %collective-permute-start.15 = (bf16[2,2,256,128]{3,2,1,0:T(8,128)(2,1)S(1)}, bf16[2,2,256,128]{3,2,1,0:T(8,128)(2,1)}, u32[]{:S(2)}, u32[]{:S(2)}) collective-permute-start(bf16[2,2,256,128]{3,2,1,0:T(8,128)(2,1)S(1)} %pad_maximum_fusion.15), channel_id=1, source_target_pairs={{0,192},{64,256},{128,320},{192,384},{256,448},{320,0},{384,64},{4... | collective-permute-start | bytes 786440 | tf_op jit(solution)/shard_map/ppermute | solution.py:130
  189.7 4.5 %collective-permute-start.20 = (bf16[2,2,256,128]{3,2,1,0:T(8,128)(2,1)}, bf16[2,2,256,128]{3,2,1,0:T(8,128)(2,1)}, u32[]{:S(2)}, u32[]{:S(2)}) collective-permute-start(bf16[2,2,256,128]{3,2,1,0:T(8,128)(2,1)} %pad_maximum_fusion.16), channel_id=1, source_target_pairs={{0,256},{64,320},{128,384},{192,448},{256,0},{320,64},{384,128},{4... | collective-permute-start | bytes 786440 | tf_op jit(solution)/shard_map/ppermute | solution.py:130
  199.6 4.8 %collective-permute-start.22 = (bf16[2,2,256,128]{3,2,1,0:T(8,128)(2,1)}, bf16[2,2,256,128]{3,2,1,0:T(8,128)(2,1)}, u32[]{:S(2)}, u32[]{:S(2)}) collective-permute-start(bf16[2,2,256,128]{3,2,1,0:T(8,128)(2,1)} %pad_maximum_fusion.18), channel_id=1, source_target_pairs={{0,384},{64,448},{128,0},{192,64},{256,128},{320,192},{384,256},{4... | collective-permute-start | bytes 786440 | tf_op jit(solution)/shard_map/ppermute | solution.py:130
  207.5 10.0 %collective-permute-done.15 = bf16[2,2,256,128]{3,2,1,0:T(8,128)(2,1)} collective-permute-done((bf16[2,2,256,128]{3,2,1,0:T(8,128)(2,1)S(1)}, bf16[2,2,256,128]{3,2,1,0:T(8,128)(2,1)}, u32[]{:S(2)}, u32[]{:S(2)}) %collective-permute-start.15) | collective-permute-done | bytes 262176 | tf_op jit(solution)/shard_map/ppermute | solution.py:130
  223.2 4.9 %collective-permute-start.16 = (bf16[2,352,128]{2,1,0:T(8,128)(2,1)}, bf16[2,352,128]{2,1,0:T(8,128)(2,1)}, u32[]{:S(2)}, u32[]{:S(2)}) collective-permute-start(bf16[2,352,128]{2,1,0:T(8,128)(2,1)} %get-tuple-element.118), channel_id=1, source_target_pairs={{0,8},{4,12},{8,16},{12,20},{16,24},{20,28},{24,0},{28,4},{1,9},{5... | collective-permute-start | bytes 540680 | tf_op jit(solution)/shard_map/ppermute | solution.py:130
  229.2 8.4 %collective-permute-start.18 = (bf16[2,352,128]{2,1,0:T(8,128)(2,1)}, bf16[2,352,128]{2,1,0:T(8,128)(2,1)S(1)}, u32[]{:S(2)}, u32[]{:S(2)}) collective-permute-start(bf16[2,352,128]{2,1,0:T(8,128)(2,1)} %get-tuple-element.119), channel_id=1, source_target_pairs={{0,24},{4,28},{8,0},{12,4},{16,8},{20,12},{24,16},{28,20},{1,25},{... | collective-permute-start | bytes 540680 | tf_op jit(solution)/shard_map/ppermute | solution.py:130
  250.3 8.7 %all-to-all-start.3 = ((f32[16,2,16]{2,1,0:T(2,128)}), f32[16,2,16]{2,1,0:T(2,128)S(1)}, u32[]{:S(2)}, u32[]{:S(2)}) async-start(f32[16,2,16]{2,1,0:T(2,128)} %bitcast.58), calls=%async_computation.3 | async-start | bytes 32768 | tf_op jit(solution)/shard_map/all_to_all | solution.py:125
  260.2 6.2 %all-to-all-done.3 = f32[16,2,16]{2,1,0:T(2,128)S(1)} async-done(((f32[16,2,16]{2,1,0:T(2,128)}), f32[16,2,16]{2,1,0:T(2,128)S(1)}, u32[]{:S(2)}, u32[]{:S(2)}) %all-to-all-start.3) | async-done | bytes 2080 | tf_op jit(solution)/shard_map/all_to_all | solution.py:125
  267.0 9.4 %all-to-all-start.4 = ((f32[32,2,16]{2,1,0:T(2,128)}), f32[32,2,16]{2,1,0:T(2,128)S(1)}, u32[]{:S(2)}, u32[]{:S(2)}) async-start(f32[32,2,16]{2,1,0:T(2,128)} %broadcast_in_dim.32), calls=%async_computation.4 | async-start | bytes 65536 | tf_op jit(solution)/shard_map/all_to_all | solution.py:125
  (144 shorter events, 106.1 us)
Async XLA Ops:
  7.2 100.9 %all-gather.3.cloned.1.call-start = ((), (), s32[]{:S(2)}) async-start(), calls=%async_computation.5 | async-start | bytes 5947392 | tf_op jit(solution)/shard_map/all_gather | solution.py:200
  32.0 73.8 %all-to-all-start.1 = ((bf16[32,256,128]{2,1,0:T(8,128)(2,1)}), bf16[32,256,128]{2,1,0:T(8,128)(2,1)S(1)}, u32[]{:S(2)}, u32[]{:S(2)}) async-start(bf16[32,256,128]{2,1,0:T(8,128)(2,1)} %copy.104), calls=%async_computation.1 | async-start | bytes 4194304 | tf_op jit(solution)/shard_map/all_to_all | solution.py:125
  45.3 44.9 %collective-permute-start.1 = (bf16[2,2,128,256]{3,2,1,0:T(8,128)(2,1)S(1)}, bf16[2,2,128,256]{3,2,1,0:T(8,128)(2,1)}, u32[]{:S(2)}, u32[]{:S(2)}) collective-permute-start(bf16[2,2,128,256]{3,2,1,0:T(8,128)(2,1)S(1)} %pad_maximum_fusion.5), channel_id=1, source_target_pairs={{0,64},{64,128},{128,192},{192,256},{256,320},{320,384},{384,448},... | collective-permute-start | bytes 786440 | tf_op jit(solution)/shard_map/ppermute | solution.py:130
  48.8 51.5 %collective-permute-start.2 = (bf16[2,2,128,256]{3,2,1,0:T(8,128)(2,1)S(1)}, bf16[2,2,128,256]{3,2,1,0:T(8,128)(2,1)}, u32[]{:S(2)}, u32[]{:S(2)}) collective-permute-start(bf16[2,2,128,256]{3,2,1,0:T(8,128)(2,1)S(1)} %pad_maximum_fusion.6), channel_id=1, source_target_pairs={{0,128},{64,192},{128,256},{192,320},{256,384},{320,448},{384,0},{... | collective-permute-start | bytes 786440 | tf_op jit(solution)/shard_map/ppermute | solution.py:130
  53.6 64.4 %collective-permute-start.3 = (bf16[2,2,128,256]{3,2,1,0:T(8,128)(2,1)}, bf16[2,2,128,256]{3,2,1,0:T(8,128)(2,1)}, u32[]{:S(2)}, u32[]{:S(2)}) collective-permute-start(bf16[2,2,128,256]{3,2,1,0:T(8,128)(2,1)} %pad_maximum_fusion.7), channel_id=1, source_target_pairs={{0,192},{64,256},{128,320},{192,384},{256,448},{320,0},{384,64},{4... | collective-permute-start | bytes 786440 | tf_op jit(solution)/shard_map/ppermute | solution.py:130
  58.6 69.4 %collective-permute-start.4 = (bf16[2,2,128,256]{3,2,1,0:T(8,128)(2,1)}, bf16[2,2,128,256]{3,2,1,0:T(8,128)(2,1)}, u32[]{:S(2)}, u32[]{:S(2)}) collective-permute-start(bf16[2,2,128,256]{3,2,1,0:T(8,128)(2,1)} %pad_maximum_fusion.8), channel_id=1, source_target_pairs={{0,256},{64,320},{128,384},{192,448},{256,0},{320,64},{384,128},{4... | collective-permute-start | bytes 786440 | tf_op jit(solution)/shard_map/ppermute | solution.py:130
  63.3 64.8 %collective-permute-start.5 = (bf16[2,2,128,256]{3,2,1,0:T(8,128)(2,1)}, bf16[2,2,128,256]{3,2,1,0:T(8,128)(2,1)}, u32[]{:S(2)}, u32[]{:S(2)}) collective-permute-start(bf16[2,2,128,256]{3,2,1,0:T(8,128)(2,1)} %pad_maximum_fusion.9), channel_id=1, source_target_pairs={{0,320},{64,384},{128,448},{192,0},{256,64},{320,128},{384,192},{4... | collective-permute-start | bytes 786440 | tf_op jit(solution)/shard_map/ppermute | solution.py:130
  90.2 37.8 %collective-permute-start.6 = (bf16[2,2,128,256]{3,2,1,0:T(8,128)(2,1)}, bf16[2,2,128,256]{3,2,1,0:T(8,128)(2,1)}, u32[]{:S(2)}, u32[]{:S(2)}) collective-permute-start(bf16[2,2,128,256]{3,2,1,0:T(8,128)(2,1)} %pad_maximum_fusion.10), channel_id=1, source_target_pairs={{0,384},{64,448},{128,0},{192,64},{256,128},{320,192},{384,256},{4... | collective-permute-start | bytes 786440 | tf_op jit(solution)/shard_map/ppermute | solution.py:130
  100.3 28.2 %collective-permute-start.7 = (bf16[2,2,128,256]{3,2,1,0:T(8,128)(2,1)}, bf16[2,2,128,256]{3,2,1,0:T(8,128)(2,1)}, u32[]{:S(2)}, u32[]{:S(2)}) collective-permute-start(bf16[2,2,128,256]{3,2,1,0:T(8,128)(2,1)} %pad_maximum_fusion.11), channel_id=1, source_target_pairs={{0,448},{64,0},{128,64},{192,128},{256,192},{320,256},{384,320},{4... | collective-permute-start | bytes 786440 | tf_op jit(solution)/shard_map/ppermute | solution.py:130
  128.4 89.0 %all-to-all-start.2 = ((bf16[32,256,128]{2,1,0:T(8,128)(2,1)}), bf16[32,256,128]{2,1,0:T(8,128)(2,1)S(1)}, u32[]{:S(2)}, u32[]{:S(2)}) async-start(bf16[32,256,128]{2,1,0:T(8,128)(2,1)} %bitcast.128), calls=%async_computation.2 | async-start | bytes 4194304 | tf_op jit(solution)/shard_map/all_to_all | solution.py:125
  149.5 24.9 %collective-permute-start.12 = (bf16[8,2,256,128]{3,2,1,0:T(8,128)(2,1)S(1)}, bf16[8,2,256,128]{3,2,1,0:T(8,128)(2,1)S(1)}, u32[]{:S(2)}, u32[]{:S(2)}) collective-permute-start(bf16[8,2,256,128]{3,2,1,0:T(8,128)(2,1)S(1)} %slice_bitcast_fusion), channel_id=1, source_target_pairs={{0,32},{32,0},{1,33},{33,1},{2,34},{34,2},{3,35},{35,3},{4,36},{36... | collective-permute-start | bytes 3145736 | tf_op jit(solution)/shard_map/ppermute | solution.py:130
  167.1 22.6 %collective-permute-start.11 = (bf16[8,352,128]{2,1,0:T(8,128)(2,1)S(1)}, bf16[8,352,128]{2,1,0:T(8,128)(2,1)S(1)}, u32[]{:S(2)}, u32[]{:S(2)}) collective-permute-start(bf16[8,352,128]{2,1,0:T(8,128)(2,1)S(1)} %pad_maximum_fusion.3), channel_id=1, source_target_pairs={{0,3},{1,0},{2,1},{3,2},{4,7},{5,4},{6,5},{7,6},{8,11},{9,8},{10,9... | collective-permute-start | bytes 2162696 | tf_op jit(solution)/shard_map/ppermute | solution.py:130
  172.5 21.8 %collective-permute-start.9 = (bf16[8,352,128]{2,1,0:T(8,128)(2,1)S(1)}, bf16[8,352,128]{2,1,0:T(8,128)(2,1)S(1)}, u32[]{:S(2)}, u32[]{:S(2)}) collective-permute-start(bf16[8,352,128]{2,1,0:T(8,128)(2,1)S(1)} %pad_maximum_fusion.2), channel_id=1, source_target_pairs={{0,1},{1,2},{2,3},{3,0},{4,5},{5,6},{6,7},{7,4},{8,9},{9,10},{10,1... | collective-permute-start | bytes 2162696 | tf_op jit(solution)/shard_map/ppermute | solution.py:130
  174.5 25.1 %collective-permute-start.13 = (bf16[2,2,256,128]{3,2,1,0:T(8,128)(2,1)S(1)}, bf16[2,2,256,128]{3,2,1,0:T(8,128)(2,1)S(1)}, u32[]{:S(2)}, u32[]{:S(2)}) collective-permute-start(bf16[2,2,256,128]{3,2,1,0:T(8,128)(2,1)S(1)} %pad_maximum_fusion.13), channel_id=1, source_target_pairs={{0,64},{64,128},{128,192},{192,256},{256,320},{320,384},{384,448},... | collective-permute-start | bytes 786440 | tf_op jit(solution)/shard_map/ppermute | solution.py:130
  178.4 26.0 %collective-permute-start.14 = (bf16[2,2,256,128]{3,2,1,0:T(8,128)(2,1)S(1)}, bf16[2,2,256,128]{3,2,1,0:T(8,128)(2,1)S(1)}, u32[]{:S(2)}, u32[]{:S(2)}) collective-permute-start(bf16[2,2,256,128]{3,2,1,0:T(8,128)(2,1)S(1)} %pad_maximum_fusion.14), channel_id=1, source_target_pairs={{0,128},{64,192},{128,256},{192,320},{256,384},{320,448},{384,0},{... | collective-permute-start | bytes 786440 | tf_op jit(solution)/shard_map/ppermute | solution.py:130
  182.4 35.1 %collective-permute-start.15 = (bf16[2,2,256,128]{3,2,1,0:T(8,128)(2,1)S(1)}, bf16[2,2,256,128]{3,2,1,0:T(8,128)(2,1)}, u32[]{:S(2)}, u32[]{:S(2)}) collective-permute-start(bf16[2,2,256,128]{3,2,1,0:T(8,128)(2,1)S(1)} %pad_maximum_fusion.15), channel_id=1, source_target_pairs={{0,192},{64,256},{128,320},{192,384},{256,448},{320,0},{384,64},{4... | collective-permute-start | bytes 786440 | tf_op jit(solution)/shard_map/ppermute | solution.py:130
  189.7 39.5 %collective-permute-start.20 = (bf16[2,2,256,128]{3,2,1,0:T(8,128)(2,1)}, bf16[2,2,256,128]{3,2,1,0:T(8,128)(2,1)}, u32[]{:S(2)}, u32[]{:S(2)}) collective-permute-start(bf16[2,2,256,128]{3,2,1,0:T(8,128)(2,1)} %pad_maximum_fusion.16), channel_id=1, source_target_pairs={{0,256},{64,320},{128,384},{192,448},{256,0},{320,64},{384,128},{4... | collective-permute-start | bytes 786440 | tf_op jit(solution)/shard_map/ppermute | solution.py:130
  194.2 44.3 %collective-permute-start.21 = (bf16[2,2,256,128]{3,2,1,0:T(8,128)(2,1)}, bf16[2,2,256,128]{3,2,1,0:T(8,128)(2,1)}, u32[]{:S(2)}, u32[]{:S(2)}) collective-permute-start(bf16[2,2,256,128]{3,2,1,0:T(8,128)(2,1)} %pad_maximum_fusion.17), channel_id=1, source_target_pairs={{0,320},{64,384},{128,448},{192,0},{256,64},{320,128},{384,192},{4... | collective-permute-start | bytes 786440 | tf_op jit(solution)/shard_map/ppermute | solution.py:130
  199.6 44.0 %collective-permute-start.22 = (bf16[2,2,256,128]{3,2,1,0:T(8,128)(2,1)}, bf16[2,2,256,128]{3,2,1,0:T(8,128)(2,1)}, u32[]{:S(2)}, u32[]{:S(2)}) collective-permute-start(bf16[2,2,256,128]{3,2,1,0:T(8,128)(2,1)} %pad_maximum_fusion.18), channel_id=1, source_target_pairs={{0,384},{64,448},{128,0},{192,64},{256,128},{320,192},{384,256},{4... | collective-permute-start | bytes 786440 | tf_op jit(solution)/shard_map/ppermute | solution.py:130
  204.4 40.2 %collective-permute-start.23 = (bf16[2,2,256,128]{3,2,1,0:T(8,128)(2,1)}, bf16[2,2,256,128]{3,2,1,0:T(8,128)(2,1)}, u32[]{:S(2)}, u32[]{:S(2)}) collective-permute-start(bf16[2,2,256,128]{3,2,1,0:T(8,128)(2,1)} %pad_maximum_fusion.19), channel_id=1, source_target_pairs={{0,448},{64,0},{128,64},{192,128},{256,192},{320,256},{384,320},{4... | collective-permute-start | bytes 786440 | tf_op jit(solution)/shard_map/ppermute | solution.py:130
  223.2 53.3 %collective-permute-start.16 = (bf16[2,352,128]{2,1,0:T(8,128)(2,1)}, bf16[2,352,128]{2,1,0:T(8,128)(2,1)}, u32[]{:S(2)}, u32[]{:S(2)}) collective-permute-start(bf16[2,352,128]{2,1,0:T(8,128)(2,1)} %get-tuple-element.118), channel_id=1, source_target_pairs={{0,8},{4,12},{8,16},{12,20},{16,24},{20,28},{24,0},{28,4},{1,9},{5... | collective-permute-start | bytes 540680 | tf_op jit(solution)/shard_map/ppermute | solution.py:130
  229.2 47.3 %collective-permute-start.18 = (bf16[2,352,128]{2,1,0:T(8,128)(2,1)}, bf16[2,352,128]{2,1,0:T(8,128)(2,1)S(1)}, u32[]{:S(2)}, u32[]{:S(2)}) collective-permute-start(bf16[2,352,128]{2,1,0:T(8,128)(2,1)} %get-tuple-element.119), channel_id=1, source_target_pairs={{0,24},{4,28},{8,0},{12,4},{16,8},{20,12},{24,16},{28,20},{1,25},{... | collective-permute-start | bytes 540680 | tf_op jit(solution)/shard_map/ppermute | solution.py:130
  238.5 38.0 %collective-permute-start.17 = (bf16[2,352,128]{2,1,0:T(8,128)(2,1)}, bf16[2,352,128]{2,1,0:T(8,128)(2,1)S(1)}, u32[]{:S(2)}, u32[]{:S(2)}) collective-permute-start(bf16[2,352,128]{2,1,0:T(8,128)(2,1)} %get-tuple-element.120), channel_id=1, source_target_pairs={{0,16},{4,20},{8,24},{12,28},{16,0},{20,4},{24,8},{28,12},{1,17},{... | collective-permute-start | bytes 540680 | tf_op jit(solution)/shard_map/ppermute | solution.py:130
  267.0 18.1 %all-to-all-start.4 = ((f32[32,2,16]{2,1,0:T(2,128)}), f32[32,2,16]{2,1,0:T(2,128)S(1)}, u32[]{:S(2)}, u32[]{:S(2)}) async-start(f32[32,2,16]{2,1,0:T(2,128)} %broadcast_in_dim.32), calls=%async_computation.4 | async-start | bytes 65536 | tf_op jit(solution)/shard_map/all_to_all | solution.py:125
  (17 other events, 144.5 us)
Sparse Core Ops, SparseCore 0:
  11.2 96.9 all-gather.2

commit v8 on v7

--- a/solution.py
+++ b/solution.py
@@ -149,9 +149,12 @@
     return (at_y & at_c & (a % segments == b % segments)).astype(jnp.float32)
 
 
-def spread(parts):
+def cross(parts):
     crossed = shift(parts[1], "c", 1)
-    outs = [jnp.stack([parts[0, k], crossed[k]]) for k in range(parts.shape[1])]
+    return [jnp.stack([parts[0, k], crossed[k]]) for k in range(parts.shape[1])]
+
+
+def spread(outs):
     return [shift(out, "y", k) if k else out for k, out in enumerate(outs)]
 
 
@@ -210,7 +213,7 @@
     turned_routes = from_here(turned_routes, 0, "y")
     local_down = merge(turned_routes.swapaxes(0, 1).reshape(-1, experts), down_weight)
     local_down = local_down.reshape(2, n_y, segments, hidden, width)
-    downs = spread(local_down)
+    downs = spread(cross(local_down))
     down_halves = jnp.concatenate([down_weight[:, :, :lanes], down_weight[:, :, lanes:]], axis=1)
     place = placing(n_y, segments)
     back_routes = backwards(turned_routes).reshape(-1, experts)
@@ -241,10 +244,9 @@
     )
     right, left = start_sum(parts)
     near = second_hop(parts[0], right, left)
-    up_terms = spread(up_terms)
-    near, early, down_terms = lax.optimization_barrier((near, up_terms[: n_y // 2], down_terms))
-    up_terms = jnp.stack(early + up_terms[n_y // 2 :]).reshape(-1, width, hidden)
+    outs = cross(up_terms)
     summed = finish_sum(near)
+    up_terms = jnp.stack(spread(outs)).reshape(-1, width, hidden)
     down_grad = jnp.einsum(
         "ke,kab->eab", flat_routes, down_terms.astype(jnp.float32), precision=high
     ).astype(bf16)

time: 295 us -> 312 us (1.058)
  waiting for transfers between devices: 66.9 us -> 92.2 us
  starting transfers between devices: 125 us -> 120 us
  matrix products: 13.8 us -> 17.9 us
  other arithmetic: 17.3 us -> 13.8 us
  local copies, waits for them, and re-layouts: 17.6 us -> 14.2 us
    ppermute x24, waiting for transfers between devices: 57.9 us -> 80.3 us  [shift(): lax.ppermute(value, axis, [(i, (i + by) % size) for i in range(size)])]
    all_to_all x4, starting transfers between devices: 28.7 us -> 22.1 us  [exchange(): return lax.all_to_all(value, axes, split_axis=0, concat_axis=0, tiled=True)]
    unnamed x33 -> x20, local copies, waits for them, and re-layouts: 6.65 us -> 2.8 us
    another operation x16 -> x15, other arithmetic: 7.51 us -> 4.65 us  [cross(): return [jnp.stack([parts[0, k], crossed[k]]) for k in range(parts.shape[1])]]
  transfers between devices with their start and end apart: 29 -> 29, of which waited for: 11 -> 17; matrix products, arithmetic and copies ran while one was open for 15% -> 10% of each run, Pallas kernels for 7% -> 2%
where the time goes in v8:
time: 312 us; the launch traced here: 311 us
  starting transfers between devices  120 us (38%)
  waiting for transfers between devices  92.2 us (30%)
  Pallas kernels  20.9 us (7%)
  matrix products  17.9 us (6%)
  blocking collectives  16.7 us (5%)
  between operations  15.5 us (5%)
  local copies, waits for them, and re-layouts  14.2 us (5%)
  other arithmetic  13.8 us (4%)
    ppermute x24, starting transfers between devices, shift(): lax.ppermute(value, axis, [(i, (i + by) % size) for i in range(size)])  97.5 us
    ppermute x24, waiting for transfers between devices, shift(): lax.ppermute(value, axis, [(i, (i + by) % size) for i in range(size)])  80.3 us
    all_to_all x4, starting transfers between devices, exchange(): return lax.all_to_all(value, axes, split_axis=0, concat_axis=0, tiled=True)  22.1 us
    pallas_call x4, Pallas kernels, local_kernel(): pl.pallas_call(kernel, out_shape=out_shapes, in_specs=smem + vmem(len(arg...  20.9 us
    all_to_all x1, blocking collectives, exchange(): return lax.all_to_all(value, axes, split_axis=0, concat_axis=0, tiled=True)  16.7 us
    all_to_all x4, waiting for transfers between devices, exchange(): return lax.all_to_all(value, axes, split_axis=0, concat_axis=0, tiled=True)  9.72 us
  transfers between devices with their start and end apart: 29, of which 17 were waited for; matrix products, arithmetic and copies ran while one was open for 10% of the time, Pallas kernels for 2%

profile of v8, /device:TPU:1, one launch (start us, length us, event | category | flops | bytes accessed | tf_op | source)
XLA Modules:
  0.0 310.7 jit_solution(5357580451704279464)
XLA Ops:
  11.3 16.7 %all_to_all.25 = f32[16,2,16]{2,1,0:T(2,128)S(1)} all-to-all(f32[16,2,16]{2,1,0:T(2,128)S(1)} %broadcast_in_dim.29), channel_id=1, replica_groups=mesh['y'=8,'c'=2,'z'=8,'x'=4] {'y','c'}, dimensions={0} | all-to-all | bytes 4096 | tf_op jit(solution)/shard_map/all_to_all | solution.py:125
  69.1 21.1 %collective-permute-done.1.refs_1_ = bf16[2,2,128,256]{3,2,1,0:T(8,128)(2,1)} collective-permute-done((bf16[2,2,128,256]{3,2,1,0:T(8,128)(2,1)S(1)}, bf16[2,2,128,256]{3,2,1,0:T(8,128)(2,1)}, u32[]{:S(2)}, u32[]{:S(2)}) %collective-permute-start.1) | collective-permute-done | bytes 262176 | tf_op jit(solution)/shard_map/ppermute | solution.py:130
  94.2 6.1 %collective-permute-done.2.refs_2_ = bf16[2,2,128,256]{3,2,1,0:T(8,128)(2,1)} collective-permute-done((bf16[2,2,128,256]{3,2,1,0:T(8,128)(2,1)S(1)}, bf16[2,2,128,256]{3,2,1,0:T(8,128)(2,1)}, u32[]{:S(2)}, u32[]{:S(2)}) %collective-permute-start.2) | collective-permute-done | bytes 262176 | tf_op jit(solution)/shard_map/ppermute | solution.py:130
  100.2 4.9 %collective-permute-start.7 = (bf16[2,2,128,256]{3,2,1,0:T(8,128)(2,1)}, bf16[2,2,128,256]{3,2,1,0:T(8,128)(2,1)}, u32[]{:S(2)}, u32[]{:S(2)}) collective-permute-start(bf16[2,2,128,256]{3,2,1,0:T(8,128)(2,1)} %pad_maximum_fusion.11), channel_id=1, source_target_pairs={{0,448},{64,0},{128,64},{192,128},{256,192},{320,256},{384,320},{4... | collective-permute-start | bytes 786440 | tf_op jit(solution)/shard_map/ppermute | solution.py:130
  108.1 6.5 %shard_map.93 = (f32[352,128]{1,0:T(8,128)}, bf16[16,2,256,128]{3,2,1,0:T(8,128)(2,1)}) custom-call(bf16[32,704,128]{2,1,0:T(8,128)(2,1)} %bitcast.122, bf16[16,2,256,128]{3,2,1,0:T(8,128)(2,1)} %bitcast.125), custom_call_target="tpu_custom_call" | custom-call | tf_op jit(solution)/shard_map/pallas_call | solution.py:39
  117.9 10.1 %collective-permute-done.4.refs_4_ = bf16[2,2,128,256]{3,2,1,0:T(8,128)(2,1)} collective-permute-done((bf16[2,2,128,256]{3,2,1,0:T(8,128)(2,1)}, bf16[2,2,128,256]{3,2,1,0:T(8,128)(2,1)}, u32[]{:S(2)}, u32[]{:S(2)}) %collective-permute-start.4) | collective-permute-done | bytes 262176 | tf_op jit(solution)/shard_map/ppermute | solution.py:130
  128.4 4.8 %shard_map.94.hid_ref = bf16[352,128]{1,0:T(8,128)(2,1)} custom-call(s32[4]{0:T(128)} %pad_add_fusion.where_ref, bf16[32,704,128]{2,1,0:T(8,128)(2,1)} %bitcast.123, f32[352,128]{1,0:T(8,128)} %get-tuple-element.24.slope_ref, bf16[2,2,128,256]{3,2,1,0:T(8,128)(2,1)} %pad_maximum_fusion.4.refs_0_, bf16[2,2,128,256]{3,2,1,0:T(8,128)(2,1)} %collective-permute-done.1.refs_1_, ...), custom_call_target="tpu_custom_call" | custom-call | tf_op jit(solution)/shard_map/pallas_call | solution.py:39
  133.2 5.3 %shard_map.96 = bf16[2,8,2,256,128]{4,3,2,1,0:T(8,128)(2,1)} custom-call(s32[4]{0:T(128)} %pad_add_fusion.where_ref, bf16[32,704,128]{2,1,0:T(8,128)(2,1)} %bitcast.124, bf16[352,128]{1,0:T(8,128)(2,1)} %shard_map.94.hid_ref), custom_call_target="tpu_custom_call" | custom-call | tf_op jit(solution)/shard_map/pallas_call | solution.py:39
  155.4 6.3 %all-to-all-start.2 = ((bf16[32,256,128]{2,1,0:T(8,128)(2,1)}), bf16[32,256,128]{2,1,0:T(8,128)(2,1)}, u32[]{:S(2)}, u32[]{:S(2)}) async-start(bf16[32,256,128]{2,1,0:T(8,128)(2,1)} %bitcast.130), calls=%async_computation.2 | async-start | bytes 4194304 | tf_op jit(solution)/shard_map/all_to_all | solution.py:125
  164.8 5.3 %collective-permute-start.11 = (bf16[8,352,128]{2,1,0:T(8,128)(2,1)S(1)}, bf16[8,352,128]{2,1,0:T(8,128)(2,1)S(1)}, u32[]{:S(2)}, u32[]{:S(2)}) collective-permute-start(bf16[8,352,128]{2,1,0:T(8,128)(2,1)S(1)} %pad_maximum_fusion.3), channel_id=1, source_target_pairs={{0,3},{1,0},{2,1},{3,2},{4,7},{5,4},{6,5},{7,6},{8,11},{9,8},{10,9... | collective-permute-start | bytes 2162696 | tf_op jit(solution)/shard_map/ppermute | solution.py:130
  176.9 4.9 %collective-permute-start.18 = (bf16[2,2,256,128]{3,2,1,0:T(8,128)(2,1)S(1)}, bf16[2,2,256,128]{3,2,1,0:T(8,128)(2,1)S(1)}, u32[]{:S(2)}, u32[]{:S(2)}) collective-permute-start(bf16[2,2,256,128]{3,2,1,0:T(8,128)(2,1)S(1)} %pad_maximum_fusion.13), channel_id=1, source_target_pairs={{0,128},{64,192},{128,256},{192,320},{256,384},{320,448},{384,0},{... | collective-permute-start | bytes 786440 | tf_op jit(solution)/shard_map/ppermute | solution.py:130
  184.5 5.2 %collective-permute-done.9 = bf16[8,352,128]{2,1,0:T(8,128)(2,1)S(1)} collective-permute-done((bf16[8,352,128]{2,1,0:T(8,128)(2,1)S(1)}, bf16[8,352,128]{2,1,0:T(8,128)(2,1)S(1)}, u32[]{:S(2)}, u32[]{:S(2)}) %collective-permute-start.9) | collective-permute-done | bytes 720928 | tf_op jit(solution)/shard_map/ppermute | solution.py:130
  191.1 4.9 %collective-permute-start.12 = (bf16[2,352,128]{2,1,0:T(8,128)(2,1)S(1)}, bf16[2,352,128]{2,1,0:T(8,128)(2,1)S(1)}, u32[]{:S(2)}, u32[]{:S(2)}) collective-permute-start(bf16[2,352,128]{2,1,0:T(8,128)(2,1)S(1)} %get-tuple-element.106), channel_id=1, source_target_pairs={{0,8},{4,12},{8,16},{12,20},{16,24},{20,28},{24,0},{28,4},{1,9},{5... | collective-permute-start | bytes 540680 | tf_op jit(solution)/shard_map/ppermute | solution.py:130
  196.0 6.8 %collective-permute-start.14 = (bf16[2,352,128]{2,1,0:T(8,128)(2,1)S(1)}, bf16[2,352,128]{2,1,0:T(8,128)(2,1)S(1)}, u32[]{:S(2)}, u32[]{:S(2)}) collective-permute-start(bf16[2,352,128]{2,1,0:T(8,128)(2,1)S(1)} %get-tuple-element.107), channel_id=1, source_target_pairs={{0,24},{4,28},{8,0},{12,4},{16,8},{20,12},{24,16},{28,20},{1,25},{... | collective-permute-start | bytes 540680 | tf_op jit(solution)/shard_map/ppermute | solution.py:130
  202.8 5.4 %collective-permute-start.13 = (bf16[2,352,128]{2,1,0:T(8,128)(2,1)S(1)}, bf16[2,352,128]{2,1,0:T(8,128)(2,1)S(1)}, u32[]{:S(2)}, u32[]{:S(2)}) collective-permute-start(bf16[2,352,128]{2,1,0:T(8,128)(2,1)S(1)} %get-tuple-element.108), channel_id=1, source_target_pairs={{0,16},{4,20},{8,24},{12,28},{16,0},{20,4},{24,8},{28,12},{1,17},{... | collective-permute-start | bytes 540680 | tf_op jit(solution)/shard_map/ppermute | solution.py:130
  208.3 6.0 %collective-permute-start.19 = (bf16[2,2,256,128]{3,2,1,0:T(8,128)(2,1)S(1)}, bf16[2,2,256,128]{3,2,1,0:T(8,128)(2,1)S(1)}, u32[]{:S(2)}, u32[]{:S(2)}) collective-permute-start(bf16[2,2,256,128]{3,2,1,0:T(8,128)(2,1)S(1)} %pad_maximum_fusion.14), channel_id=1, source_target_pairs={{0,192},{64,256},{128,320},{192,384},{256,448},{320,0},{384,64},{4... | collective-permute-start | bytes 786440 | tf_op jit(solution)/shard_map/ppermute | solution.py:130
  219.4 4.9 %collective-permute-start.21 = (bf16[2,2,256,128]{3,2,1,0:T(8,128)(2,1)S(1)}, bf16[2,2,256,128]{3,2,1,0:T(8,128)(2,1)S(1)}, u32[]{:S(2)}, u32[]{:S(2)}) collective-permute-start(bf16[2,2,256,128]{3,2,1,0:T(8,128)(2,1)S(1)} %pad_maximum_fusion.16), channel_id=1, source_target_pairs={{0,320},{64,384},{128,448},{192,0},{256,64},{320,128},{384,192},{4... | collective-permute-start | bytes 786440 | tf_op jit(solution)/shard_map/ppermute | solution.py:130
  224.5 5.3 %collective-permute-start.22 = (bf16[2,2,256,128]{3,2,1,0:T(8,128)(2,1)S(1)}, bf16[2,2,256,128]{3,2,1,0:T(8,128)(2,1)S(1)}, u32[]{:S(2)}, u32[]{:S(2)}) collective-permute-start(bf16[2,2,256,128]{3,2,1,0:T(8,128)(2,1)S(1)} %pad_maximum_fusion.17), channel_id=1, source_target_pairs={{0,384},{64,448},{128,0},{192,64},{256,128},{320,192},{384,256},{4... | collective-permute-start | bytes 786440 | tf_op jit(solution)/shard_map/ppermute | solution.py:130
  233.2 10.5 %collective-permute-done.19 = bf16[2,2,256,128]{3,2,1,0:T(8,128)(2,1)S(1)} collective-permute-done((bf16[2,2,256,128]{3,2,1,0:T(8,128)(2,1)S(1)}, bf16[2,2,256,128]{3,2,1,0:T(8,128)(2,1)S(1)}, u32[]{:S(2)}, u32[]{:S(2)}) %collective-permute-start.19) | collective-permute-done | bytes 262176 | tf_op jit(solution)/shard_map/ppermute | solution.py:130
  247.0 6.8 %collective-permute-done.20 = bf16[2,2,256,128]{3,2,1,0:T(8,128)(2,1)S(1)} collective-permute-done((bf16[2,2,256,128]{3,2,1,0:T(8,128)(2,1)S(1)}, bf16[2,2,256,128]{3,2,1,0:T(8,128)(2,1)S(1)}, u32[]{:S(2)}, u32[]{:S(2)}) %collective-permute-start.20) | collective-permute-done | bytes 262176 | tf_op jit(solution)/shard_map/ppermute | solution.py:130
  253.9 7.9 %collective-permute-done.22 = bf16[2,2,256,128]{3,2,1,0:T(8,128)(2,1)S(1)} collective-permute-done((bf16[2,2,256,128]{3,2,1,0:T(8,128)(2,1)S(1)}, bf16[2,2,256,128]{3,2,1,0:T(8,128)(2,1)S(1)}, u32[]{:S(2)}, u32[]{:S(2)}) %collective-permute-start.22) | collective-permute-done | bytes 262176 | tf_op jit(solution)/shard_map/ppermute | solution.py:130
  274.7 7.4 %all-to-all-start.3 = ((f32[16,2,16]{2,1,0:T(2,128)}), f32[16,2,16]{2,1,0:T(2,128)S(1)}, u32[]{:S(2)}, u32[]{:S(2)}) async-start(f32[16,2,16]{2,1,0:T(2,128)} %bitcast.58), calls=%async_computation.3 | async-start | bytes 32768 | tf_op jit(solution)/shard_map/all_to_all | solution.py:125
  290.0 4.5 %all-to-all-start.4 = ((f32[32,2,16]{2,1,0:T(2,128)}), f32[32,2,16]{2,1,0:T(2,128)S(1)}, u32[]{:S(2)}, u32[]{:S(2)}) async-start(f32[32,2,16]{2,1,0:T(2,128)} %broadcast_in_dim.32), calls=%async_computation.4 | async-start | bytes 65536 | tf_op jit(solution)/shard_map/all_to_all | solution.py:125
  297.2 6.0 %all-to-all-done.4 = f32[32,2,16]{2,1,0:T(2,128)S(1)} async-done(((f32[32,2,16]{2,1,0:T(2,128)}), f32[32,2,16]{2,1,0:T(2,128)S(1)}, u32[]{:S(2)}, u32[]{:S(2)}) %all-to-all-start.4) | async-done | bytes 4128 | tf_op jit(solution)/shard_map/all_to_all | solution.py:125
  (131 shorter events, 121.5 us)
Async XLA Ops:
  7.2 100.9 %all-gather.3.cloned.1.call-start = ((), (), s32[]{:S(2)}) async-start(), calls=%async_computation.5 | async-start | bytes 5947392 | tf_op jit(solution)/shard_map/all_gather | solution.py:203
  32.0 74.0 %all-to-all-start.1 = ((bf16[32,256,128]{2,1,0:T(8,128)(2,1)}), bf16[32,256,128]{2,1,0:T(8,128)(2,1)S(1)}, u32[]{:S(2)}, u32[]{:S(2)}) async-start(bf16[32,256,128]{2,1,0:T(8,128)(2,1)} %copy.104), calls=%async_computation.1 | async-start | bytes 4194304 | tf_op jit(solution)/shard_map/all_to_all | solution.py:125
  45.3 44.9 %collective-permute-start.1 = (bf16[2,2,128,256]{3,2,1,0:T(8,128)(2,1)S(1)}, bf16[2,2,128,256]{3,2,1,0:T(8,128)(2,1)}, u32[]{:S(2)}, u32[]{:S(2)}) collective-permute-start(bf16[2,2,128,256]{3,2,1,0:T(8,128)(2,1)S(1)} %pad_maximum_fusion.5), channel_id=1, source_target_pairs={{0,64},{64,128},{128,192},{192,256},{256,320},{320,384},{384,448},... | collective-permute-start | bytes 786440 | tf_op jit(solution)/shard_map/ppermute | solution.py:130
  48.7 51.5 %collective-permute-start.2 = (bf16[2,2,128,256]{3,2,1,0:T(8,128)(2,1)S(1)}, bf16[2,2,128,256]{3,2,1,0:T(8,128)(2,1)}, u32[]{:S(2)}, u32[]{:S(2)}) collective-permute-start(bf16[2,2,128,256]{3,2,1,0:T(8,128)(2,1)S(1)} %pad_maximum_fusion.6), channel_id=1, source_target_pairs={{0,128},{64,192},{128,256},{192,320},{256,384},{320,448},{384,0},{... | collective-permute-start | bytes 786440 | tf_op jit(solution)/shard_map/ppermute | solution.py:130
  53.5 64.4 %collective-permute-start.3 = (bf16[2,2,128,256]{3,2,1,0:T(8,128)(2,1)}, bf16[2,2,128,256]{3,2,1,0:T(8,128)(2,1)}, u32[]{:S(2)}, u32[]{:S(2)}) collective-permute-start(bf16[2,2,128,256]{3,2,1,0:T(8,128)(2,1)} %pad_maximum_fusion.7), channel_id=1, source_target_pairs={{0,192},{64,256},{128,320},{192,384},{256,448},{320,0},{384,64},{4... | collective-permute-start | bytes 786440 | tf_op jit(solution)/shard_map/ppermute | solution.py:130
  58.6 69.5 %collective-permute-start.4 = (bf16[2,2,128,256]{3,2,1,0:T(8,128)(2,1)}, bf16[2,2,128,256]{3,2,1,0:T(8,128)(2,1)}, u32[]{:S(2)}, u32[]{:S(2)}) collective-permute-start(bf16[2,2,128,256]{3,2,1,0:T(8,128)(2,1)} %pad_maximum_fusion.8), channel_id=1, source_target_pairs={{0,256},{64,320},{128,384},{192,448},{256,0},{320,64},{384,128},{4... | collective-permute-start | bytes 786440 | tf_op jit(solution)/shard_map/ppermute | solution.py:130
  63.3 64.8 %collective-permute-start.5 = (bf16[2,2,128,256]{3,2,1,0:T(8,128)(2,1)}, bf16[2,2,128,256]{3,2,1,0:T(8,128)(2,1)}, u32[]{:S(2)}, u32[]{:S(2)}) collective-permute-start(bf16[2,2,128,256]{3,2,1,0:T(8,128)(2,1)} %pad_maximum_fusion.9), channel_id=1, source_target_pairs={{0,320},{64,384},{128,448},{192,0},{256,64},{320,128},{384,192},{4... | collective-permute-start | bytes 786440 | tf_op jit(solution)/shard_map/ppermute | solution.py:130
  90.2 37.8 %collective-permute-start.6 = (bf16[2,2,128,256]{3,2,1,0:T(8,128)(2,1)}, bf16[2,2,128,256]{3,2,1,0:T(8,128)(2,1)}, u32[]{:S(2)}, u32[]{:S(2)}) collective-permute-start(bf16[2,2,128,256]{3,2,1,0:T(8,128)(2,1)} %pad_maximum_fusion.10), channel_id=1, source_target_pairs={{0,384},{64,448},{128,0},{192,64},{256,128},{320,192},{384,256},{4... | collective-permute-start | bytes 786440 | tf_op jit(solution)/shard_map/ppermute | solution.py:130
  100.2 28.2 %collective-permute-start.7 = (bf16[2,2,128,256]{3,2,1,0:T(8,128)(2,1)}, bf16[2,2,128,256]{3,2,1,0:T(8,128)(2,1)}, u32[]{:S(2)}, u32[]{:S(2)}) collective-permute-start(bf16[2,2,128,256]{3,2,1,0:T(8,128)(2,1)} %pad_maximum_fusion.11), channel_id=1, source_target_pairs={{0,448},{64,0},{128,64},{192,128},{256,192},{320,256},{384,320},{4... | collective-permute-start | bytes 786440 | tf_op jit(solution)/shard_map/ppermute | solution.py:130
  143.8 28.4 %collective-permute-start.16 = (bf16[8,2,256,128]{3,2,1,0:T(8,128)(2,1)}, bf16[8,2,256,128]{3,2,1,0:T(8,128)(2,1)}, u32[]{:S(2)}, u32[]{:S(2)}) collective-permute-start(bf16[8,2,256,128]{3,2,1,0:T(8,128)(2,1)} %slice_bitcast_fusion), channel_id=1, source_target_pairs={{0,32},{32,0},{1,33},{33,1},{2,34},{34,2},{3,35},{35,3},{4,36},{36... | collective-permute-start | bytes 3145736 | tf_op jit(solution)/shard_map/ppermute | solution.py:130
  155.4 109.0 %all-to-all-start.2 = ((bf16[32,256,128]{2,1,0:T(8,128)(2,1)}), bf16[32,256,128]{2,1,0:T(8,128)(2,1)}, u32[]{:S(2)}, u32[]{:S(2)}) async-start(bf16[32,256,128]{2,1,0:T(8,128)(2,1)} %bitcast.130), calls=%async_computation.2 | async-start | bytes 4194304 | tf_op jit(solution)/shard_map/all_to_all | solution.py:125
  164.8 19.6 %collective-permute-start.11 = (bf16[8,352,128]{2,1,0:T(8,128)(2,1)S(1)}, bf16[8,352,128]{2,1,0:T(8,128)(2,1)S(1)}, u32[]{:S(2)}, u32[]{:S(2)}) collective-permute-start(bf16[8,352,128]{2,1,0:T(8,128)(2,1)S(1)} %pad_maximum_fusion.3), channel_id=1, source_target_pairs={{0,3},{1,0},{2,1},{3,2},{4,7},{5,4},{6,5},{7,6},{8,11},{9,8},{10,9... | collective-permute-start | bytes 2162696 | tf_op jit(solution)/shard_map/ppermute | solution.py:130
  170.2 19.4 %collective-permute-start.9 = (bf16[8,352,128]{2,1,0:T(8,128)(2,1)S(1)}, bf16[8,352,128]{2,1,0:T(8,128)(2,1)S(1)}, u32[]{:S(2)}, u32[]{:S(2)}) collective-permute-start(bf16[8,352,128]{2,1,0:T(8,128)(2,1)S(1)} %pad_maximum_fusion.2), channel_id=1, source_target_pairs={{0,1},{1,2},{2,3},{3,0},{4,5},{5,6},{6,7},{7,4},{8,9},{9,10},{10,1... | collective-permute-start | bytes 2162696 | tf_op jit(solution)/shard_map/ppermute | solution.py:130
  173.6 50.9 %collective-permute-start.17 = (bf16[2,2,256,128]{3,2,1,0:T(8,128)(2,1)S(1)}, bf16[2,2,256,128]{3,2,1,0:T(8,128)(2,1)S(1)}, u32[]{:S(2)}, u32[]{:S(2)}) collective-permute-start(bf16[2,2,256,128]{3,2,1,0:T(8,128)(2,1)S(1)} %pad_maximum_fusion.12), channel_id=1, source_target_pairs={{0,64},{64,128},{128,192},{192,256},{256,320},{320,384},{384,448},... | collective-permute-start | bytes 786440 | tf_op jit(solution)/shard_map/ppermute | solution.py:130
  176.9 53.0 %collective-permute-start.18 = (bf16[2,2,256,128]{3,2,1,0:T(8,128)(2,1)S(1)}, bf16[2,2,256,128]{3,2,1,0:T(8,128)(2,1)S(1)}, u32[]{:S(2)}, u32[]{:S(2)}) collective-permute-start(bf16[2,2,256,128]{3,2,1,0:T(8,128)(2,1)S(1)} %pad_maximum_fusion.13), channel_id=1, source_target_pairs={{0,128},{64,192},{128,256},{192,320},{256,384},{320,448},{384,0},{... | collective-permute-start | bytes 786440 | tf_op jit(solution)/shard_map/ppermute | solution.py:130
  191.1 17.2 %collective-permute-start.12 = (bf16[2,352,128]{2,1,0:T(8,128)(2,1)S(1)}, bf16[2,352,128]{2,1,0:T(8,128)(2,1)S(1)}, u32[]{:S(2)}, u32[]{:S(2)}) collective-permute-start(bf16[2,352,128]{2,1,0:T(8,128)(2,1)S(1)} %get-tuple-element.106), channel_id=1, source_target_pairs={{0,8},{4,12},{8,16},{12,20},{16,24},{20,28},{24,0},{28,4},{1,9},{5... | collective-permute-start | bytes 540680 | tf_op jit(solution)/shard_map/ppermute | solution.py:130
  196.0 18.3 %collective-permute-start.14 = (bf16[2,352,128]{2,1,0:T(8,128)(2,1)S(1)}, bf16[2,352,128]{2,1,0:T(8,128)(2,1)S(1)}, u32[]{:S(2)}, u32[]{:S(2)}) collective-permute-start(bf16[2,352,128]{2,1,0:T(8,128)(2,1)S(1)} %get-tuple-element.107), channel_id=1, source_target_pairs={{0,24},{4,28},{8,0},{12,4},{16,8},{20,12},{24,16},{28,20},{1,25},{... | collective-permute-start | bytes 540680 | tf_op jit(solution)/shard_map/ppermute | solution.py:130
  202.8 16.6 %collective-permute-start.13 = (bf16[2,352,128]{2,1,0:T(8,128)(2,1)S(1)}, bf16[2,352,128]{2,1,0:T(8,128)(2,1)S(1)}, u32[]{:S(2)}, u32[]{:S(2)}) collective-permute-start(bf16[2,352,128]{2,1,0:T(8,128)(2,1)S(1)} %get-tuple-element.108), channel_id=1, source_target_pairs={{0,16},{4,20},{8,24},{12,28},{16,0},{20,4},{24,8},{28,12},{1,17},{... | collective-permute-start | bytes 540680 | tf_op jit(solution)/shard_map/ppermute | solution.py:130
  208.3 35.4 %collective-permute-start.19 = (bf16[2,2,256,128]{3,2,1,0:T(8,128)(2,1)S(1)}, bf16[2,2,256,128]{3,2,1,0:T(8,128)(2,1)S(1)}, u32[]{:S(2)}, u32[]{:S(2)}) collective-permute-start(bf16[2,2,256,128]{3,2,1,0:T(8,128)(2,1)S(1)} %pad_maximum_fusion.14), channel_id=1, source_target_pairs={{0,192},{64,256},{128,320},{192,384},{256,448},{320,0},{384,64},{4... | collective-permute-start | bytes 786440 | tf_op jit(solution)/shard_map/ppermute | solution.py:130
  214.3 39.5 %collective-permute-start.20 = (bf16[2,2,256,128]{3,2,1,0:T(8,128)(2,1)S(1)}, bf16[2,2,256,128]{3,2,1,0:T(8,128)(2,1)S(1)}, u32[]{:S(2)}, u32[]{:S(2)}) collective-permute-start(bf16[2,2,256,128]{3,2,1,0:T(8,128)(2,1)S(1)} %pad_maximum_fusion.15), channel_id=1, source_target_pairs={{0,256},{64,320},{128,384},{192,448},{256,0},{320,64},{384,128},{4... | collective-permute-start | bytes 786440 | tf_op jit(solution)/shard_map/ppermute | solution.py:130
  219.4 34.4 %collective-permute-start.21 = (bf16[2,2,256,128]{3,2,1,0:T(8,128)(2,1)S(1)}, bf16[2,2,256,128]{3,2,1,0:T(8,128)(2,1)S(1)}, u32[]{:S(2)}, u32[]{:S(2)}) collective-permute-start(bf16[2,2,256,128]{3,2,1,0:T(8,128)(2,1)S(1)} %pad_maximum_fusion.16), channel_id=1, source_target_pairs={{0,320},{64,384},{128,448},{192,0},{256,64},{320,128},{384,192},{4... | collective-permute-start | bytes 786440 | tf_op jit(solution)/shard_map/ppermute | solution.py:130
  224.5 37.4 %collective-permute-start.22 = (bf16[2,2,256,128]{3,2,1,0:T(8,128)(2,1)S(1)}, bf16[2,2,256,128]{3,2,1,0:T(8,128)(2,1)S(1)}, u32[]{:S(2)}, u32[]{:S(2)}) collective-permute-start(bf16[2,2,256,128]{3,2,1,0:T(8,128)(2,1)S(1)} %pad_maximum_fusion.17), channel_id=1, source_target_pairs={{0,384},{64,448},{128,0},{192,64},{256,128},{320,192},{384,256},{4... | collective-permute-start | bytes 786440 | tf_op jit(solution)/shard_map/ppermute | solution.py:130
  229.9 33.8 %collective-permute-start.23 = (bf16[2,2,256,128]{3,2,1,0:T(8,128)(2,1)S(1)}, bf16[2,2,256,128]{3,2,1,0:T(8,128)(2,1)S(1)}, u32[]{:S(2)}, u32[]{:S(2)}) collective-permute-start(bf16[2,2,256,128]{3,2,1,0:T(8,128)(2,1)S(1)} %pad_maximum_fusion.18), channel_id=1, source_target_pairs={{0,448},{64,0},{128,64},{192,128},{256,192},{320,256},{384,320},{4... | collective-permute-start | bytes 786440 | tf_op jit(solution)/shard_map/ppermute | solution.py:130
  243.7 20.1 %collective-permute-start.15 = (bf16[352,128]{1,0:T(8,128)(2,1)S(1)}, bf16[352,128]{1,0:T(8,128)(2,1)S(1)}, u32[]{:S(2)}, u32[]{:S(2)}) collective-permute-start(bf16[352,128]{1,0:T(8,128)(2,1)S(1)} %slice_bitcast_fusion.24), channel_id=1, source_target_pairs={{0,4},{4,8},{8,12},{12,16},{16,20},{20,24},{24,28},{28,0},{1,5},{5... | collective-permute-start | bytes 270344 | tf_op jit(solution)/shard_map/ppermute | solution.py:130
  (11 other events, 97.0 us)
Sparse Core Ops, SparseCore 0:
  11.2 96.9 all-gather.2
